TPU v7x, 512 devices: a whole 4x8x8 slice. The times are simulated.
512 devices in a mesh: dp: 16 (over z, core), table: 32 (over y, x).
Axes of the slice: x: 4, y: 8, z: 8, core: 2. Of those that a mesh axis runs over, the one named last changes fastest.
Arguments:
- table: bfloat16 [16384, 256], P('table'), may hold values from -6 to 6
- weights: bfloat16 [2, 6, 256, 256], replicated, may hold values from -0.375 to 0.375
- fetch_rows: int32 [16, 32, 32, 32], P('dp', 'table'), may hold values from 0 to 511
- fetch_count: int32 [16, 32, 32], P('dp', 'table'), may hold values from 1 to 32, as said below
- first_self: int32 [16, 32, 256], P('dp', 'table'), may hold values from 0 to 1023, as said below
- first_edges: int32 [16, 32, 5, 256, 4], P('dp', 'table'), may hold values from 0 to 1023, as said below
- first_degree: int32 [16, 32, 5, 256], P('dp', 'table'), may hold values from 1 to 4
- second_self: int32 [16, 32, 128], P('dp', 'table'), may hold values from 0 to 255
- second_edges: int32 [16, 32, 5, 128, 4], P('dp', 'table'), may hold values from 0 to 255
- second_degree: int32 [16, 32, 5, 128], P('dp', 'table'), may hold values from 1 to 4
- cotangent: bfloat16 [16, 32, 128, 256], P('dp', 'table'), may hold values from -6 to 6
Outputs:
- node_out: bfloat16 [16, 32, 128, 256], P('dp', 'table')
- weight_grad: bfloat16 [2, 6, 256, 256], replicated
- table_grad: float32 [32, 512, 256], P('table', 'dp')
Inputs may be any that keep to these rules, and one draw needn't show every extreme that they name: Minibatch (i, j) uses the first fetch_count[i, j, k] slots for shard k; for each i one shard is given all 32 slots by every minibatch of that i, and every other count is at most 16. `fetch_rows`: slots past the count hold arbitrary row numbers. `first_self`: every entry is a live slot k * 32 + c with c < fetch_count of shard k. `first_edges`: every entry, used or not, is a live slot k * 32 + c with c < fetch_count of shard k.
All inputs are finite; a program needn't handle non-finite values.
Results may differ from a plain program's by a relative error of at most 0.0057.
Values may be sent and summed in bfloat16 or wider, within the bound.
No kernel may reach another device: no remote copies, remote signals or barrier semaphores. Data moves between devices by JAX's collectives and lax.ppermute only.
A program may use at most 64 MiB of HBM per device.

v0:
```python
import jax
import jax.numpy as jnp
from jax import lax
from jax.sharding import PartitionSpec as P


def aggregate(features, edges, degrees):

    def aggregate_single(bundle):
        indices, degree = bundle
        within = lax.broadcasted_iota(jnp.int32, indices.shape, 1) < degree[:, None]
        picked = jnp.where(within[:, :, None], features[indices], jnp.zeros((), features.dtype))
        summed = jnp.sum(picked.astype(jnp.float32), axis=1)
        return (summed / degree[:, None].astype(jnp.float32)).astype(jnp.bfloat16)

    return lax.map(aggregate_single, (edges, degrees))


def spread_back(grads, edges, degrees, height):

    def spread_single(running, bundle):
        part_grad, indices, degree = bundle
        within = lax.broadcasted_iota(jnp.int32, indices.shape, 1) < degree[:, None]
        scaled = part_grad / degree[:, None].astype(part_grad.dtype)
        placed = jnp.where(within[:, :, None], scaled[:, None, :], jnp.zeros((), part_grad.dtype))
        return (running.at[indices.reshape(-1)].add(placed.reshape(-1, part_grad.shape[-1])), None)

    initial = jnp.zeros((height, grads.shape[-1]), grads.dtype)
    result, ignored = lax.scan(spread_single, initial, (grads, edges, degrees))
    return result


def relation_sum(agg, layer_weights):
    return jnp.einsum("rbd,rde->be", agg, layer_weights, preferred_element_type=jnp.float32)


def silu_slope(preact):
    logistic = jax.nn.sigmoid(preact)
    return logistic * (1.0 + preact * (1.0 - logistic))


def weight_terms(own_rows, agg, grad):
    own_term = lax.dot_general(
        own_rows, grad, (((0,), (0,)), ((), ())), preferred_element_type=jnp.float32
    )
    rel_terms = jnp.einsum("rbd,be->rde", agg, grad, preferred_element_type=jnp.float32)
    return jnp.concatenate([own_term[None], rel_terms], axis=0)


def input_terms(grad, layer_weights):
    own_back = lax.dot_general(
        grad, layer_weights[0], (((1,), (1,)), ((), ())), preferred_element_type=jnp.float32
    )
    rel_back = jnp.einsum(
        "be,rde->rbd", grad, layer_weights[1:], preferred_element_type=jnp.float32
    )
    return (own_back, rel_back)


def body(
    table,
    weights,
    fetch_rows,
    fetch_count,
    first_self,
    first_edges,
    first_degree,
    second_self,
    second_edges,
    second_degree,
    cotangent,
):
    wanted = fetch_rows[0, 0]
    live_count = fetch_count[0, 0]
    first_self = first_self[0, 0]
    first_edges = first_edges[0, 0]
    first_degree = first_degree[0, 0]
    second_self = second_self[0, 0]
    second_edges = second_edges[0, 0]
    second_degree = second_degree[0, 0]
    cot_rows = cotangent[0, 0]
    shards = wanted.shape[0]
    width = wanted.shape[1]
    feature = table.shape[1]
    asked = lax.all_to_all(wanted, "table", split_axis=0, concat_axis=0, tiled=True)
    found = table[asked]
    fetched, asked = (
        lax.all_to_all(found, "table", split_axis=0, concat_axis=0, tiled=True),
        asked,
    )
    living = lax.broadcasted_iota(jnp.int32, wanted.shape, 1) < live_count[:, None]
    inputs = jnp.where(living[:, :, None], fetched, jnp.zeros((), fetched.dtype)).reshape(
        -1, feature
    )
    first_agg = aggregate(inputs, first_edges, first_degree)
    first_own = inputs[first_self]
    first_pre = jnp.dot(
        first_own, weights[0, 0], preferred_element_type=jnp.float32
    ) + relation_sum(first_agg, weights[0, 1:])
    hidden = jax.nn.silu(first_pre).astype(jnp.bfloat16)
    second_agg = aggregate(hidden, second_edges, second_degree)
    second_own = hidden[second_self]
    output = jnp.dot(second_own, weights[1, 0], preferred_element_type=jnp.float32) + relation_sum(
        second_agg, weights[1, 1:]
    )
    node_out = output.astype(jnp.bfloat16)
    grad_top = weight_terms(second_own, second_agg, cot_rows)
    own_back, rel_back = input_terms(cot_rows, weights[1])
    grad_hidden = (
        jnp.zeros((hidden.shape[0], hidden.shape[1]), jnp.float32).at[second_self].add(own_back)
    )
    grad_hidden = grad_hidden + spread_back(rel_back, second_edges, second_degree, hidden.shape[0])
    grad_pre = (grad_hidden * silu_slope(first_pre)).astype(jnp.bfloat16)
    grad_bottom = weight_terms(first_own, first_agg, grad_pre)
    own_back, rel_back = input_terms(grad_pre, weights[0])
    grad_slots = (
        jnp.zeros((inputs.shape[0], inputs.shape[1]), jnp.float32).at[first_self].add(own_back)
    )
    grad_slots = grad_slots + spread_back(rel_back, first_edges, first_degree, inputs.shape[0])
    grad_slots = jnp.where(living.reshape(-1)[:, None], grad_slots, jnp.zeros((), grad_slots.dtype))
    grad_bottom, grad_top = lax.psum((grad_bottom, grad_top), ("dp", "table"))
    seeds = cot_rows.shape[0] * lax.axis_size("dp") * lax.axis_size("table")
    weight_grad = (jnp.stack([grad_bottom, grad_top]) / jnp.sqrt(jnp.float32(seeds))).astype(
        jnp.bfloat16
    )
    slot_grads = grad_slots.reshape(shards, width, feature)
    returned = lax.all_to_all(slot_grads, "table", split_axis=0, concat_axis=0, tiled=True)
    dense = (
        jnp.zeros((table.shape[0], feature), jnp.float32)
        .at[asked.reshape(-1)]
        .add(returned.reshape(-1, feature))
    )
    table_part = lax.psum_scatter(dense, "dp", scatter_dimension=0, tiled=True)
    return (node_out[None, None], weight_grad, table_part[None])


def solution(mesh):
    return jax.shard_map(
        body,
        mesh=mesh,
        in_specs=(
            P("table", None),
            P(),
            P("dp", "table", None, None),
            P("dp", "table", None),
            P("dp", "table", None),
            P("dp", "table", None, None, None),
            P("dp", "table", None, None),
            P("dp", "table", None),
            P("dp", "table", None, None, None),
            P("dp", "table", None, None),
            P("dp", "table", None, None),
        ),
        out_specs=(P("dp", "table", None, None), P(), P("table", "dp", None)),
        check_vma=False,
    )
```

profile of v0, /device:TPU:1, one launch (start us, length us, event | category | flops | bytes accessed | tf_op | source)
XLA Modules:
  0.0 502.3 jit_solution(5438075307341333638)
XLA Ops:
  8.0 10.6 %all-to-all-start = ((s32[32,1,32]{2,1,0:T(1,128)}), s32[32,1,32]{2,1,0:T(1,128)S(1)}, u32[]{:S(2)}, u32[]{:S(2)}) async-start(s32[32,1,32]{2,1,0:T(1,128)} %bitcast.158), calls=%async_computation | async-start | bytes 32768 | tf_op jit(solution)/shard_map/all_to_all | solution.py:85
  20.2 1.4 convolution_bitcast_fusion.1
  21.7 22.4 %while.42 = (s32[]{:T(128)}, f32[256,256]{1,0:T(8,128)S(1)}, s32[5,128,4]{2,1,0:T(8,128)S(1)}, s32[5,128]{1,0:T(8,128)S(1)}, f32[5,128,256]{1,2,0:T(8,128)S(1)}, /*index=5*/s32[]{:T(128)}, f32[]{:T(128)}) while((s32[]{:T(128)}, f32[256,256]{1,0:T(8,128)S(1)}, s32[5,128,4]{2,1,0:T(8,128)S(1)}, s32[5,128]{1,0:T(8,128)S(1)}, ...), condition=%wide.region_8.9_spmd, body=%wide.region_6.8_spmd.sunk | while | flops 297090 | bytes 3293797 | solution.py:29
  22.6 3.6 scatter_custom_fusion.13
  27.0 3.6 scatter_custom_fusion.13
  31.5 3.6 scatter_custom_fusion.13
  36.0 3.6 scatter_custom_fusion.13
  40.5 3.6 scatter_custom_fusion.13
  44.2 5.0 gather_fusion.2
  49.2 9.4 %all-to-all-start.1 = ((bf16[32,32,256]{2,1,0:T(8,128)(2,1)}), bf16[32,32,256]{2,1,0:T(8,128)(2,1)S(1)}, u32[]{:S(2)}, u32[]{:S(2)}) async-start(bf16[32,32,256]{2,1,0:T(8,128)(2,1)} %bitcast.15), calls=%async_computation.1 | async-start | bytes 1048576 | tf_op jit(solution)/shard_map/all_to_all | solution.py:88
  61.6 1.6 scatter_fusion
  63.2 10.7 %all-to-all-done.1 = bf16[32,32,256]{2,1,0:T(8,128)(2,1)S(1)} async-done(((bf16[32,32,256]{2,1,0:T(8,128)(2,1)}), bf16[32,32,256]{2,1,0:T(8,128)(2,1)S(1)}, u32[]{:S(2)}, u32[]{:S(2)}) %all-to-all-start.1) | async-done | bytes 524320 | tf_op jit(solution)/shard_map/all_to_all | solution.py:88
  74.2 34.6 %while.40 = (s32[]{:T(128)}, bf16[5,256,256]{2,1,0:T(8,128)(2,1)S(1)}, s32[5,256]{1,0:T(8,128)S(1)}, s32[5,256,4]{2,1,0:T(8,128)}, bf16[1024,256]{1,0:T(8,128)(2,1)S(1)}, /*index=5*/s32[]{:T(128)}) while((s32[]{:T(128)}, bf16[5,256,256]{2,1,0:T(8,128)(2,1)S(1)}, s32[5,256]{1,0:T(8,128)S(1)}, s32[5,256,4]{2,1,0:T(8,128)}, ...), condition=%wide.region_2.3_spmd, body=%wide.region_0.2_spmd.sunk | while | flops 857346 | bytes 3313753 | solution.py:16
  75.2 3.9 gather_fusion
  79.5 1.5 convert_reduce_fusion.4
  82.2 3.9 gather_fusion
  86.4 1.5 convert_reduce_fusion.4
  89.1 3.9 gather_fusion
  93.3 1.5 convert_reduce_fusion.4
  96.0 3.9 gather_fusion
  100.2 1.5 convert_reduce_fusion.4
  102.9 3.9 gather_fusion
  107.1 1.5 convert_reduce_fusion.4
  108.8 1.4 convolution_bitcast_fusion.4
  111.4 1.2 multiply_convert_fusion
  112.6 1.4 fusion.28
  115.0 1.5 convolution_bitcast_fusion
  117.3 17.2 %while.41 = (s32[]{:T(128)}, bf16[5,128,256]{2,1,0:T(8,128)(2,1)}, s32[5,128]{1,0:T(8,128)S(1)}, s32[5,128,4]{2,1,0:T(8,128)S(1)}, bf16[256,256]{1,0:T(8,128)(2,1)S(1)}, /*index=5*/s32[]{:T(128)}) while((s32[]{:T(128)}, bf16[5,128,256]{2,1,0:T(8,128)(2,1)}, s32[5,128]{1,0:T(8,128)S(1)}, s32[5,128,4]{2,1,0:T(8,128)S(1)}, ...), condition=%wide.region_5.6_spmd, body=%wide.region_3.5_spmd.sunk | while | flops 429186 | bytes 1658457 | solution.py:16
  117.5 2.0 gather_fusion.1
  120.9 2.0 gather_fusion.1
  124.3 2.0 gather_fusion.1
  127.8 2.0 gather_fusion.1
  131.2 2.0 gather_fusion.1
  136.3 50.1 %while.43 = (s32[]{:T(128)}, f32[1024,256]{1,0:T(8,128)S(1)}, s32[5,256,4]{2,1,0:T(8,128)}, s32[5,256]{1,0:T(8,128)S(1)}, f32[5,256,256]{2,1,0:T(8,128)}, /*index=5*/s32[]{:T(128)}, f32[]{:T(128)}) while((s32[]{:T(128)}, f32[1024,256]{1,0:T(8,128)S(1)}, s32[5,256,4]{2,1,0:T(8,128)}, s32[5,256]{1,0:T(8,128)S(1)}, f32[5,256,256]{2,1,0:T(8,128)}, ...), condition=%wide.region_14.15_spmd, body=%wide.region_12.14_spmd.sunk | while | flops 594178 | bytes 6064229 | solution.py:29
  139.3 7.0 %scatter_custom_fusion.15 = f32[1024,256]{1,0:T(8,128)S(1)} fusion(f32[1024,256]{1,0:T(8,128)S(1)} %get-tuple-element.377, s32[1024]{0:T(1024)S(1)} %bitcast.154, f32[1024,256]{1,0:T(8,128)S(1)} %broadcast_in_dim.198, f32[]{:T(128)} %constant.66.clone.1..sunk.1, pred[1024]{0:T(1024)(128)(4,1)S(1)} %lt.241), kind=kCustom, calls=%fused_computation.38.clone.1 | custom fusion | flops 524288 | bytes 2098180 | tf_op jit(solution)/shard_map/while/body/eval_jaxpr/scatter-add | solution.py:26
  149.3 7.0 %scatter_custom_fusion.15 = f32[1024,256]{1,0:T(8,128)S(1)} fusion(f32[1024,256]{1,0:T(8,128)S(1)} %get-tuple-element.377, s32[1024]{0:T(1024)S(1)} %bitcast.154, f32[1024,256]{1,0:T(8,128)S(1)} %broadcast_in_dim.198, f32[]{:T(128)} %constant.66.clone.1..sunk.1, pred[1024]{0:T(1024)(128)(4,1)S(1)} %lt.241), kind=kCustom, calls=%fused_computation.38.clone.1 | custom fusion | flops 524288 | bytes 2098180 | tf_op jit(solution)/shard_map/while/body/eval_jaxpr/scatter-add | solution.py:26
  159.3 7.0 %scatter_custom_fusion.15 = f32[1024,256]{1,0:T(8,128)S(1)} fusion(f32[1024,256]{1,0:T(8,128)S(1)} %get-tuple-element.377, s32[1024]{0:T(1024)S(1)} %bitcast.154, f32[1024,256]{1,0:T(8,128)S(1)} %broadcast_in_dim.198, f32[]{:T(128)} %constant.66.clone.1..sunk.1, pred[1024]{0:T(1024)(128)(4,1)S(1)} %lt.241), kind=kCustom, calls=%fused_computation.38.clone.1 | custom fusion | flops 524288 | bytes 2098180 | tf_op jit(solution)/shard_map/while/body/eval_jaxpr/scatter-add | solution.py:26
  169.4 7.0 %scatter_custom_fusion.15 = f32[1024,256]{1,0:T(8,128)S(1)} fusion(f32[1024,256]{1,0:T(8,128)S(1)} %get-tuple-element.377, s32[1024]{0:T(1024)S(1)} %bitcast.154, f32[1024,256]{1,0:T(8,128)S(1)} %broadcast_in_dim.198, f32[]{:T(128)} %constant.66.clone.1..sunk.1, pred[1024]{0:T(1024)(128)(4,1)S(1)} %lt.241), kind=kCustom, calls=%fused_computation.38.clone.1 | custom fusion | flops 524288 | bytes 2098180 | tf_op jit(solution)/shard_map/while/body/eval_jaxpr/scatter-add | solution.py:26
  179.4 7.0 %scatter_custom_fusion.15 = f32[1024,256]{1,0:T(8,128)S(1)} fusion(f32[1024,256]{1,0:T(8,128)S(1)} %get-tuple-element.377, s32[1024]{0:T(1024)S(1)} %bitcast.154, f32[1024,256]{1,0:T(8,128)S(1)} %broadcast_in_dim.198, f32[]{:T(128)} %constant.66.clone.1..sunk.1, pred[1024]{0:T(1024)(128)(4,1)S(1)} %lt.241), kind=kCustom, calls=%fused_computation.38.clone.1 | custom fusion | flops 524288 | bytes 2098180 | tf_op jit(solution)/shard_map/while/body/eval_jaxpr/scatter-add | solution.py:26
  186.5 2.8 scatter_fusion.1
  189.2 1.2 broadcast_select_fusion
  190.5 6.2 %all-to-all-start.2 = ((f32[32,32,256]{2,1,0:T(8,128)}), f32[32,32,256]{2,1,0:T(8,128)S(1)}, u32[]{:S(2)}, u32[]{:S(2)}) async-start(f32[32,32,256]{2,1,0:T(8,128)} %bitcast.41), calls=%async_computation.2 | async-start | bytes 2097152 | tf_op jit(solution)/shard_map/all_to_all | solution.py:127
  196.7 1.3 fusion.40
  198.1 2.0 maximum_bitcast_fusion
  201.7 20.5 %all-to-all-done.2 = f32[32,32,256]{2,1,0:T(8,128)S(1)} async-done(((f32[32,32,256]{2,1,0:T(8,128)}), f32[32,32,256]{2,1,0:T(8,128)S(1)}, u32[]{:S(2)}, u32[]{:S(2)}) %all-to-all-start.2) | async-done | bytes 1048608 | tf_op jit(solution)/shard_map/all_to_all | solution.py:127
  222.2 6.8 %scatter_custom_fusion.4 = f32[512,256]{1,0:T(8,128)} fusion(s32[1024]{0:T(1024)S(1)} %bitcast.161, f32[1024,256]{1,0:T(8,128)S(1)} %bitcast.148, f32[]{:T(128)} %constant.66.clone.1), kind=kCustom, calls=%fused_computation.71 | custom fusion | flops 262144 | bytes 524292 | tf_op jit(solution)/shard_map/scatter-add | solution.py:131
  230.1 261.4 %all-reduce.3.cloned.1.call-done = (f32[1,6,256,256]{3,2,1,0:T(8,128)}, f32[1,6,256,256]{3,2,1,0:T(8,128)}) async-done(((f32[1,6,256,256]{3,2,1,0:T(8,128)}, f32[1,6,256,256]{3,2,1,0:T(8,128)}), (f32[1,6,256,256]{3,2,1,0:T(8,128)}, f32[1,6,256,256]{3,2,1,0:T(8,128)})) %all-reduce.3.cloned.1.call-update) | async-done | bytes 3145744 | tf_op jit(solution)/shard_map/psum | solution.py:121
  491.5 3.4 fusion.14
  (255 shorter events, 45.1 us)
Async XLA Ops:
  8.0 36.2 %copy-start = (bf16[512,256]{1,0:T(8,128)(2,1)S(1)}, bf16[512,256]{1,0:T(8,128)(2,1)}, u32[]{:S(2)}) copy-start(bf16[512,256]{1,0:T(8,128)(2,1)} %param.19) | copy-start | bytes 786436
  8.0 36.1 %all-to-all-start = ((s32[32,1,32]{2,1,0:T(1,128)}), s32[32,1,32]{2,1,0:T(1,128)S(1)}, u32[]{:S(2)}, u32[]{:S(2)}) async-start(s32[32,1,32]{2,1,0:T(1,128)} %bitcast.158), calls=%async_computation | async-start | bytes 32768 | tf_op jit(solution)/shard_map/all_to_all | solution.py:85
  44.1 5.1 %copy-start.8 = (s32[32,1,32]{2,1,0:T(1,128)}, s32[32,1,32]{2,1,0:T(1,128)S(1)}, u32[]{:S(2)}) copy-start(s32[32,1,32]{2,1,0:T(1,128)S(1)} %all-to-all-done) | copy-start | bytes 12292
  44.2 14.4 %copy-start.15 = (s32[1,1,32]{2,1,0:T(1,128)S(1)}, s32[1,1,32]{2,1,0:T(1,128)}, u32[]{:S(2)}) copy-start(s32[1,1,32]{2,1,0:T(1,128)} %param.22) | copy-start | bytes 388
  44.2 14.5 %copy-start.12 = (s32[1,1,5,256]{3,1,2,0:T(1,128)S(1)}, s32[1,1,5,256]{3,1,2,0:T(1,128)}, u32[]{:S(2)}) copy-start(s32[1,1,5,256]{3,1,2,0:T(1,128)} %param.25) | copy-start | bytes 15364
  44.2 14.5 %copy-start.10 = (s32[1,1,5,256,4]{3,4,2,1,0:T(4,128)S(1)}, s32[1,1,5,256,4]{3,4,2,1,0:T(4,128)}, u32[]{:S(2)}) copy-start(s32[1,1,5,256,4]{3,4,2,1,0:T(4,128)} %param.24) | copy-start | bytes 61444
  49.2 11.3 %copy-start.16 = (s32[1,1,128]{2,1,0:T(1,128)S(1)}, s32[1,1,128]{2,1,0:T(1,128)}, u32[]{:S(2)}) copy-start(s32[1,1,128]{2,1,0:T(1,128)} %param.26) | copy-start | bytes 1540
  49.2 11.3 %copy-start.6 = (bf16[1,1,128,256]{3,2,1,0:T(8,128)(2,1)S(1)}, bf16[1,1,128,256]{3,2,1,0:T(8,128)(2,1)}, u32[]{:S(2)}) copy-start(bf16[1,1,128,256]{3,2,1,0:T(8,128)(2,1)} %param.29) | copy-start | bytes 196612
  49.2 24.8 %all-to-all-start.1 = ((bf16[32,32,256]{2,1,0:T(8,128)(2,1)}), bf16[32,32,256]{2,1,0:T(8,128)(2,1)S(1)}, u32[]{:S(2)}, u32[]{:S(2)}) async-start(bf16[32,32,256]{2,1,0:T(8,128)(2,1)} %bitcast.15), calls=%async_computation.1 | async-start | bytes 1048576 | tf_op jit(solution)/shard_map/all_to_all | solution.py:88
  58.7 4.5 copy-start.14
  63.2 11.0 %copy-start.11 = (s32[256,1]{0,1:T(1,128)}, s32[256,1]{0,1:T(1,128)S(1)}, u32[]{:S(2)}) copy-start(s32[256,1]{0,1:T(1,128)S(1)} %compare_select_fusion.6) | copy-start | bytes 3076
  112.5 2.4 copy-start.2
  186.4 2.8 copy-start.13
  190.5 7.6 %copy-start.1 = (f32[5,256,256]{2,1,0:T(8,128)S(1)}, f32[5,256,256]{2,1,0:T(8,128)}, u32[]{:S(2)}) copy-start(f32[5,256,256]{2,1,0:T(8,128)} %fusion.28) | copy-start | bytes 3932164
  190.5 7.6 %copy-start.4 = (f32[1,256,256]{2,1,0:T(8,128)S(1)}, f32[1,256,256]{2,1,0:T(8,128)}, u32[]{:S(2)}) copy-start(f32[1,256,256]{2,1,0:T(8,128)} %convolution_bitcast_fusion.3) | copy-start | bytes 786436
  190.5 7.6 %copy-start.5 = (f32[1,256,256]{2,1,0:T(8,128)S(1)}, f32[1,256,256]{2,1,0:T(8,128)}, u32[]{:S(2)}) copy-start(f32[1,256,256]{2,1,0:T(8,128)} %convolution_bitcast_fusion.2) | copy-start | bytes 786436
  190.5 31.7 %all-to-all-start.2 = ((f32[32,32,256]{2,1,0:T(8,128)}), f32[32,32,256]{2,1,0:T(8,128)S(1)}, u32[]{:S(2)}, u32[]{:S(2)}) async-start(f32[32,32,256]{2,1,0:T(8,128)} %bitcast.41), calls=%async_computation.2 | async-start | bytes 2097152 | tf_op jit(solution)/shard_map/all_to_all | solution.py:127
  196.7 294.8 %all-reduce.3.cloned.1.call-start = ((), (), s32[]{:S(2)}) async-start(), calls=%async_computation.5 | async-start | bytes 6291456 | tf_op jit(solution)/shard_map/psum | solution.py:121
  200.1 0.8 copy-start.9
  200.1 29.0 %copy-start.3 = (bf16[2,6,256,256]{3,2,1,0:T(8,128)(2,1)S(1)}, bf16[2,6,256,256]{3,2,1,0:T(8,128)(2,1)}, u32[]{:S(2)}) copy-start(bf16[2,6,256,256]{3,2,1,0:T(8,128)(2,1)} %param.20) | copy-start | bytes 4718596
  200.1 29.0 %copy-start.7 = (bf16[5,128,256]{2,1,0:T(8,128)(2,1)S(1)}, bf16[5,128,256]{2,1,0:T(8,128)(2,1)}, u32[]{:S(2)}) copy-start(bf16[5,128,256]{2,1,0:T(8,128)(2,1)} %get-tuple-element.112) | copy-start | bytes 983044
  200.1 294.7 %reduce-scatter.2.cloned.1.call-start = ((), (), s32[]{:S(2)}) async-start(), calls=%async_computation.4 | async-start | bytes 557056 | tf_op jit(solution)/shard_map/reduce_scatter | solution.py:133
Sparse Core Ops, SparseCore 0:
  203.2 288.1 all-reduce.2
Sparse Core Ops, SparseCore 1:
  229.1 61.6 reduce-scatter.1
where the time goes:
time: 504 us; the launch traced here: 502 us
  waiting for transfers between devices  293 us (58%)
  other arithmetic  98.2 us (19%)
  local copies, waits for them, and re-layouts  54.5 us (11%)
  starting transfers between devices  26.5 us (5%)
  between operations  15.8 us (3%)
  matrix products  13.2 us (3%)
    psum x1, waiting for transfers between devices, body(): grad_bottom, grad_top = lax.psum((grad_bottom, grad_top), ('dp', 'table'))  261 us
    scatter-add x10, other arithmetic, spread_single(): running.at[indices.reshape(-1)].add(placed.reshape(-1, part_grad.shape[-1]))  53.1 us
    gather x20, local copies, waits for them, and re-layouts, aggregate_single(): features[indices]  30.4 us
    all_to_all x1, waiting for transfers between devices, body(): lax.all_to_all(slot_grads, 'table', split_axis=0, concat_axis=0, tiled=True)  20.5 us
    all_to_all x1, waiting for transfers between devices, body(): lax.all_to_all(found, 'table', split_axis=0, concat_axis=0, tiled=True)  10.7 us
    all_to_all x1, starting transfers between devices, body(): lax.all_to_all(wanted, 'table', split_axis=0, concat_axis=0, tiled=True)  10.6 us
  transfers between devices with their start and end apart: 5, of which 3 were waited for; matrix products, arithmetic and copies ran while one was open for 9% of the time, Pallas kernels for 0%

commit v1 on v0

v1 whole, which is shorter than its diff:
```python
import jax
import jax.numpy as jnp
from jax import lax
from jax.experimental import pallas as pl
from jax.experimental.pallas import tpu as pltpu
from jax.sharding import PartitionSpec as P

BF = jnp.bfloat16
F32 = jnp.float32
PARAMS = pltpu.CompilerParams(vmem_limit_bytes=48 * 1024 * 1024)


def dot(a, b):
    return lax.dot_general(a, b, (((1,), (0,)), ((), ())), preferred_element_type=F32)


def dot_nt(a, b):
    return lax.dot_general(a, b, (((1,), (1,)), ((), ())), preferred_element_type=F32)


def two_part(x):
    high = x.astype(BF)
    return high, (x - high.astype(F32)).astype(BF)


def gather_kernel(asked_ref, table_ref, out_ref, hot_ref):
    groups, width = asked_ref.shape
    rows = table_ref.shape[0]
    columns = jnp.transpose(asked_ref[...].astype(F32))
    lanes = lax.broadcasted_iota(jnp.int32, (width, rows), 1).astype(F32)
    for j in range(groups):
        hot_ref[pl.ds(j * width, width), :] = jnp.where(
            lanes == columns[:, j : j + 1], 1.0, 0.0
        ).astype(BF)
    out_ref[...] = dot(hot_ref[...], table_ref[...]).astype(BF)


def counts_of(selfs, edges_ref, degree_ref, out_ref, height):
    relations, fan, nodes = edges_ref.shape
    slots = lax.broadcasted_iota(jnp.int32, (height, nodes), 0)
    out_ref[:, 0:nodes] = jnp.where(slots == selfs, 1.0, 0.0).astype(BF)
    for r in range(relations):
        degree = degree_ref[r : r + 1, :]
        total = None
        for f in range(fan):
            edge = jnp.where(degree > f, edges_ref[r, f : f + 1, :], -1)
            hit = jnp.where(slots == edge, 1.0, 0.0)
            total = hit if total is None else total + hit
        out_ref[:, (r + 1) * nodes : (r + 2) * nodes] = total.astype(BF)


def inverse_columns(degree_ref):
    relations, nodes = degree_ref.shape
    inverse = 1.0 / degree_ref[...].astype(F32)
    padded = jnp.concatenate([inverse, jnp.ones((8 - relations, nodes), F32)], axis=0)
    return jnp.transpose(padded)


def prepare_kernel(
    self1_ref,
    edges1_ref,
    degree1_ref,
    self2_ref,
    edges2_ref,
    degree2_ref,
    weights_ref,
    cot_ref,
    m1_ref,
    m2_ref,
    wt_ref,
    back_ref,
    column_ref,
    high_ref,
    low_ref,
):
    counts_of(self1_ref[...], edges1_ref, degree1_ref, m1_ref, m1_ref.shape[0])
    counts_of(self2_ref[...], edges2_ref, degree2_ref, m2_ref, m2_ref.shape[0])
    layers, kinds = weights_ref.shape[0], weights_ref.shape[1]
    for layer in range(layers):
        for r in range(kinds):
            wt_ref[layer, r] = jnp.transpose(weights_ref[layer, r].astype(F32)).astype(BF)
    column_ref[...] = inverse_columns(degree1_ref)
    column2 = inverse_columns(degree2_ref)
    seeds = cot_ref.shape[0]
    cot = cot_ref[...]
    for r in range(kinds):
        part = dot_nt(cot, weights_ref[1, r])
        if r > 0:
            part = part * column2[:, r - 1 : r]
        high, low = two_part(part)
        high_ref[pl.ds(r * seeds, seeds), :] = high
        low_ref[pl.ds(r * seeds, seeds), :] = low
    m2 = m2_ref[...]
    back_ref[...] = jnp.transpose(dot(m2, high_ref[...]) + dot(m2, low_ref[...]))


def main_kernel(
    count_ref,
    core_ref,
    x_ref,
    m1_ref,
    m2_ref,
    wt_ref,
    back_ref,
    column_ref,
    degree1_ref,
    degree2_ref,
    cot_ref,
    node_ref,
    slot_ref,
    keep_ref,
    send_ref,
    live_ref,
    agg_ref,
    agg2_ref,
    spread_ref,
):
    shards = count_ref.shape[1]
    slots, feature = x_ref.shape
    width = slots // shards
    kinds = wt_ref.shape[1]
    nodes = degree1_ref.shape[1]
    seeds = degree2_ref.shape[1]
    position = lax.broadcasted_iota(jnp.int32, (width, feature), 0)
    for k in range(shards):
        rows = x_ref[pl.ds(k * width, width), :].astype(F32)
        live_ref[pl.ds(k * width, width), :] = jnp.where(position < count_ref[0, k], rows, 0.0)
    xt = jnp.transpose(live_ref[...]).astype(BF)
    inverse1 = 1.0 / degree1_ref[...].astype(F32)
    inverse2 = 1.0 / degree2_ref[...].astype(F32)
    pre = None
    for r in range(kinds):
        part = dot(xt, m1_ref[:, r * nodes : (r + 1) * nodes])
        if r > 0:
            part = part * inverse1[r - 1 : r, :]
        part = part.astype(BF)
        agg_ref[:, r * nodes : (r + 1) * nodes] = part
        term = dot(wt_ref[0, r], part)
        pre = term if pre is None else pre + term
    logistic = 1.0 / (1.0 + jnp.exp(-pre))
    hidden = (pre * logistic).astype(BF)
    slope = logistic * (1.0 + pre * (1.0 - logistic))
    grad_pre = jnp.transpose(back_ref[...] * slope).astype(BF)
    out = None
    for r in range(kinds):
        part = dot(hidden, m2_ref[:, r * seeds : (r + 1) * seeds])
        if r > 0:
            part = part * inverse2[r - 1 : r, :]
        part = part.astype(BF)
        agg2_ref[:, r * seeds : (r + 1) * seeds] = part
        term = dot(wt_ref[1, r], part)
        out = term if out is None else out + term
    node_ref[...] = jnp.transpose(out).astype(BF)
    for r in range(kinds):
        part = dot(grad_pre, wt_ref[0, r])
        if r > 0:
            part = part * column_ref[:, r - 1 : r]
        spread_ref[pl.ds(r * nodes, nodes), :] = part.astype(BF)
    live_ref[...] = dot(m1_ref[...], spread_ref[...])
    for k in range(shards):
        rows = live_ref[pl.ds(k * width, width), :]
        slot_ref[pl.ds(k * width, width), :] = jnp.where(
            position < count_ref[0, k], rows, 0.0
        ).astype(BF)

    def bottom(r):
        return dot(agg_ref[:, r * nodes : (r + 1) * nodes], grad_pre)

    def top(r):
        return dot(agg2_ref[:, r * seeds : (r + 1) * seeds], cot_ref[...])

    @pl.when(core_ref[0] == 0)
    def first():
        for r in range(kinds):
            keep_ref[r] = bottom(r)
            send_ref[r] = top(r).astype(BF)

    @pl.when(core_ref[0] != 0)
    def second():
        for r in range(kinds):
            keep_ref[r] = top(r)
            send_ref[r] = bottom(r).astype(BF)


def scatter_kernel(asked_ref, back_ref, core_ref, out_ref):
    shards, height, feature = back_ref.shape
    groups, piece = out_ref.shape[0], out_ref.shape[1]
    width = asked_ref.shape[1] // shards
    rows = 512
    share = rows // groups
    grads = back_ref[:, 0:width, :].reshape(shards * width, feature)
    index = lax.broadcasted_iota(jnp.int32, (rows, shards * width), 0)
    hot = jnp.where(index == asked_ref[...], 1.0, 0.0).astype(BF)
    dense = dot(hot, grads)
    out_ref[:, 0:share, :] = dense.reshape(groups, share, feature).astype(BF)


def whole(n):
    return [pl.BlockSpec(memory_space=pltpu.VMEM)] * n


def shaped(shape, kind):
    return jax.ShapeDtypeStruct(shape, kind)


def body(
    table,
    weights,
    fetch_rows,
    fetch_count,
    first_self,
    first_edges,
    first_degree,
    second_self,
    second_edges,
    second_degree,
    cotangent,
):
    wanted = fetch_rows[0, 0]
    shards, width = wanted.shape
    rows, feature = table.shape
    slots = shards * width
    kinds = weights.shape[1]
    nodes = first_self.shape[2]
    seeds = second_self.shape[2]
    groups = lax.axis_size("dp")
    chips = groups // 2
    core = lax.axis_index("dp") % 2
    swap = [(i, i ^ 1) for i in range(groups)]
    lines = [[c + 2 * z for z in range(chips)] for c in range(2)]
    smem = pl.BlockSpec(memory_space=pltpu.SMEM)

    asked = lax.all_to_all(wanted, "table", split_axis=0, concat_axis=0, tiled=True)

    degree1 = first_degree[0, 0]
    degree2 = second_degree[0, 0]
    cot = cotangent[0, 0]
    m1, m2, wt, back, column = pl.pallas_call(
        prepare_kernel,
        out_shape=(
            shaped((slots, kinds * nodes), BF),
            shaped((nodes, kinds * seeds), BF),
            shaped(weights.shape, BF),
            shaped((feature, nodes), F32),
            shaped((nodes, 8), F32),
        ),
        in_specs=whole(8),
        out_specs=tuple(whole(5)),
        scratch_shapes=[
            pltpu.VMEM((kinds * seeds, feature), BF),
            pltpu.VMEM((kinds * seeds, feature), BF),
        ],
        compiler_params=PARAMS,
        name="prepare",
    )(
        first_self[0],
        jnp.swapaxes(first_edges[0, 0], 1, 2),
        degree1,
        second_self[0],
        jnp.swapaxes(second_edges[0, 0], 1, 2),
        degree2,
        weights,
        cot,
    )

    found = pl.pallas_call(
        gather_kernel,
        out_shape=shaped((slots, feature), BF),
        in_specs=whole(2),
        out_specs=whole(1)[0],
        scratch_shapes=[pltpu.VMEM((slots, rows), BF)],
        compiler_params=PARAMS,
        name="gather",
    )(asked, table)
    inputs = lax.all_to_all(found, "table", split_axis=0, concat_axis=0, tiled=True)

    node_out, slot_grads, keep, send = pl.pallas_call(
        main_kernel,
        out_shape=(
            shaped((seeds, feature), BF),
            shaped((slots, feature), BF),
            shaped((kinds, feature, feature), F32),
            shaped((kinds, feature, feature), BF),
        ),
        in_specs=[smem, smem] + whole(9),
        out_specs=tuple(whole(4)),
        scratch_shapes=[
            pltpu.VMEM((slots, feature), F32),
            pltpu.VMEM((feature, kinds * nodes), BF),
            pltpu.VMEM((feature, kinds * seeds), BF),
            pltpu.VMEM((kinds * nodes, feature), BF),
        ],
        compiler_params=PARAMS,
        name="step",
    )(
        fetch_count[0],
        core.reshape(1),
        inputs,
        m1,
        m2,
        wt,
        back,
        column,
        degree1,
        degree2,
        cot,
    )

    other = lax.ppermute(send, "dp", swap)
    half = (keep + other.astype(F32)).astype(BF)
    joined = jnp.concatenate(
        [slot_grads.reshape(shards, width, feature), half.reshape(shards, -1, feature)], axis=1
    )
    returned = lax.all_to_all(joined, "table", split_axis=0, concat_axis=0, tiled=True)

    share = rows // groups
    dense = pl.pallas_call(
        scatter_kernel,
        out_shape=shaped((groups, share, feature), BF),
        in_specs=whole(2) + [smem],
        out_specs=whole(1)[0],
        compiler_params=PARAMS,
        name="scatter",
    )(asked.reshape(1, slots), returned, core.reshape(1))
    partial = jnp.sum(returned[:, width:, :].astype(F32), axis=0)
    part_high, part_low = two_part(partial)
    parts = jnp.concatenate(
        [part_high.reshape(chips, 1, -1, feature), part_low.reshape(chips, 1, -1, feature)], axis=2
    )
    mine = lax.broadcasted_iota(jnp.int32, (1, 2, 1, 1), 1) == core
    parts = jnp.where(mine, parts, jnp.zeros((), BF)).reshape(groups, -1, feature)
    crossed = lax.all_to_all(
        jnp.concatenate([dense, parts], axis=1), "dp", split_axis=0, concat_axis=0, tiled=True
    )
    summed = jnp.sum(crossed.astype(F32), axis=0)
    table_part = summed[:share]
    piece = (summed.shape[0] - share) // 2
    total = summed[share : share + piece] + summed[share + piece :]
    batch = seeds * groups * shards
    mean = (total / jnp.sqrt(jnp.float32(batch))).astype(BF)
    stack = lax.all_to_all(
        jnp.broadcast_to(mean[None], (chips, piece, feature)).reshape(-1, feature),
        "dp",
        split_axis=0,
        concat_axis=0,
        tiled=True,
        axis_index_groups=lines,
    )
    mine_half = lax.all_to_all(
        jnp.broadcast_to(stack[None], (shards,) + stack.shape).reshape(-1, feature),
        "table",
        split_axis=0,
        concat_axis=0,
        tiled=True,
    ).reshape(kinds, feature, feature)
    other_half = lax.ppermute(mine_half, "dp", swap)
    weight_grad = jnp.stack(
        [
            jnp.where(core == 0, mine_half, other_half),
            jnp.where(core == 0, other_half, mine_half),
        ]
    )
    return (node_out[None, None], weight_grad, table_part[None])


def solution(mesh):
    return jax.shard_map(
        body,
        mesh=mesh,
        in_specs=(
            P("table", None),
            P(),
            P("dp", "table", None, None),
            P("dp", "table", None),
            P("dp", "table", None),
            P("dp", "table", None, None, None),
            P("dp", "table", None, None),
            P("dp", "table", None),
            P("dp", "table", None, None, None),
            P("dp", "table", None, None),
            P("dp", "table", None, None),
        ),
        out_specs=(P("dp", "table", None, None), P(), P("table", "dp", None)),
        check_vma=False,
    )
```

time: 504 us -> 167 us (0.33)
  waiting for transfers between devices: 293 us -> 39.3 us
  other arithmetic: 98.2 us -> 3.72 us
  blocking collectives: 0 us -> 80.9 us
  local copies, waits for them, and re-layouts: 54.5 us -> 4.93 us
  Pallas kernels: 0 us -> 17 us
  between operations: 15.8 us -> 0.91 us
  matrix products: 13.2 us -> 0 us
  starting transfers between devices: 26.5 us -> 19.4 us
    psum x1 -> x0, waiting for transfers between devices: 261 us -> none  [body(): grad_bottom, grad_top = lax.psum((grad_bottom, grad_top), ('dp', 'table'))]
    all_to_all x0 -> x4, blocking collectives: none -> 80.9 us  [the longest x1 27.2 us: body(): lax.all_to_all(jnp.concatenate([dense, parts], axis=1), 'dp', split_axis=...]
    scatter-add x13 -> x0, other arithmetic: 64.3 us -> none  [the longest x10 53.1 us: spread_single(): running.at[indices.reshape(-1)].add(placed.reshape(-1, part_grad.shape[-1]))]
    gather x23 -> x0, local copies, waits for them, and re-layouts: 37.4 us -> none  [the longest x20 30.4 us: aggregate_single(): features[indices]]
    pallas_call x0 -> x4, Pallas kernels: none -> 17 us  [the longest x1 8.41 us: body(): pl.pallas_call(prepare_kernel, out_shape=(shaped((slots, kinds * nodes),...]
    dot_general x12 -> x0, matrix products: 13.2 us -> none  [the longest x2 2.86 us: input_terms(): jnp.einsum('be,rde->rbd', grad, layer_weights[1:], preferred_element_type...]
    all_to_all x2 -> x1, starting transfers between devices: 16.8 us -> 3.95 us  [body(): lax.all_to_all(joined, 'table', split_axis=0, concat_axis=0, tiled=True)]
    ppermute x0 -> x2, starting transfers between devices: none -> 11.4 us  [the longest x1 6.44 us: body(): other = lax.ppermute(send, 'dp', swap)]
  transfers between devices with their start and end apart: 5 -> 4, of which waited for: 3 -> 4; matrix products, arithmetic and copies ran while one was open for 9% -> 1% of each run, Pallas kernels for 0% -> 5%
where the time goes in v1:
time: 167 us; the launch traced here: 166 us
  blocking collectives  80.9 us (48%)
  waiting for transfers between devices  39.3 us (24%)
  starting transfers between devices  19.4 us (12%)
  Pallas kernels  17 us (10%)
  local copies, waits for them, and re-layouts  4.93 us (3%)
  other arithmetic  3.72 us (2%)
    all_to_all x1, waiting for transfers between devices, body(): lax.all_to_all(joined, 'table', split_axis=0, concat_axis=0, tiled=True)  31.1 us
    all_to_all x1, blocking collectives, body(): lax.all_to_all(jnp.concatenate([dense, parts], axis=1), 'dp', split_axis=...  27.2 us
    all_to_all x1, blocking collectives, body(): lax.all_to_all(jnp.broadcast_to(stack[None], (shards,) + stack.shape).res...  25.4 us
    all_to_all x1, blocking collectives, body(): lax.all_to_all(wanted, 'table', split_axis=0, concat_axis=0, tiled=True)  19.2 us
    all_to_all x1, blocking collectives, body(): lax.all_to_all(jnp.broadcast_to(mean[None], (chips, piece, feature)).resh...  9.25 us
    pallas_call x1, Pallas kernels, body(): pl.pallas_call(prepare_kernel, out_shape=(shaped((slots, kinds * nodes),...  8.41 us
    pallas_call x1, Pallas kernels, body(): pl.pallas_call(main_kernel, out_shape=(shaped((seeds, feature), BF), shap...  6.78 us
    ppermute x1, starting transfers between devices, body(): other = lax.ppermute(send, 'dp', swap)  6.44 us
  transfers between devices with their start and end apart: 4, of which 4 were waited for; matrix products, arithmetic and copies ran while one was open for 1% of the time, Pallas kernels for 5%

profile of v1, /device:TPU:1, one launch (start us, length us, event | category | flops | bytes accessed | tf_op | source)
XLA Modules:
  0.0 166.1 jit_solution(18387035017299814246)
XLA Ops:
  0.6 0.0 copy-start.3
  0.6 0.0 copy-start
  0.7 19.2 %all_to_all.44 = s32[32,1,32]{2,1,0:T(1,128)S(1)} all-to-all(s32[32,1,32]{2,1,0:T(1,128)} %bitcast.52), channel_id=1, replica_groups=mesh['dp'=16,'table'=32] {'table'}, dimensions={0} | all-to-all | bytes 8192 | tf_op jit(solution)/shard_map/all_to_all | solution.py:233
  19.8 0.0 copy-start.4
  19.8 0.9 copy-done.4
  20.8 0.0 copy-start.11
  20.8 0.0 copy-start.10
  20.8 0.0 copy-start.7
  20.8 0.0 copy-start.8
  20.8 1.4 gather.1
  22.2 4.0 %all-to-all-start.1 = ((bf16[32,32,256]{2,1,0:T(8,128)(2,1)}), bf16[32,32,256]{2,1,0:T(8,128)(2,1)S(1)}, u32[]{:S(2)}, u32[]{:S(2)}) async-start(bf16[32,32,256]{2,1,0:T(8,128)(2,1)} %bitcast.4), calls=%async_computation.1 | async-start | bytes 1048576 | tf_op jit(solution)/shard_map/all_to_all | solution.py:275
  26.2 0.0 copy-done.11
  26.2 0.0 copy-done.10
  26.2 0.0 copy-done.3
  26.3 0.0 copy-done
  26.3 0.0 copy-done.5
  26.3 0.0 copy-done.6
  26.3 0.0 copy-done.7
  26.3 0.0 copy-done.8
  26.3 8.4 %prepare.1 = (bf16[1024,1536]{1,0:T(8,128)(2,1)}, bf16[256,768]{1,0:T(8,128)(2,1)S(1)}, bf16[2,6,256,256]{3,2,1,0:T(8,128)(2,1)S(1)}, f32[256,256]{1,0:T(8,128)S(1)}, f32[256,8]{1,0:T(8,128)S(1)}) custom-call(s32[1,256]{1,0:T(1,128)S(1)} %bitcast.46, s32[5,4,256]{2,1,0:T(4,128)S(1)} %bitcast.44, s32[5,256]{1,0:T(8,128)S(1)} %bitcast.40, ...), custom_call_target="tpu_custom_call" | custom-call | tf_op jit(solution)/shard_map/prepare/pallas_call | solution.py:238
  34.7 1.1 copy-done.1
  35.9 5.0 %all-to-all-done.1 = bf16[32,32,256]{2,1,0:T(8,128)(2,1)S(1)} async-done(((bf16[32,32,256]{2,1,0:T(8,128)(2,1)}), bf16[32,32,256]{2,1,0:T(8,128)(2,1)S(1)}, u32[]{:S(2)}, u32[]{:S(2)}) %all-to-all-start.1) | async-done | bytes 524320 | tf_op jit(solution)/shard_map/all_to_all | solution.py:275
  40.8 0.0 copy-done.9
  40.8 1.4 copy-done.2
  42.3 6.8 %step.1 = (bf16[128,256]{1,0:T(8,128)(2,1)}, bf16[1024,256]{1,0:T(8,128)(2,1)S(1)}, f32[6,256,256]{2,1,0:T(8,128)S(1)}, bf16[6,256,256]{2,1,0:T(8,128)(2,1)S(1)}) custom-call(s32[1,32]{1,0:T(1,128)S(1)} %bitcast.48, s32[1]{0:T(128)} %bitcast.1.core_ref, bf16[1024,256]{1,0:T(8,128)(2,1)S(1)} %bitcast.35, bf16[1024,1536]{1,0:T(8,128)(2,1)} %get-tuple-element.12.m1_ref, ...), custom_call_target="tpu_custom_call" | custom-call | tf_op jit(solution)/shard_map/step/pallas_call | solution.py:277
  49.0 6.4 %collective-permute-start = (bf16[6,256,256]{2,1,0:T(8,128)(2,1)S(1)}, bf16[6,256,256]{2,1,0:T(8,128)(2,1)S(1)}, u32[]{:S(2)}, u32[]{:S(2)}) collective-permute-start(bf16[6,256,256]{2,1,0:T(8,128)(2,1)S(1)} %get-tuple-element.20), channel_id=1, source_target_pairs={{0,32},{32,0},{64,96},{96,64},{128,160},{160,128},{192,224},{224,1... | collective-permute-start | bytes 2359304 | tf_op jit(solution)/shard_map/ppermute | solution.py:309
  55.5 1.9 %collective-permute-done = bf16[6,256,256]{2,1,0:T(8,128)(2,1)S(1)} collective-permute-done((bf16[6,256,256]{2,1,0:T(8,128)(2,1)S(1)}, bf16[6,256,256]{2,1,0:T(8,128)(2,1)S(1)}, u32[]{:S(2)}, u32[]{:S(2)}) %collective-permute-start) | collective-permute-done | bytes 786464 | tf_op jit(solution)/shard_map/ppermute | solution.py:309
  57.4 0.2 add_convert_fusion
  57.6 1.1 pad_maximum_fusion.1
  58.8 4.0 %all-to-all-start.2 = ((bf16[32,80,256]{2,1,0:T(8,128)(2,1)}), bf16[32,80,256]{2,1,0:T(8,128)(2,1)S(1)}, u32[]{:S(2)}, u32[]{:S(2)}) async-start(bf16[32,80,256]{2,1,0:T(8,128)(2,1)} %pad_maximum_fusion.1), calls=%async_computation.2 | async-start | bytes 2621440 | tf_op jit(solution)/shard_map/all_to_all | solution.py:314
  62.7 0.1 broadcast_in_dim.50
  62.8 0.5 broadcast.15
  63.3 0.6 reduce.3
  64.0 0.1 reshape.80.asked_ref
  64.0 31.1 %all-to-all-done.2.back_ref = bf16[32,80,256]{2,1,0:T(8,128)(2,1)S(1)} async-done(((bf16[32,80,256]{2,1,0:T(8,128)(2,1)}), bf16[32,80,256]{2,1,0:T(8,128)(2,1)S(1)}, u32[]{:S(2)}, u32[]{:S(2)}) %all-to-all-start.2) | async-done | bytes 1310752 | tf_op jit(solution)/shard_map/all_to_all | solution.py:314
  95.2 0.1 convert_reduce_fusion
  95.3 0.1 bitcast_select_fusion
  95.4 0.4 scatter.1
  95.9 27.2 %all_to_all.45 = bf16[16,44,256]{2,1,0:T(8,128)(2,1)S(1)} all-to-all(bf16[16,44,256]{2,1,0:T(8,128)(2,1)S(1)} %pad_maximum_fusion.2), channel_id=1, replica_groups=mesh['dp'=16,'table'=32] {'dp'}, dimensions={0} | all-to-all | bytes 720896 | tf_op jit(solution)/shard_map/all_to_all | solution.py:332
  123.1 0.1 convert_reduce_fusion.1
  123.2 9.2 %all_to_all.46 = bf16[8,6,256]{2,1,0:T(8,128)(2,1)S(1)} all-to-all(bf16[8,6,256]{2,1,0:T(8,128)(2,1)S(1)} %broadcast_in_dim.56), channel_id=1, replica_groups={{0,64,128,192,256,320,384,448},{32,96,160,224,288,352,416,480},{1,65,12..., dimensions={0} | all-to-all | bytes 49152 | tf_op jit(solution)/shard_map/all_to_all | solution.py:341
  132.4 0.1 broadcast_in_dim.58
  132.5 25.4 %all_to_all.47 = bf16[32,48,256]{2,1,0:T(8,128)(2,1)S(1)} all-to-all(bf16[32,48,256]{2,1,0:T(8,128)(2,1)S(1)} %broadcast_in_dim.58), channel_id=1, replica_groups=mesh['dp'=16,'table'=32] {'table'}, dimensions={0} | all-to-all | bytes 1572864 | tf_op jit(solution)/shard_map/all_to_all | solution.py:349
  157.9 5.0 %collective-permute-start.1 = (bf16[6,256,256]{2,1,0:T(8,128)(2,1)S(1)}, bf16[6,256,256]{2,1,0:T(8,128)(2,1)S(1)}, u32[]{:S(2)}, u32[]{:S(2)}) collective-permute-start(bf16[6,256,256]{2,1,0:T(8,128)(2,1)S(1)} %bitcast.50), channel_id=1, source_target_pairs={{0,32},{32,0},{64,96},{96,64},{128,160},{160,128},{192,224},{224,1... | collective-permute-start | bytes 2359304 | tf_op jit(solution)/shard_map/ppermute | solution.py:356
  162.8 0.6 slice_bitcast_fusion
  163.5 1.3 collective-permute-done.1
  164.7 0.1 select_bitcast_fusion.1
  164.8 1.3 pad_maximum_fusion
  (16 shorter events, 0.1 us)
Async XLA Ops:
  0.6 25.6 %copy-start.3 = (bf16[1,1,128,256]{3,2,1,0:T(8,128)(2,1)S(1)}, bf16[1,1,128,256]{3,2,1,0:T(8,128)(2,1)}, u32[]{:S(2)}) copy-start(bf16[1,1,128,256]{3,2,1,0:T(8,128)(2,1)} %param.21) | copy-start | bytes 196612
  0.6 25.6 %copy-start = (bf16[2,6,256,256]{3,2,1,0:T(8,128)(2,1)S(1)}, bf16[2,6,256,256]{3,2,1,0:T(8,128)(2,1)}, u32[]{:S(2)}) copy-start(bf16[2,6,256,256]{3,2,1,0:T(8,128)(2,1)} %weights_ref.1) | copy-start | bytes 4718596
  19.8 1.0 copy-start.4
  20.8 5.4 %copy-start.11 = (s32[1,1,5,128]{3,1,2,0:T(1,128)S(1)}, s32[1,1,5,128]{3,1,2,0:T(1,128)}, u32[]{:S(2)}) copy-start(s32[1,1,5,128]{3,1,2,0:T(1,128)} %param.20) | copy-start | bytes 7684
  20.8 5.5 %copy-start.10 = (s32[1,1,5,256]{3,1,2,0:T(1,128)S(1)}, s32[1,1,5,256]{3,1,2,0:T(1,128)}, u32[]{:S(2)}) copy-start(s32[1,1,5,256]{3,1,2,0:T(1,128)} %param.17) | copy-start | bytes 15364
  20.8 5.5 %copy-start.5 = (s32[1,1,5,256,4]{3,4,2,1,0:T(4,128)S(1)}, s32[1,1,5,256,4]{3,4,2,1,0:T(4,128)}, u32[]{:S(2)}) copy-start(s32[1,1,5,256,4]{3,4,2,1,0:T(4,128)} %param.16) | copy-start | bytes 61444
  20.8 5.5 %copy-start.6 = (s32[1,1,5,128,4]{3,4,2,1,0:T(4,128)S(1)}, s32[1,1,5,128,4]{3,4,2,1,0:T(4,128)}, u32[]{:S(2)}) copy-start(s32[1,1,5,128,4]{3,4,2,1,0:T(4,128)} %param.19) | copy-start | bytes 30724
  20.8 5.5 %copy-start.7 = (s32[1,1,256]{2,1,0:T(1,128)S(1)}, s32[1,1,256]{2,1,0:T(1,128)}, u32[]{:S(2)}) copy-start(s32[1,1,256]{2,1,0:T(1,128)} %param.15) | copy-start | bytes 3076
  20.8 5.5 %copy-start.8 = (s32[1,1,128]{2,1,0:T(1,128)S(1)}, s32[1,1,128]{2,1,0:T(1,128)}, u32[]{:S(2)}) copy-start(s32[1,1,128]{2,1,0:T(1,128)} %param.18) | copy-start | bytes 1540
  22.2 18.7 %copy-start.9 = (s32[1,1,32]{2,1,0:T(1,128)S(1)}, s32[1,1,32]{2,1,0:T(1,128)}, u32[]{:S(2)}) copy-start(s32[1,1,32]{2,1,0:T(1,128)} %param.14) | copy-start | bytes 388
  22.2 18.7 %all-to-all-start.1 = ((bf16[32,32,256]{2,1,0:T(8,128)(2,1)}), bf16[32,32,256]{2,1,0:T(8,128)(2,1)S(1)}, u32[]{:S(2)}, u32[]{:S(2)}) async-start(bf16[32,32,256]{2,1,0:T(8,128)(2,1)} %bitcast.4), calls=%async_computation.1 | async-start | bytes 1048576 | tf_op jit(solution)/shard_map/all_to_all | solution.py:275
  34.7 1.1 copy-start.1
  40.8 1.4 copy-start.2
  49.0 8.3 %collective-permute-start = (bf16[6,256,256]{2,1,0:T(8,128)(2,1)S(1)}, bf16[6,256,256]{2,1,0:T(8,128)(2,1)S(1)}, u32[]{:S(2)}, u32[]{:S(2)}) collective-permute-start(bf16[6,256,256]{2,1,0:T(8,128)(2,1)S(1)} %get-tuple-element.20), channel_id=1, source_target_pairs={{0,32},{32,0},{64,96},{96,64},{128,160},{160,128},{192,224},{224,1... | collective-permute-start | bytes 2359304 | tf_op jit(solution)/shard_map/ppermute | solution.py:309
  58.8 36.4 %all-to-all-start.2 = ((bf16[32,80,256]{2,1,0:T(8,128)(2,1)}), bf16[32,80,256]{2,1,0:T(8,128)(2,1)S(1)}, u32[]{:S(2)}, u32[]{:S(2)}) async-start(bf16[32,80,256]{2,1,0:T(8,128)(2,1)} %pad_maximum_fusion.1), calls=%async_computation.2 | async-start | bytes 2621440 | tf_op jit(solution)/shard_map/all_to_all | solution.py:314
  157.9 6.9 %collective-permute-start.1 = (bf16[6,256,256]{2,1,0:T(8,128)(2,1)S(1)}, bf16[6,256,256]{2,1,0:T(8,128)(2,1)S(1)}, u32[]{:S(2)}, u32[]{:S(2)}) collective-permute-start(bf16[6,256,256]{2,1,0:T(8,128)(2,1)S(1)} %bitcast.50), channel_id=1, source_target_pairs={{0,32},{32,0},{64,96},{96,64},{128,160},{160,128},{192,224},{224,1... | collective-permute-start | bytes 2359304 | tf_op jit(solution)/shard_map/ppermute | solution.py:356

commit v2 on v1

--- a/solution.py
+++ b/solution.py
@@ -102,18 +102,16 @@
     m2_ref,
     wt_ref,
     back_ref,
-    column_ref,
     degree1_ref,
     degree2_ref,
     cot_ref,
     node_ref,
-    slot_ref,
+    grad_ref,
     keep_ref,
     send_ref,
     live_ref,
     agg_ref,
     agg2_ref,
-    spread_ref,
 ):
     shards = count_ref.shape[1]
     slots, feature = x_ref.shape
@@ -151,6 +149,35 @@
         term = dot(wt_ref[1, r], part)
         out = term if out is None else out + term
     node_ref[...] = jnp.transpose(out).astype(BF)
+    grad_ref[...] = grad_pre
+
+    def bottom(r):
+        return dot(agg_ref[:, r * nodes : (r + 1) * nodes], grad_pre)
+
+    def top(r):
+        return dot(agg2_ref[:, r * seeds : (r + 1) * seeds], cot_ref[...])
+
+    @pl.when(core_ref[0] == 0)
+    def first():
+        for r in range(kinds):
+            keep_ref[r] = bottom(r)
+            send_ref[r] = top(r).astype(BF)
+
+    @pl.when(core_ref[0] != 0)
+    def second():
+        for r in range(kinds):
+            keep_ref[r] = top(r)
+            send_ref[r] = bottom(r).astype(BF)
+
+
+def slots_kernel(count_ref, grad_ref, m1_ref, wt_ref, column_ref, slot_ref, spread_ref, live_ref):
+    shards = count_ref.shape[1]
+    slots, feature = slot_ref.shape
+    width = slots // shards
+    kinds = wt_ref.shape[1]
+    nodes = grad_ref.shape[0]
+    position = lax.broadcasted_iota(jnp.int32, (width, feature), 0)
+    grad_pre = grad_ref[...]
     for r in range(kinds):
         part = dot(grad_pre, wt_ref[0, r])
         if r > 0:
@@ -163,36 +190,14 @@
             position < count_ref[0, k], rows, 0.0
         ).astype(BF)
 
-    def bottom(r):
-        return dot(agg_ref[:, r * nodes : (r + 1) * nodes], grad_pre)
-
-    def top(r):
-        return dot(agg2_ref[:, r * seeds : (r + 1) * seeds], cot_ref[...])
-
-    @pl.when(core_ref[0] == 0)
-    def first():
-        for r in range(kinds):
-            keep_ref[r] = bottom(r)
-            send_ref[r] = top(r).astype(BF)
-
-    @pl.when(core_ref[0] != 0)
-    def second():
-        for r in range(kinds):
-            keep_ref[r] = top(r)
-            send_ref[r] = bottom(r).astype(BF)
-
-
-def scatter_kernel(asked_ref, back_ref, core_ref, out_ref):
-    shards, height, feature = back_ref.shape
-    groups, piece = out_ref.shape[0], out_ref.shape[1]
-    width = asked_ref.shape[1] // shards
-    rows = 512
-    share = rows // groups
-    grads = back_ref[:, 0:width, :].reshape(shards * width, feature)
-    index = lax.broadcasted_iota(jnp.int32, (rows, shards * width), 0)
+
+def scatter_kernel(asked_ref, grads_ref, out_ref):
+    groups, share, feature = out_ref.shape
+    rows = groups * share
+    index = lax.broadcasted_iota(jnp.int32, (rows, asked_ref.shape[1]), 0)
     hot = jnp.where(index == asked_ref[...], 1.0, 0.0).astype(BF)
-    dense = dot(hot, grads)
-    out_ref[:, 0:share, :] = dense.reshape(groups, share, feature).astype(BF)
+    dense = dot(hot, grads_ref[...])
+    out_ref[...] = dense.reshape(groups, share, feature).astype(BF)
 
 
 def whole(n):
@@ -227,7 +232,26 @@
     chips = groups // 2
     core = lax.axis_index("dp") % 2
     swap = [(i, i ^ 1) for i in range(groups)]
-    lines = [[c + 2 * z for z in range(chips)] for c in range(2)]
+    both = ("dp", "table")
+    down = 8
+    across = shards // down
+
+    def device(z, c, y, x):
+        return ((z * 2 + c) * down + y) * across + x
+
+    planes = [
+        [device(z, 0, y, x) for y in range(down) for x in range(across)] for z in range(chips)
+    ] + [[device(z, 1, y, x) for z in range(chips) for x in range(across)] for y in range(down)]
+
+    def exchange(stride):
+        pairs = []
+        for z in range(chips):
+            for y in range(down):
+                for x in range(across):
+                    pairs.append((device(z, 0, y, x), device(z ^ stride, 0, y, x)))
+                    pairs.append((device(z, 1, y, x), device(z, 1, y ^ stride, x)))
+        return pairs
+
     smem = pl.BlockSpec(memory_space=pltpu.SMEM)
 
     asked = lax.all_to_all(wanted, "table", split_axis=0, concat_axis=0, tiled=True)
@@ -274,21 +298,20 @@
     )(asked, table)
     inputs = lax.all_to_all(found, "table", split_axis=0, concat_axis=0, tiled=True)
 
-    node_out, slot_grads, keep, send = pl.pallas_call(
+    node_out, grad_pre, keep, send = pl.pallas_call(
         main_kernel,
         out_shape=(
             shaped((seeds, feature), BF),
-            shaped((slots, feature), BF),
+            shaped((nodes, feature), BF),
             shaped((kinds, feature, feature), F32),
             shaped((kinds, feature, feature), BF),
         ),
-        in_specs=[smem, smem] + whole(9),
+        in_specs=[smem, smem] + whole(8),
         out_specs=tuple(whole(4)),
         scratch_shapes=[
             pltpu.VMEM((slots, feature), F32),
             pltpu.VMEM((feature, kinds * nodes), BF),
             pltpu.VMEM((feature, kinds * seeds), BF),
-            pltpu.VMEM((kinds * nodes, feature), BF),
         ],
         compiler_params=PARAMS,
         name="step",
@@ -300,59 +323,56 @@
         m2,
         wt,
         back,
-        column,
         degree1,
         degree2,
         cot,
     )
-
     other = lax.ppermute(send, "dp", swap)
-    half = (keep + other.astype(F32)).astype(BF)
-    joined = jnp.concatenate(
-        [slot_grads.reshape(shards, width, feature), half.reshape(shards, -1, feature)], axis=1
+    slot_grads = pl.pallas_call(
+        slots_kernel,
+        out_shape=shaped((slots, feature), BF),
+        in_specs=[smem] + whole(4),
+        out_specs=whole(1)[0],
+        scratch_shapes=[
+            pltpu.VMEM((kinds * nodes, feature), BF),
+            pltpu.VMEM((slots, feature), F32),
+        ],
+        compiler_params=PARAMS,
+        name="slots",
+    )(fetch_count[0], grad_pre, m1, wt, column)
+
+    half = (keep + other.astype(F32)).astype(BF).reshape(-1, feature)
+    scattered = lax.all_to_all(
+        half, both, split_axis=0, concat_axis=0, tiled=True, axis_index_groups=planes
     )
-    returned = lax.all_to_all(joined, "table", split_axis=0, concat_axis=0, tiled=True)
+    slot_grads, scattered = lax.optimization_barrier((slot_grads, scattered))
+    returned = lax.all_to_all(slot_grads, "table", split_axis=0, concat_axis=0, tiled=True)
+    total = jnp.sum(scattered.reshape(shards, -1, feature).astype(F32), axis=0)
+    for stride in (1, 2, 4):
+        total = total + lax.ppermute(total, both, exchange(stride))
+    batch = seeds * groups * shards
+    mean = (total / jnp.sqrt(jnp.float32(batch))).astype(BF)
 
     share = rows // groups
     dense = pl.pallas_call(
         scatter_kernel,
         out_shape=shaped((groups, share, feature), BF),
-        in_specs=whole(2) + [smem],
+        in_specs=whole(2),
         out_specs=whole(1)[0],
         compiler_params=PARAMS,
         name="scatter",
-    )(asked.reshape(1, slots), returned, core.reshape(1))
-    partial = jnp.sum(returned[:, width:, :].astype(F32), axis=0)
-    part_high, part_low = two_part(partial)
-    parts = jnp.concatenate(
-        [part_high.reshape(chips, 1, -1, feature), part_low.reshape(chips, 1, -1, feature)], axis=2
-    )
-    mine = lax.broadcasted_iota(jnp.int32, (1, 2, 1, 1), 1) == core
-    parts = jnp.where(mine, parts, jnp.zeros((), BF)).reshape(groups, -1, feature)
-    crossed = lax.all_to_all(
-        jnp.concatenate([dense, parts], axis=1), "dp", split_axis=0, concat_axis=0, tiled=True
-    )
-    summed = jnp.sum(crossed.astype(F32), axis=0)
-    table_part = summed[:share]
-    piece = (summed.shape[0] - share) // 2
-    total = summed[share : share + piece] + summed[share + piece :]
-    batch = seeds * groups * shards
-    mean = (total / jnp.sqrt(jnp.float32(batch))).astype(BF)
-    stack = lax.all_to_all(
-        jnp.broadcast_to(mean[None], (chips, piece, feature)).reshape(-1, feature),
-        "dp",
+    )(asked.reshape(1, slots), returned)
+    mine_half = lax.all_to_all(
+        jnp.broadcast_to(mean[None], (shards,) + mean.shape).reshape(-1, feature),
+        both,
         split_axis=0,
         concat_axis=0,
         tiled=True,
-        axis_index_groups=lines,
-    )
-    mine_half = lax.all_to_all(
-        jnp.broadcast_to(stack[None], (shards,) + stack.shape).reshape(-1, feature),
-        "table",
-        split_axis=0,
-        concat_axis=0,
-        tiled=True,
+        axis_index_groups=planes,
     ).reshape(kinds, feature, feature)
+    dense, mine_half = lax.optimization_barrier((dense, mine_half))
+    crossed = lax.all_to_all(dense, "dp", split_axis=0, concat_axis=0, tiled=True)
+    table_part = jnp.sum(crossed.astype(F32), axis=0)
     other_half = lax.ppermute(mine_half, "dp", swap)
     weight_grad = jnp.stack(
         [

time: 167 us -> 160 us (0.958)
  blocking collectives: 80.9 us -> 19.2 us
  starting transfers between devices: 19.4 us -> 59 us
  waiting for transfers between devices: 39.3 us -> 51 us
    all_to_all x3 -> x0, blocking collectives: 61.8 us -> none  [the longest x1 27.2 us: body(): lax.all_to_all(jnp.concatenate([dense, parts], axis=1), 'dp', split_axis=...]
    all_to_all x1 -> x4, starting transfers between devices: 3.95 us -> 33.5 us  [the longest x1 12.1 us: body(): lax.all_to_all(half, both, split_axis=0, concat_axis=0, tiled=True, axis_...]
    ppermute x0 -> x3, starting transfers between devices: none -> 13.1 us  [body(): total = total + lax.ppermute(total, both, exchange(stride))]
    ppermute x0 -> x3, waiting for transfers between devices: none -> 9.36 us  [body(): total = total + lax.ppermute(total, both, exchange(stride))]
    all_to_all x1 -> x4, waiting for transfers between devices: 31.1 us -> 35 us  [the longest x1 12.4 us: body(): lax.all_to_all(jnp.broadcast_to(mean[None], (shards,) + mean.shape).resha...]
    ppermute x1, starting transfers between devices: 4.96 us -> 1.91 us  [body(): other_half = lax.ppermute(mine_half, 'dp', swap)]
    pallas_call x0 -> x1, Pallas kernels: none -> 1.78 us  [body(): pl.pallas_call(slots_kernel, out_shape=shaped((slots, feature), BF), in_s...]
    reduce_sum x2, other arithmetic: 0.18 us -> 1.91 us  [the longest x1 1.26 us: body(): total = jnp.sum(scattered.reshape(shards, -1, feature).astype(F32), axis=0)]
  transfers between devices with their start and end apart: 4 -> 10, of which waited for: 4 -> 8; matrix products, arithmetic and copies ran while one was open for 1% -> 2% of each run, Pallas kernels for 5% -> 7%
where the time goes in v2:
time: 160 us
  starting transfers between devices  59 us (37%)
  waiting for transfers between devices  51 us (32%)
  blocking collectives  19.2 us (12%)
  Pallas kernels  18.3 us (11%)
  local copies, waits for them, and re-layouts  6.18 us (4%)
  other arithmetic  5.06 us (3%)
    all_to_all x1, blocking collectives, body(): lax.all_to_all(wanted, 'table', split_axis=0, concat_axis=0, tiled=True)  19.2 us
    ppermute x3, starting transfers between devices, body(): total = total + lax.ppermute(total, both, exchange(stride))  13.1 us
    all_to_all x1, waiting for transfers between devices, body(): lax.all_to_all(jnp.broadcast_to(mean[None], (shards,) + mean.shape).resha...  12.4 us
    all_to_all x1, starting transfers between devices, body(): lax.all_to_all(half, both, split_axis=0, concat_axis=0, tiled=True, axis_...  12.1 us
    all_to_all x1, waiting for transfers between devices, body(): lax.all_to_all(dense, 'dp', split_axis=0, concat_axis=0, tiled=True)  11.7 us
    all_to_all x1, waiting for transfers between devices, body(): lax.all_to_all(half, both, split_axis=0, concat_axis=0, tiled=True, axis_...  10.9 us
    all_to_all x1, starting transfers between devices, body(): lax.all_to_all(jnp.broadcast_to(mean[None], (shards,) + mean.shape).resha...  10.1 us
    ppermute x3, waiting for transfers between devices, body(): total = total + lax.ppermute(total, both, exchange(stride))  9.36 us
  transfers between devices with their start and end apart: 10, of which 8 were waited for; matrix products, arithmetic and copies ran while one was open for 2% of the time, Pallas kernels for 7%

profile of v2, /device:TPU:1, one launch (start us, length us, event | category | flops | bytes accessed | tf_op | source)
XLA Modules:
  0.0 159.5 jit_solution(8667927829383239447)
XLA Ops:
  0.6 0.0 copy-start.5
  0.6 19.2 %all_to_all.56 = s32[32,1,32]{2,1,0:T(1,128)S(1)} all-to-all(s32[32,1,32]{2,1,0:T(1,128)} %bitcast.54), channel_id=1, replica_groups=mesh['dp'=16,'table'=32] {'table'}, dimensions={0} | all-to-all | bytes 8192 | tf_op jit(solution)/shard_map/all_to_all | solution.py:257
  19.8 0.9 copy-done.6
  20.8 0.0 copy-start.10
  20.8 0.0 copy-start.11
  20.8 1.3 gather.1
  22.1 4.0 %all-to-all-start.1 = ((bf16[32,32,256]{2,1,0:T(8,128)(2,1)}), bf16[32,32,256]{2,1,0:T(8,128)(2,1)S(1)}, u32[]{:S(2)}, u32[]{:S(2)}) async-start(bf16[32,32,256]{2,1,0:T(8,128)(2,1)} %bitcast.4), calls=%async_computation.1 | async-start | bytes 1048576 | tf_op jit(solution)/shard_map/all_to_all | solution.py:299
  26.2 0.0 copy-done.13
  26.2 0.0 copy-done.12
  26.2 0.0 copy-done.5
  26.3 0.0 copy-start.4
  26.3 1.4 copy-done.4
  27.7 8.4 %prepare.1 = (bf16[1024,1536]{1,0:T(8,128)(2,1)}, bf16[256,768]{1,0:T(8,128)(2,1)S(1)}, bf16[2,6,256,256]{3,2,1,0:T(8,128)(2,1)S(1)}, f32[256,256]{1,0:T(8,128)S(1)}, f32[256,8]{1,0:T(8,128)S(1)}) custom-call(s32[1,256]{1,0:T(1,128)S(1)} %bitcast.48, s32[5,4,256]{2,1,0:T(4,128)S(1)} %bitcast.44, s32[5,256]{1,0:T(8,128)S(1)} %bitcast.40, ...), custom_call_target="tpu_custom_call" | custom-call | tf_op jit(solution)/shard_map/prepare/pallas_call | solution.py:262
  36.1 4.7 %all-to-all-done.1 = bf16[32,32,256]{2,1,0:T(8,128)(2,1)S(1)} async-done(((bf16[32,32,256]{2,1,0:T(8,128)(2,1)}), bf16[32,32,256]{2,1,0:T(8,128)(2,1)S(1)}, u32[]{:S(2)}, u32[]{:S(2)}) %all-to-all-start.1) | async-done | bytes 524320 | tf_op jit(solution)/shard_map/all_to_all | solution.py:299
  40.8 5.6 %step.1 = (bf16[128,256]{1,0:T(8,128)(2,1)}, bf16[256,256]{1,0:T(8,128)(2,1)S(1)}, f32[6,256,256]{2,1,0:T(8,128)S(1)}, bf16[6,256,256]{2,1,0:T(8,128)(2,1)S(1)}) custom-call(s32[1,32]{1,0:T(1,128)S(1)} %bitcast.46, s32[1]{0:T(128)} %bitcast.1.core_ref, bf16[1024,256]{1,0:T(8,128)(2,1)S(1)} %bitcast.35, bf16[1024,1536]{1,0:T(8,128)(2,1)} %get-tuple-element.16.m1_ref, ...), custom_call_target="tpu_custom_call" | custom-call | tf_op jit(solution)/shard_map/step/pallas_call | solution.py:301
  46.4 6.4 %collective-permute-start = (bf16[6,256,256]{2,1,0:T(8,128)(2,1)S(1)}, bf16[6,256,256]{2,1,0:T(8,128)(2,1)S(1)}, u32[]{:S(2)}, u32[]{:S(2)}) collective-permute-start(bf16[6,256,256]{2,1,0:T(8,128)(2,1)S(1)} %get-tuple-element.24), channel_id=1, source_target_pairs={{0,32},{32,0},{64,96},{96,64},{128,160},{160,128},{192,224},{224,1... | collective-permute-start | bytes 2359304 | tf_op jit(solution)/shard_map/ppermute | solution.py:330
  52.8 1.9 %collective-permute-done = bf16[6,256,256]{2,1,0:T(8,128)(2,1)S(1)} collective-permute-done((bf16[6,256,256]{2,1,0:T(8,128)(2,1)S(1)}, bf16[6,256,256]{2,1,0:T(8,128)(2,1)S(1)}, u32[]{:S(2)}, u32[]{:S(2)}) %collective-permute-start) | collective-permute-done | bytes 786464 | tf_op jit(solution)/shard_map/ppermute | solution.py:330
  54.7 1.1 add_convert_fusion
  55.8 12.1 %all-to-all-start.2 = ((bf16[32,48,256]{2,1,0:T(8,128)(2,1)}), bf16[32,48,256]{2,1,0:T(8,128)(2,1)}, u32[]{:S(2)}, u32[]{:S(2)}) async-start(bf16[32,48,256]{2,1,0:T(8,128)(2,1)} %bitcast.50), calls=%async_computation.2 | async-start | bytes 1572864 | tf_op jit(solution)/shard_map/all_to_all | solution.py:345
  67.9 0.0 copy-start.2
  68.0 1.4 copy-done.2
  69.4 1.8 %slots.1 = bf16[1024,256]{1,0:T(8,128)(2,1)S(1)} custom-call(s32[1,32]{1,0:T(1,128)S(1)} %bitcast.47, bf16[256,256]{1,0:T(8,128)(2,1)S(1)} %get-tuple-element.21.grad_ref, bf16[1024,1536]{1,0:T(8,128)(2,1)S(1)} %copy-done, bf16[2,6,256,256]{3,2,1,0:T(8,128)(2,1)S(1)} %copy-done.2, f32[256,8]{1,0:T(8,128)S(1)} %get-tuple-element.22.column_ref), custom_call_target="tpu_custom_call" | custom-call | tf_op jit(solution)/shard_map/slots/pallas_call | solution.py:331
  71.1 0.0 copy-start.3
  71.2 0.8 copy-done.3
  71.9 10.9 %all-to-all-done.2 = bf16[32,48,256]{2,1,0:T(8,128)(2,1)} async-done(((bf16[32,48,256]{2,1,0:T(8,128)(2,1)}), bf16[32,48,256]{2,1,0:T(8,128)(2,1)}, u32[]{:S(2)}, u32[]{:S(2)}) %all-to-all-start.2) | async-done | bytes 786464 | tf_op jit(solution)/shard_map/all_to_all | solution.py:345
  82.8 4.7 %all-to-all-start.3 = ((bf16[32,32,256]{2,1,0:T(8,128)(2,1)}), bf16[32,32,256]{2,1,0:T(8,128)(2,1)S(1)}, u32[]{:S(2)}, u32[]{:S(2)}) async-start(bf16[32,32,256]{2,1,0:T(8,128)(2,1)} %bitcast.36), calls=%async_computation.3 | async-start | bytes 1048576 | tf_op jit(solution)/shard_map/all_to_all | solution.py:349
  87.5 1.3 convert_reduce_fusion
  88.8 3.1 %collective-permute-start.1 = (f32[48,256]{1,0:T(8,128)S(1)}, f32[48,256]{1,0:T(8,128)S(1)}, u32[]{:S(2)}, u32[]{:S(2)}) collective-permute-start(f32[48,256]{1,0:T(8,128)S(1)} %convert_reduce_fusion), channel_id=1, source_target_pairs={{0,64},{32,36},{1,65},{33,37},{2,66},{34,38},{3,67},{35,39},{4,68}... | collective-permute-start | bytes 147464 | tf_op jit(solution)/shard_map/ppermute | solution.py:352
  91.9 4.3 %collective-permute-done.1 = f32[48,256]{1,0:T(8,128)S(1)} collective-permute-done((f32[48,256]{1,0:T(8,128)S(1)}, f32[48,256]{1,0:T(8,128)S(1)}, u32[]{:S(2)}, u32[]{:S(2)}) %collective-permute-start.1) | collective-permute-done | bytes 49184 | tf_op jit(solution)/shard_map/ppermute | solution.py:352
  96.2 4.0 %collective-permute-start.2 = (f32[48,256]{1,0:T(8,128)S(1)}, f32[48,256]{1,0:T(8,128)S(1)}, u32[]{:S(2)}, u32[]{:S(2)}) collective-permute-start(f32[48,256]{1,0:T(8,128)S(1)} %add.18), channel_id=1, source_target_pairs={{0,128},{32,40},{1,129},{33,41},{2,130},{34,42},{3,131},{35,43},{4... | collective-permute-start | bytes 147464 | tf_op jit(solution)/shard_map/ppermute | solution.py:352
  100.3 2.2 %collective-permute-done.2 = f32[48,256]{1,0:T(8,128)S(1)} collective-permute-done((f32[48,256]{1,0:T(8,128)S(1)}, f32[48,256]{1,0:T(8,128)S(1)}, u32[]{:S(2)}, u32[]{:S(2)}) %collective-permute-start.2) | collective-permute-done | bytes 49184 | tf_op jit(solution)/shard_map/ppermute | solution.py:352
  102.5 6.0 %collective-permute-start.3 = (f32[48,256]{1,0:T(8,128)S(1)}, f32[48,256]{1,0:T(8,128)S(1)}, u32[]{:S(2)}, u32[]{:S(2)}) collective-permute-start(f32[48,256]{1,0:T(8,128)S(1)} %add.19), channel_id=1, source_target_pairs={{0,256},{32,48},{1,257},{33,49},{2,258},{34,50},{3,259},{35,51},{4... | collective-permute-start | bytes 147464 | tf_op jit(solution)/shard_map/ppermute | solution.py:352
  108.5 2.8 %collective-permute-done.3 = f32[48,256]{1,0:T(8,128)S(1)} collective-permute-done((f32[48,256]{1,0:T(8,128)S(1)}, f32[48,256]{1,0:T(8,128)S(1)}, u32[]{:S(2)}, u32[]{:S(2)}) %collective-permute-start.3) | collective-permute-done | bytes 49184 | tf_op jit(solution)/shard_map/ppermute | solution.py:352
  111.3 0.0 all-to-all-done.3
  111.3 0.9 broadcast_in_dim.13
  112.3 10.1 %all-to-all-start.4 = ((bf16[32,48,256]{2,1,0:T(8,128)(2,1)}), bf16[32,48,256]{2,1,0:T(8,128)(2,1)S(1)}, u32[]{:S(2)}, u32[]{:S(2)}) async-start(bf16[32,48,256]{2,1,0:T(8,128)(2,1)} %broadcast_in_dim.13), calls=%async_computation.4 | async-start | bytes 1572864 | tf_op jit(solution)/shard_map/all_to_all | solution.py:365
  122.4 0.6 broadcast.6
  122.9 0.7 reduce.3
  123.6 0.1 reshape.37.asked_ref
  123.7 1.1 scatter.1
  124.8 12.4 %all-to-all-done.4 = bf16[32,48,256]{2,1,0:T(8,128)(2,1)S(1)} async-done(((bf16[32,48,256]{2,1,0:T(8,128)(2,1)}), bf16[32,48,256]{2,1,0:T(8,128)(2,1)S(1)}, u32[]{:S(2)}, u32[]{:S(2)}) %all-to-all-start.4) | async-done | bytes 786464 | tf_op jit(solution)/shard_map/all_to_all | solution.py:365
  137.2 1.9 %collective-permute-start.4 = (bf16[6,256,256]{2,1,0:T(8,128)(2,1)S(1)}, bf16[6,256,256]{2,1,0:T(8,128)(2,1)S(1)}, u32[]{:S(2)}, u32[]{:S(2)}) collective-permute-start(bf16[6,256,256]{2,1,0:T(8,128)(2,1)S(1)} %bitcast.51), channel_id=1, source_target_pairs={{0,32},{32,0},{64,96},{96,64},{128,160},{160,128},{192,224},{224,1... | collective-permute-start | bytes 2359304 | tf_op jit(solution)/shard_map/ppermute | solution.py:376
  139.2 6.6 %all-to-all-start.5 = ((bf16[16,32,256]{2,1,0:T(8,128)(2,1)}), bf16[16,32,256]{2,1,0:T(8,128)(2,1)S(1)}, u32[]{:S(2)}, u32[]{:S(2)}) async-start(bf16[16,32,256]{2,1,0:T(8,128)(2,1)} %scatter.1), calls=%async_computation.5 | async-start | bytes 524288 | tf_op jit(solution)/shard_map/all_to_all | solution.py:374
  145.7 11.7 %all-to-all-done.5 = bf16[16,32,256]{2,1,0:T(8,128)(2,1)S(1)} async-done(((bf16[16,32,256]{2,1,0:T(8,128)(2,1)}), bf16[16,32,256]{2,1,0:T(8,128)(2,1)S(1)}, u32[]{:S(2)}, u32[]{:S(2)}) %all-to-all-start.5) | async-done | bytes 262176 | tf_op jit(solution)/shard_map/all_to_all | solution.py:374
  157.5 0.7 convert_reduce_fusion.1
  158.1 0.0 collective-permute-done.4
  158.1 0.1 select_bitcast_fusion.1
  158.2 1.3 pad_maximum_fusion
  (20 shorter events, 0.1 us)
Async XLA Ops:
  0.6 25.6 %copy-start.5 = (bf16[1,1,128,256]{3,2,1,0:T(8,128)(2,1)S(1)}, bf16[1,1,128,256]{3,2,1,0:T(8,128)(2,1)}, u32[]{:S(2)}) copy-start(bf16[1,1,128,256]{3,2,1,0:T(8,128)(2,1)} %param.21) | copy-start | bytes 196612
  19.8 1.0 copy-start.6
  20.7 5.4 %copy-start.13 = (s32[1,1,5,128]{3,1,2,0:T(1,128)S(1)}, s32[1,1,5,128]{3,1,2,0:T(1,128)}, u32[]{:S(2)}) copy-start(s32[1,1,5,128]{3,1,2,0:T(1,128)} %param.20) | copy-start | bytes 7684
  20.7 5.4 %copy-start.12 = (s32[1,1,5,256]{3,1,2,0:T(1,128)S(1)}, s32[1,1,5,256]{3,1,2,0:T(1,128)}, u32[]{:S(2)}) copy-start(s32[1,1,5,256]{3,1,2,0:T(1,128)} %param.17) | copy-start | bytes 15364
  20.7 5.5 %copy-start.7 = (s32[1,1,5,256,4]{3,4,2,1,0:T(4,128)S(1)}, s32[1,1,5,256,4]{3,4,2,1,0:T(4,128)}, u32[]{:S(2)}) copy-start(s32[1,1,5,256,4]{3,4,2,1,0:T(4,128)} %param.16) | copy-start | bytes 61444
  20.7 5.5 %copy-start.8 = (s32[1,1,5,128,4]{3,4,2,1,0:T(4,128)S(1)}, s32[1,1,5,128,4]{3,4,2,1,0:T(4,128)}, u32[]{:S(2)}) copy-start(s32[1,1,5,128,4]{3,4,2,1,0:T(4,128)} %param.19) | copy-start | bytes 30724
  20.8 5.5 %copy-start.10 = (s32[1,1,256]{2,1,0:T(1,128)S(1)}, s32[1,1,256]{2,1,0:T(1,128)}, u32[]{:S(2)}) copy-start(s32[1,1,256]{2,1,0:T(1,128)} %param.15) | copy-start | bytes 3076
  20.8 5.5 %copy-start.11 = (s32[1,1,128]{2,1,0:T(1,128)S(1)}, s32[1,1,128]{2,1,0:T(1,128)}, u32[]{:S(2)}) copy-start(s32[1,1,128]{2,1,0:T(1,128)} %param.18) | copy-start | bytes 1540
  22.1 18.7 %copy-start.9 = (s32[1,1,32]{2,1,0:T(1,128)S(1)}, s32[1,1,32]{2,1,0:T(1,128)}, u32[]{:S(2)}) copy-start(s32[1,1,32]{2,1,0:T(1,128)} %param.14) | copy-start | bytes 388
  22.1 18.7 %all-to-all-start.1 = ((bf16[32,32,256]{2,1,0:T(8,128)(2,1)}), bf16[32,32,256]{2,1,0:T(8,128)(2,1)S(1)}, u32[]{:S(2)}, u32[]{:S(2)}) async-start(bf16[32,32,256]{2,1,0:T(8,128)(2,1)} %bitcast.4), calls=%async_computation.1 | async-start | bytes 1048576 | tf_op jit(solution)/shard_map/all_to_all | solution.py:299
  26.3 1.4 copy-start.4
  36.1 10.3 %copy-start.1 = (bf16[2,6,256,256]{3,2,1,0:T(8,128)(2,1)}, bf16[2,6,256,256]{3,2,1,0:T(8,128)(2,1)S(1)}, u32[]{:S(2)}) copy-start(bf16[2,6,256,256]{3,2,1,0:T(8,128)(2,1)S(1)} %get-tuple-element.18.wt_ref) | copy-start | bytes 4718596
  46.4 8.3 %collective-permute-start = (bf16[6,256,256]{2,1,0:T(8,128)(2,1)S(1)}, bf16[6,256,256]{2,1,0:T(8,128)(2,1)S(1)}, u32[]{:S(2)}, u32[]{:S(2)}) collective-permute-start(bf16[6,256,256]{2,1,0:T(8,128)(2,1)S(1)} %get-tuple-element.24), channel_id=1, source_target_pairs={{0,32},{32,0},{64,96},{96,64},{128,160},{160,128},{192,224},{224,1... | collective-permute-start | bytes 2359304 | tf_op jit(solution)/shard_map/ppermute | solution.py:330
  54.7 13.2 %copy-start = (bf16[1024,1536]{1,0:T(8,128)(2,1)S(1)}, bf16[1024,1536]{1,0:T(8,128)(2,1)}, u32[]{:S(2)}) copy-start(bf16[1024,1536]{1,0:T(8,128)(2,1)} %get-tuple-element.16.m1_ref) | copy-start | bytes 9437188
  55.8 27.0 %all-to-all-start.2 = ((bf16[32,48,256]{2,1,0:T(8,128)(2,1)}), bf16[32,48,256]{2,1,0:T(8,128)(2,1)}, u32[]{:S(2)}, u32[]{:S(2)}) async-start(bf16[32,48,256]{2,1,0:T(8,128)(2,1)} %bitcast.50), calls=%async_computation.2 | async-start | bytes 1572864 | tf_op jit(solution)/shard_map/all_to_all | solution.py:345
  67.9 1.4 copy-start.2
  71.1 0.8 copy-start.3
  82.8 28.5 %all-to-all-start.3 = ((bf16[32,32,256]{2,1,0:T(8,128)(2,1)}), bf16[32,32,256]{2,1,0:T(8,128)(2,1)S(1)}, u32[]{:S(2)}, u32[]{:S(2)}) async-start(bf16[32,32,256]{2,1,0:T(8,128)(2,1)} %bitcast.36), calls=%async_computation.3 | async-start | bytes 1048576 | tf_op jit(solution)/shard_map/all_to_all | solution.py:349
  88.8 7.5 %collective-permute-start.1 = (f32[48,256]{1,0:T(8,128)S(1)}, f32[48,256]{1,0:T(8,128)S(1)}, u32[]{:S(2)}, u32[]{:S(2)}) collective-permute-start(f32[48,256]{1,0:T(8,128)S(1)} %convert_reduce_fusion), channel_id=1, source_target_pairs={{0,64},{32,36},{1,65},{33,37},{2,66},{34,38},{3,67},{35,39},{4,68}... | collective-permute-start | bytes 147464 | tf_op jit(solution)/shard_map/ppermute | solution.py:352
  96.2 6.2 %collective-permute-start.2 = (f32[48,256]{1,0:T(8,128)S(1)}, f32[48,256]{1,0:T(8,128)S(1)}, u32[]{:S(2)}, u32[]{:S(2)}) collective-permute-start(f32[48,256]{1,0:T(8,128)S(1)} %add.18), channel_id=1, source_target_pairs={{0,128},{32,40},{1,129},{33,41},{2,130},{34,42},{3,131},{35,43},{4... | collective-permute-start | bytes 147464 | tf_op jit(solution)/shard_map/ppermute | solution.py:352
  102.5 8.8 %collective-permute-start.3 = (f32[48,256]{1,0:T(8,128)S(1)}, f32[48,256]{1,0:T(8,128)S(1)}, u32[]{:S(2)}, u32[]{:S(2)}) collective-permute-start(f32[48,256]{1,0:T(8,128)S(1)} %add.19), channel_id=1, source_target_pairs={{0,256},{32,48},{1,257},{33,49},{2,258},{34,50},{3,259},{35,51},{4... | collective-permute-start | bytes 147464 | tf_op jit(solution)/shard_map/ppermute | solution.py:352
  112.3 25.0 %all-to-all-start.4 = ((bf16[32,48,256]{2,1,0:T(8,128)(2,1)}), bf16[32,48,256]{2,1,0:T(8,128)(2,1)S(1)}, u32[]{:S(2)}, u32[]{:S(2)}) async-start(bf16[32,48,256]{2,1,0:T(8,128)(2,1)} %broadcast_in_dim.13), calls=%async_computation.4 | async-start | bytes 1572864 | tf_op jit(solution)/shard_map/all_to_all | solution.py:365
  137.2 20.9 %collective-permute-start.4 = (bf16[6,256,256]{2,1,0:T(8,128)(2,1)S(1)}, bf16[6,256,256]{2,1,0:T(8,128)(2,1)S(1)}, u32[]{:S(2)}, u32[]{:S(2)}) collective-permute-start(bf16[6,256,256]{2,1,0:T(8,128)(2,1)S(1)} %bitcast.51), channel_id=1, source_target_pairs={{0,32},{32,0},{64,96},{96,64},{128,160},{160,128},{192,224},{224,1... | collective-permute-start | bytes 2359304 | tf_op jit(solution)/shard_map/ppermute | solution.py:376
  139.2 18.3 %all-to-all-start.5 = ((bf16[16,32,256]{2,1,0:T(8,128)(2,1)}), bf16[16,32,256]{2,1,0:T(8,128)(2,1)S(1)}, u32[]{:S(2)}, u32[]{:S(2)}) async-start(bf16[16,32,256]{2,1,0:T(8,128)(2,1)} %scatter.1), calls=%async_computation.5 | async-start | bytes 524288 | tf_op jit(solution)/shard_map/all_to_all | solution.py:374

commit v3 on v2

--- a/solution.py
+++ b/solution.py
@@ -192,12 +192,9 @@
 
 
 def scatter_kernel(asked_ref, grads_ref, out_ref):
-    groups, share, feature = out_ref.shape
-    rows = groups * share
-    index = lax.broadcasted_iota(jnp.int32, (rows, asked_ref.shape[1]), 0)
+    index = lax.broadcasted_iota(jnp.int32, (out_ref.shape[0], asked_ref.shape[1]), 0)
     hot = jnp.where(index == asked_ref[...], 1.0, 0.0).astype(BF)
-    dense = dot(hot, grads_ref[...])
-    out_ref[...] = dense.reshape(groups, share, feature).astype(BF)
+    out_ref[...] = dot(hot, grads_ref[...])
 
 
 def whole(n):
@@ -243,15 +240,9 @@
         [device(z, 0, y, x) for y in range(down) for x in range(across)] for z in range(chips)
     ] + [[device(z, 1, y, x) for z in range(chips) for x in range(across)] for y in range(down)]
 
-    def exchange(stride):
-        pairs = []
-        for z in range(chips):
-            for y in range(down):
-                for x in range(across):
-                    pairs.append((device(z, 0, y, x), device(z ^ stride, 0, y, x)))
-                    pairs.append((device(z, 1, y, x), device(z, 1, y ^ stride, x)))
-        return pairs
-
+    lines = [
+        [device(z, 0, y, x) for z in range(chips)] for y in range(down) for x in range(across)
+    ] + [[device(z, 1, y, x) for y in range(down)] for z in range(chips) for x in range(across)]
     smem = pl.BlockSpec(memory_space=pltpu.SMEM)
 
     asked = lax.all_to_all(wanted, "table", split_axis=0, concat_axis=0, tiled=True)
@@ -341,44 +332,56 @@
         name="slots",
     )(fetch_count[0], grad_pre, m1, wt, column)
 
+    returned = lax.all_to_all(slot_grads, "table", split_axis=0, concat_axis=0, tiled=True)
     half = (keep + other.astype(F32)).astype(BF).reshape(-1, feature)
-    scattered = lax.all_to_all(
-        half, both, split_axis=0, concat_axis=0, tiled=True, axis_index_groups=planes
-    )
-    slot_grads, scattered = lax.optimization_barrier((slot_grads, scattered))
-    returned = lax.all_to_all(slot_grads, "table", split_axis=0, concat_axis=0, tiled=True)
-    total = jnp.sum(scattered.reshape(shards, -1, feature).astype(F32), axis=0)
-    for stride in (1, 2, 4):
-        total = total + lax.ppermute(total, both, exchange(stride))
-    batch = seeds * groups * shards
-    mean = (total / jnp.sqrt(jnp.float32(batch))).astype(BF)
-
-    share = rows // groups
     dense = pl.pallas_call(
         scatter_kernel,
-        out_shape=shaped((groups, share, feature), BF),
+        out_shape=shaped((rows, feature), F32),
         in_specs=whole(2),
         out_specs=whole(1)[0],
         compiler_params=PARAMS,
         name="scatter",
     )(asked.reshape(1, slots), returned)
-    mine_half = lax.all_to_all(
-        jnp.broadcast_to(mean[None], (shards,) + mean.shape).reshape(-1, feature),
-        both,
-        split_axis=0,
-        concat_axis=0,
-        tiled=True,
-        axis_index_groups=planes,
-    ).reshape(kinds, feature, feature)
-    dense, mine_half = lax.optimization_barrier((dense, mine_half))
-    crossed = lax.all_to_all(dense, "dp", split_axis=0, concat_axis=0, tiled=True)
-    table_part = jnp.sum(crossed.astype(F32), axis=0)
-    other_half = lax.ppermute(mine_half, "dp", swap)
-    weight_grad = jnp.stack(
-        [
-            jnp.where(core == 0, mine_half, other_half),
-            jnp.where(core == 0, other_half, mine_half),
-        ]
+    half, dense = lax.optimization_barrier((half, dense))
+    table_part = lax.psum_scatter(dense, "dp", scatter_dimension=0, tiled=True)
+
+    def reduce_weights(half):
+        scattered = lax.all_to_all(
+            half, both, split_axis=0, concat_axis=0, tiled=True, axis_index_groups=planes
+        )
+        partial = jnp.sum(scattered.reshape(shards, -1, feature).astype(F32), axis=0).astype(BF)
+        crossed = lax.all_to_all(
+            jnp.broadcast_to(partial[None], (chips,) + partial.shape).reshape(-1, feature),
+            both,
+            split_axis=0,
+            concat_axis=0,
+            tiled=True,
+            axis_index_groups=lines,
+        )
+        total = jnp.sum(crossed.reshape(chips, -1, feature).astype(F32), axis=0)
+        batch = seeds * groups * shards
+        mean = (total / jnp.sqrt(jnp.float32(batch))).astype(BF)
+        mine_half = lax.all_to_all(
+            jnp.broadcast_to(mean[None], (shards,) + mean.shape).reshape(-1, feature),
+            both,
+            split_axis=0,
+            concat_axis=0,
+            tiled=True,
+            axis_index_groups=planes,
+        ).reshape(kinds, feature, feature)
+        other_half = lax.ppermute(mine_half, "dp", swap)
+        return jnp.stack(
+            [
+                jnp.where(core == 0, mine_half, other_half),
+                jnp.where(core == 0, other_half, mine_half),
+            ]
+        )
+
+    weight_grad = lax.cond(
+        fetch_count[0, 0, 0] >= 0,
+        reduce_weights,
+        lambda half: jnp.zeros((2, kinds, feature, feature), BF),
+        half,
     )
     return (node_out[None, None], weight_grad, table_part[None])
 

time: 160 us -> 161 us (level)
  blocking collectives: 19.2 us -> 77.7 us
  starting transfers between devices: 59 us -> 21.1 us
  waiting for transfers between devices: 51 us -> 20.5 us
  between operations: 0.9 us -> 14.3 us
  other arithmetic: 5.06 us -> 2.68 us
  local copies, waits for them, and re-layouts: 6.18 us -> 4.17 us
    all_to_all x0 -> x3, blocking collectives: none -> 58.6 us  [the longest x1 28 us: reduce_weights(): lax.all_to_all(half, both, split_axis=0, concat_axis=0, tiled=True, axis_...]
    all_to_all x3 -> x0, waiting for transfers between devices: 35 us -> none  [the longest x1 12.4 us: body(): lax.all_to_all(jnp.broadcast_to(mean[None], (shards,) + mean.shape).resha...]
    all_to_all x3 -> x0, starting transfers between devices: 28.8 us -> none  [the longest x1 12.1 us: body(): lax.all_to_all(half, both, split_axis=0, concat_axis=0, tiled=True, axis_...]
    all_to_all x1, waiting for transfers between devices: 0.01 us -> 13.9 us  [body(): lax.all_to_all(slot_grads, 'table', split_axis=0, concat_axis=0, tiled=True)]
    ppermute x4 -> x1, starting transfers between devices: 15 us -> 6.59 us  [reduce_weights(): other_half = lax.ppermute(mine_half, 'dp', swap)]
    ppermute x4 -> x1, waiting for transfers between devices: 9.36 us -> 1.89 us  [reduce_weights(): other_half = lax.ppermute(mine_half, 'dp', swap)]
    ppermute x1, waiting for transfers between devices: 1.89 us -> 0.01 us  [body(): other = lax.ppermute(send, 'dp', swap)]
    reduce_sum x2, other arithmetic: 1.91 us -> 0.15 us  [the longest x1 0.12 us: reduce_weights(): jnp.sum(scattered.reshape(shards, -1, feature).astype(F32), axis=0)]
  transfers between devices with their start and end apart: 10 -> 5, of which waited for: 8 -> 3; matrix products, arithmetic and copies ran while one was open for 2% -> 2% of each run, Pallas kernels for 7% -> 7%
where the time goes in v3:
time: 161 us; the launch traced here: 160 us
  blocking collectives  77.7 us (48%)
  starting transfers between devices  21.1 us (13%)
  waiting for transfers between devices  20.5 us (13%)
  Pallas kernels  19.6 us (12%)
  between operations  14.3 us (9%)
  local copies, waits for them, and re-layouts  4.17 us (3%)
  other arithmetic  2.68 us (2%)
    all_to_all x1, blocking collectives, reduce_weights(): lax.all_to_all(half, both, split_axis=0, concat_axis=0, tiled=True, axis_...  28 us
    all_to_all x1, blocking collectives, reduce_weights(): lax.all_to_all(jnp.broadcast_to(mean[None], (shards,) + mean.shape).resha...  19.6 us
    all_to_all x1, blocking collectives, body(): lax.all_to_all(wanted, 'table', split_axis=0, concat_axis=0, tiled=True)  19.2 us
    all_to_all x1, waiting for transfers between devices, body(): lax.all_to_all(slot_grads, 'table', split_axis=0, concat_axis=0, tiled=True)  13.9 us
    all_to_all x1, blocking collectives, reduce_weights(): lax.all_to_all(jnp.broadcast_to(partial[None], (chips,) + partial.shape)....  11 us
    pallas_call x1, Pallas kernels, body(): pl.pallas_call(prepare_kernel, out_shape=(shaped((slots, kinds * nodes),...  8.43 us
    ppermute x1, starting transfers between devices, reduce_weights(): other_half = lax.ppermute(mine_half, 'dp', swap)  6.59 us
    ppermute x1, starting transfers between devices, body(): other = lax.ppermute(send, 'dp', swap)  6.51 us
  transfers between devices with their start and end apart: 5, of which 3 were waited for; matrix products, arithmetic and copies ran while one was open for 2% of the time, Pallas kernels for 7%

profile of v3, /device:TPU:1, one launch (start us, length us, event | category | flops | bytes accessed | tf_op | source)
XLA Modules:
  0.0 160.1 jit_solution(2287199870255141427)
XLA Ops:
  7.2 0.0 copy-start.3
  7.2 19.2 %all_to_all.53 = s32[32,1,32]{2,1,0:T(1,128)S(1)} all-to-all(s32[32,1,32]{2,1,0:T(1,128)} %bitcast.54), channel_id=1, replica_groups=mesh['dp'=16,'table'=32] {'table'}, dimensions={0} | all-to-all | bytes 8192 | tf_op jit(solution)/shard_map/all_to_all | solution.py:248
  26.3 0.0 copy-start.4
  26.3 0.9 copy-done.4
  27.3 0.0 copy-start.8
  27.3 0.0 copy-start.9
  27.3 1.3 gather.1
  28.7 4.0 %all-to-all-start.4 = ((bf16[32,32,256]{2,1,0:T(8,128)(2,1)}), bf16[32,32,256]{2,1,0:T(8,128)(2,1)S(1)}, u32[]{:S(2)}, u32[]{:S(2)}) async-start(bf16[32,32,256]{2,1,0:T(8,128)(2,1)} %bitcast.8), calls=%async_computation.4 | async-start | bytes 1048576 | tf_op jit(solution)/shard_map/all_to_all | solution.py:290
  32.7 0.0 copy-done.12
  32.7 0.0 copy-done.11
  32.8 0.0 copy-done.3
  32.8 0.0 copy-done.5
  32.8 0.0 copy-done.6
  32.8 0.0 copy-done.8
  32.8 0.0 copy-done.9
  32.8 0.0 copy-start.2
  32.8 1.4 copy-done.2
  34.2 8.4 %prepare.1 = (bf16[1024,1536]{1,0:T(8,128)(2,1)}, bf16[256,768]{1,0:T(8,128)(2,1)S(1)}, bf16[2,6,256,256]{3,2,1,0:T(8,128)(2,1)S(1)}, f32[256,256]{1,0:T(8,128)S(1)}, f32[256,8]{1,0:T(8,128)S(1)}) custom-call(s32[1,256]{1,0:T(1,128)S(1)} %bitcast.48, s32[5,4,256]{2,1,0:T(4,128)S(1)} %bitcast.43, s32[5,256]{1,0:T(8,128)S(1)} %bitcast.39, ...), custom_call_target="tpu_custom_call" | custom-call | tf_op jit(solution)/shard_map/prepare/pallas_call | solution.py:253
  42.6 4.7 %all-to-all-done.4 = bf16[32,32,256]{2,1,0:T(8,128)(2,1)S(1)} async-done(((bf16[32,32,256]{2,1,0:T(8,128)(2,1)}), bf16[32,32,256]{2,1,0:T(8,128)(2,1)S(1)}, u32[]{:S(2)}, u32[]{:S(2)}) %all-to-all-start.4) | async-done | bytes 524320 | tf_op jit(solution)/shard_map/all_to_all | solution.py:290
  47.3 0.0 copy-done.7
  47.3 6.0 %step.1 = (bf16[128,256]{1,0:T(8,128)(2,1)}, bf16[256,256]{1,0:T(8,128)(2,1)S(1)}, f32[6,256,256]{2,1,0:T(8,128)S(1)}, bf16[6,256,256]{2,1,0:T(8,128)(2,1)}) custom-call(s32[1,32]{1,0:T(1,128)S(1)} %bitcast.45, s32[1]{0:T(128)} %bitcast.5.core_ref, bf16[1024,256]{1,0:T(8,128)(2,1)S(1)} %bitcast.35, bf16[1024,1536]{1,0:T(8,128)(2,1)} %get-tuple-element.23.m1_ref, ...), custom_call_target="tpu_custom_call" | custom-call | tf_op jit(solution)/shard_map/step/pallas_call | solution.py:292
  53.4 6.5 %collective-permute-start.1 = (bf16[6,256,256]{2,1,0:T(8,128)(2,1)}, bf16[6,256,256]{2,1,0:T(8,128)(2,1)S(1)}, u32[]{:S(2)}, u32[]{:S(2)}) collective-permute-start(bf16[6,256,256]{2,1,0:T(8,128)(2,1)} %get-tuple-element.29), channel_id=1, source_target_pairs={{0,32},{32,0},{64,96},{96,64},{128,160},{160,128},{192,224},{224,1... | collective-permute-start | bytes 2359304 | tf_op jit(solution)/shard_map/ppermute | solution.py:321
  59.9 0.0 copy-done
  59.9 2.6 %slots.1 = bf16[1024,256]{1,0:T(8,128)(2,1)} custom-call(s32[1,32]{1,0:T(1,128)S(1)} %bitcast.46, bf16[256,256]{1,0:T(8,128)(2,1)S(1)} %get-tuple-element.30.grad_ref, bf16[1024,1536]{1,0:T(8,128)(2,1)S(1)} %copy-done, bf16[2,6,256,256]{3,2,1,0:T(8,128)(2,1)S(1)} %get-tuple-element.25.wt_ref, f32[256,8]{1,0:T(8,128)S(1)} %get-tuple-element.31.column_ref), custom_call_target="tpu_custom_call" | custom-call | tf_op jit(solution)/shard_map/slots/pallas_call | solution.py:322
  62.5 0.0 copy-done.1
  62.5 3.9 %all-to-all-start.5 = ((bf16[32,32,256]{2,1,0:T(8,128)(2,1)}), bf16[32,32,256]{2,1,0:T(8,128)(2,1)S(1)}, u32[]{:S(2)}, u32[]{:S(2)}) async-start(bf16[32,32,256]{2,1,0:T(8,128)(2,1)} %bitcast.20), calls=%async_computation.5 | async-start | bytes 1048576 | tf_op jit(solution)/shard_map/all_to_all | solution.py:335
  66.5 0.0 reduce-scatter.2.cloned.1.call-start
  66.5 0.5 broadcast.17
  67.0 0.7 reduce.5
  67.7 0.1 reshape.52.asked_ref
  67.8 0.0 collective-permute-done.1
  67.8 1.6 add_convert_fusion
  69.4 13.9 %all-to-all-done.5 = bf16[32,32,256]{2,1,0:T(8,128)(2,1)S(1)} async-done(((bf16[32,32,256]{2,1,0:T(8,128)(2,1)}), bf16[32,32,256]{2,1,0:T(8,128)(2,1)S(1)}, u32[]{:S(2)}, u32[]{:S(2)}) %all-to-all-start.5) | async-done | bytes 524320 | tf_op jit(solution)/shard_map/all_to_all | solution.py:335
  83.3 1.2 scatter.1
  84.5 0.0 reduce-scatter.2.cloned.1.call-update
  84.5 67.6 %conditional.1 = (bf16[2,6,256,256]{3,2,1,0:T(8,128)(2,1)S(1)}) conditional(s32[]{:T(128)} %bitcast.18, () %tuple.15, (s32[]{:T(128)}, bf16[1536,256]{1,0:T(8,128)(2,1)S(1)}) %tuple.24), branch_computations={%region_0.1_spmd, %region_1.0_spmd} | conditional | flops 2162689 | bytes 15138876 | solution.py:380
  84.6 28.0 %all_to_all.50 = bf16[32,48,256]{2,1,0:T(8,128)(2,1)S(1)} all-to-all(bf16[32,48,256]{2,1,0:T(8,128)(2,1)S(1)} %bitcast.51), channel_id=1, replica_groups={{0,1,2,3,4,5,6,7,8,9,10,11,12,13,14,15,16,17,18,19,20,21,22,23,24,25,26..., dimensions={0} | all-to-all | bytes 1572864 | tf_op jit(solution)/shard_map/cond/branch_1_fun/all_to_all | solution.py:349
  112.5 0.1 reduce_sum.19
  112.7 11.0 %all_to_all.51 = bf16[8,48,256]{2,1,0:T(8,128)(2,1)S(1)} all-to-all(bf16[8,48,256]{2,1,0:T(8,128)(2,1)S(1)} %broadcast_in_dim.0), channel_id=1, replica_groups={{0,64,128,192,256,320,384,448},{1,65,129,193,257,321,385,449},{2,66,130..., dimensions={0} | all-to-all | bytes 393216 | tf_op jit(solution)/shard_map/cond/branch_1_fun/all_to_all | solution.py:353
  123.7 0.1 broadcast_in_dim.1
  123.8 19.6 %all_to_all.52 = bf16[32,48,256]{2,1,0:T(8,128)(2,1)S(1)} all-to-all(bf16[32,48,256]{2,1,0:T(8,128)(2,1)S(1)} %broadcast_in_dim.1), channel_id=1, replica_groups={{0,1,2,3,4,5,6,7,8,9,10,11,12,13,14,15,16,17,18,19,20,21,22,23,24,25,26..., dimensions={0} | all-to-all | bytes 1572864 | tf_op jit(solution)/shard_map/cond/branch_1_fun/all_to_all | solution.py:364
  143.4 6.6 %collective-permute-start = (bf16[6,256,256]{2,1,0:T(8,128)(2,1)S(1)}, bf16[6,256,256]{2,1,0:T(8,128)(2,1)S(1)}, u32[]{:S(2)}, u32[]{:S(2)}) collective-permute-start(bf16[6,256,256]{2,1,0:T(8,128)(2,1)S(1)} %bitcast.52), channel_id=1, source_target_pairs={{0,32},{32,0},{64,96},{96,64},{128,160},{160,128},{192,224},{224,1... | collective-permute-start | bytes 2359304 | tf_op jit(solution)/shard_map/cond/branch_1_fun/ppermute | solution.py:372
  150.0 1.9 %collective-permute-done = bf16[6,256,256]{2,1,0:T(8,128)(2,1)S(1)} collective-permute-done((bf16[6,256,256]{2,1,0:T(8,128)(2,1)S(1)}, bf16[6,256,256]{2,1,0:T(8,128)(2,1)S(1)}, u32[]{:S(2)}, u32[]{:S(2)}) %collective-permute-start) | collective-permute-done | bytes 786464 | tf_op jit(solution)/shard_map/cond/branch_1_fun/ppermute | solution.py:372
  151.9 0.1 select_bitcast_fusion.1
  152.0 0.1 pad_maximum_fusion
  152.1 0.0 copy-start.10
  152.2 0.0 reduce-scatter.2.cloned.1.call-done
  152.2 1.1 copy-done.10
  (12 shorter events, 0.1 us)
Async XLA Ops:
  7.2 25.6 %copy-start.3 = (bf16[1,1,128,256]{3,2,1,0:T(8,128)(2,1)S(1)}, bf16[1,1,128,256]{3,2,1,0:T(8,128)(2,1)}, u32[]{:S(2)}) copy-start(bf16[1,1,128,256]{3,2,1,0:T(8,128)(2,1)} %param.23) | copy-start | bytes 196612
  26.3 1.0 copy-start.4
  27.3 5.4 %copy-start.12 = (s32[1,1,5,128]{3,1,2,0:T(1,128)S(1)}, s32[1,1,5,128]{3,1,2,0:T(1,128)}, u32[]{:S(2)}) copy-start(s32[1,1,5,128]{3,1,2,0:T(1,128)} %param.22) | copy-start | bytes 7684
  27.3 5.4 %copy-start.11 = (s32[1,1,5,256]{3,1,2,0:T(1,128)S(1)}, s32[1,1,5,256]{3,1,2,0:T(1,128)}, u32[]{:S(2)}) copy-start(s32[1,1,5,256]{3,1,2,0:T(1,128)} %param.19) | copy-start | bytes 15364
  27.3 5.5 %copy-start.5 = (s32[1,1,5,256,4]{3,4,2,1,0:T(4,128)S(1)}, s32[1,1,5,256,4]{3,4,2,1,0:T(4,128)}, u32[]{:S(2)}) copy-start(s32[1,1,5,256,4]{3,4,2,1,0:T(4,128)} %param.18) | copy-start | bytes 61444
  27.3 5.5 %copy-start.6 = (s32[1,1,5,128,4]{3,4,2,1,0:T(4,128)S(1)}, s32[1,1,5,128,4]{3,4,2,1,0:T(4,128)}, u32[]{:S(2)}) copy-start(s32[1,1,5,128,4]{3,4,2,1,0:T(4,128)} %param.21) | copy-start | bytes 30724
  27.3 5.5 %copy-start.8 = (s32[1,1,256]{2,1,0:T(1,128)S(1)}, s32[1,1,256]{2,1,0:T(1,128)}, u32[]{:S(2)}) copy-start(s32[1,1,256]{2,1,0:T(1,128)} %param.17) | copy-start | bytes 3076
  27.3 5.5 %copy-start.9 = (s32[1,1,128]{2,1,0:T(1,128)S(1)}, s32[1,1,128]{2,1,0:T(1,128)}, u32[]{:S(2)}) copy-start(s32[1,1,128]{2,1,0:T(1,128)} %param.20) | copy-start | bytes 1540
  28.7 18.7 %copy-start.7 = (s32[1,1,32]{2,1,0:T(1,128)S(1)}, s32[1,1,32]{2,1,0:T(1,128)}, u32[]{:S(2)}) copy-start(s32[1,1,32]{2,1,0:T(1,128)} %param.16) | copy-start | bytes 388
  28.7 18.7 %all-to-all-start.4 = ((bf16[32,32,256]{2,1,0:T(8,128)(2,1)}), bf16[32,32,256]{2,1,0:T(8,128)(2,1)S(1)}, u32[]{:S(2)}, u32[]{:S(2)}) async-start(bf16[32,32,256]{2,1,0:T(8,128)(2,1)} %bitcast.8), calls=%async_computation.4 | async-start | bytes 1048576 | tf_op jit(solution)/shard_map/all_to_all | solution.py:290
  32.8 1.4 copy-start.2
  47.3 12.6 %copy-start = (bf16[1024,1536]{1,0:T(8,128)(2,1)S(1)}, bf16[1024,1536]{1,0:T(8,128)(2,1)}, u32[]{:S(2)}) copy-start(bf16[1024,1536]{1,0:T(8,128)(2,1)} %get-tuple-element.23.m1_ref) | copy-start | bytes 9437188
  53.4 9.1 %copy-start.1 = (f32[6,256,256]{2,1,0:T(8,128)}, f32[6,256,256]{2,1,0:T(8,128)S(1)}, u32[]{:S(2)}) copy-start(f32[6,256,256]{2,1,0:T(8,128)S(1)} %get-tuple-element.28) | copy-start | bytes 4718596
  53.4 14.4 %collective-permute-start.1 = (bf16[6,256,256]{2,1,0:T(8,128)(2,1)}, bf16[6,256,256]{2,1,0:T(8,128)(2,1)S(1)}, u32[]{:S(2)}, u32[]{:S(2)}) collective-permute-start(bf16[6,256,256]{2,1,0:T(8,128)(2,1)} %get-tuple-element.29), channel_id=1, source_target_pairs={{0,32},{32,0},{64,96},{96,64},{128,160},{160,128},{192,224},{224,1... | collective-permute-start | bytes 2359304 | tf_op jit(solution)/shard_map/ppermute | solution.py:321
  62.5 20.8 %all-to-all-start.5 = ((bf16[32,32,256]{2,1,0:T(8,128)(2,1)}), bf16[32,32,256]{2,1,0:T(8,128)(2,1)S(1)}, u32[]{:S(2)}, u32[]{:S(2)}) async-start(bf16[32,32,256]{2,1,0:T(8,128)(2,1)} %bitcast.20), calls=%async_computation.5 | async-start | bytes 1048576 | tf_op jit(solution)/shard_map/all_to_all | solution.py:335
  66.5 85.7 %reduce-scatter.2.cloned.1.call-start = ((), (), s32[]{:S(2)}) async-start(), calls=%async_computation.7 | async-start | bytes 557056 | tf_op jit(solution)/shard_map/reduce_scatter | solution.py:346
  143.4 8.5 %collective-permute-start = (bf16[6,256,256]{2,1,0:T(8,128)(2,1)S(1)}, bf16[6,256,256]{2,1,0:T(8,128)(2,1)S(1)}, u32[]{:S(2)}, u32[]{:S(2)}) collective-permute-start(bf16[6,256,256]{2,1,0:T(8,128)(2,1)S(1)} %bitcast.52), channel_id=1, source_target_pairs={{0,32},{32,0},{64,96},{96,64},{128,160},{160,128},{192,224},{224,1... | collective-permute-start | bytes 2359304 | tf_op jit(solution)/shard_map/cond/branch_1_fun/ppermute | solution.py:372
  152.1 1.1 copy-start.10
Sparse Core Ops, SparseCore 0:
  84.6 62.0 reduce-scatter.1

commit v4 on v2

--- a/solution.py
+++ b/solution.py
@@ -191,13 +191,20 @@
         ).astype(BF)
 
 
-def scatter_kernel(asked_ref, grads_ref, out_ref):
-    groups, share, feature = out_ref.shape
-    rows = groups * share
-    index = lax.broadcasted_iota(jnp.int32, (rows, asked_ref.shape[1]), 0)
-    hot = jnp.where(index == asked_ref[...], 1.0, 0.0).astype(BF)
-    dense = dot(hot, grads_ref[...])
-    out_ref[...] = dense.reshape(groups, share, feature).astype(BF)
+def scatter_kernel(me_ref, asked_ref, grads_ref, keep_ref, give_ref, hot_ref):
+    blocks = 16
+    rows, slots = hot_ref.shape
+    share = rows // blocks
+    half = rows // 2
+    asked = asked_ref[...]
+    within = lax.broadcasted_iota(jnp.int32, (share, slots), 0)
+    for b in range(blocks):
+        flip = sum(((b >> n) & 1) << (3 - n) for n in range(4))
+        index = within + (me_ref[0] ^ flip) * share
+        hot_ref[pl.ds(b * share, share), :] = jnp.where(index == asked, 1.0, 0.0).astype(BF)
+    grads = grads_ref[...]
+    give_ref[...] = dot(hot_ref[half:, :], grads)
+    keep_ref[...] = dot(hot_ref[:half, :], grads)
 
 
 def whole(n):
@@ -243,15 +250,9 @@
         [device(z, 0, y, x) for y in range(down) for x in range(across)] for z in range(chips)
     ] + [[device(z, 1, y, x) for z in range(chips) for x in range(across)] for y in range(down)]
 
-    def exchange(stride):
-        pairs = []
-        for z in range(chips):
-            for y in range(down):
-                for x in range(across):
-                    pairs.append((device(z, 0, y, x), device(z ^ stride, 0, y, x)))
-                    pairs.append((device(z, 1, y, x), device(z, 1, y ^ stride, x)))
-        return pairs
-
+    lines = [
+        [device(z, 0, y, x) for z in range(chips)] for y in range(down) for x in range(across)
+    ] + [[device(z, 1, y, x) for y in range(down)] for z in range(chips) for x in range(across)]
     smem = pl.BlockSpec(memory_space=pltpu.SMEM)
 
     asked = lax.all_to_all(wanted, "table", split_axis=0, concat_axis=0, tiled=True)
@@ -341,27 +342,43 @@
         name="slots",
     )(fetch_count[0], grad_pre, m1, wt, column)
 
+    returned = lax.all_to_all(slot_grads, "table", split_axis=0, concat_axis=0, tiled=True)
     half = (keep + other.astype(F32)).astype(BF).reshape(-1, feature)
+    half, returned = lax.optimization_barrier((half, returned))
+    share = rows // groups
+    keep_rows, give_rows = pl.pallas_call(
+        scatter_kernel,
+        out_shape=(shaped((rows // 2, feature), F32),) * 2,
+        in_specs=[smem] + whole(2),
+        out_specs=tuple(whole(2)),
+        scratch_shapes=[pltpu.VMEM((rows, slots), BF)],
+        compiler_params=PARAMS,
+        name="scatter",
+    )(lax.axis_index("dp").reshape(1), asked.reshape(1, slots), returned)
+
+    def halve(keep_rows, give_rows, bit):
+        got = lax.ppermute(give_rows, "dp", [(i, i ^ bit) for i in range(groups)])
+        return keep_rows + got
+
     scattered = lax.all_to_all(
         half, both, split_axis=0, concat_axis=0, tiled=True, axis_index_groups=planes
     )
-    slot_grads, scattered = lax.optimization_barrier((slot_grads, scattered))
-    returned = lax.all_to_all(slot_grads, "table", split_axis=0, concat_axis=0, tiled=True)
-    total = jnp.sum(scattered.reshape(shards, -1, feature).astype(F32), axis=0)
-    for stride in (1, 2, 4):
-        total = total + lax.ppermute(total, both, exchange(stride))
+    rest = halve(keep_rows, give_rows, 1)
+    rest = halve(rest[: rows // 4], rest[rows // 4 :], 2)
+    partial = jnp.sum(scattered.reshape(shards, -1, feature).astype(F32), axis=0).astype(BF)
+    crossed = lax.all_to_all(
+        jnp.broadcast_to(partial[None], (chips,) + partial.shape).reshape(-1, feature),
+        both,
+        split_axis=0,
+        concat_axis=0,
+        tiled=True,
+        axis_index_groups=lines,
+    )
+    total = jnp.sum(crossed.reshape(chips, -1, feature).astype(F32), axis=0)
     batch = seeds * groups * shards
     mean = (total / jnp.sqrt(jnp.float32(batch))).astype(BF)
-
-    share = rows // groups
-    dense = pl.pallas_call(
-        scatter_kernel,
-        out_shape=shaped((groups, share, feature), BF),
-        in_specs=whole(2),
-        out_specs=whole(1)[0],
-        compiler_params=PARAMS,
-        name="scatter",
-    )(asked.reshape(1, slots), returned)
+    rest = halve(rest[: rows // 8], rest[rows // 8 :], 4)
+    mean, rest = lax.optimization_barrier((mean, rest))
     mine_half = lax.all_to_all(
         jnp.broadcast_to(mean[None], (shards,) + mean.shape).reshape(-1, feature),
         both,
@@ -370,9 +387,8 @@
         tiled=True,
         axis_index_groups=planes,
     ).reshape(kinds, feature, feature)
-    dense, mine_half = lax.optimization_barrier((dense, mine_half))
-    crossed = lax.all_to_all(dense, "dp", split_axis=0, concat_axis=0, tiled=True)
-    table_part = jnp.sum(crossed.astype(F32), axis=0)
+    table_part = halve(rest[:share], rest[share:], 8)
+    mine_half, table_part = lax.optimization_barrier((mine_half, table_part))
     other_half = lax.ppermute(mine_half, "dp", swap)
     weight_grad = jnp.stack(
         [

time: 160 us -> 149 us (0.931)
  waiting for transfers between devices: 51 us -> 42.9 us
  starting transfers between devices: 59 us -> 56 us
    all_to_all x1, waiting for transfers between devices: 0.01 us -> 14.3 us  [body(): lax.all_to_all(slot_grads, 'table', split_axis=0, concat_axis=0, tiled=True)]
    all_to_all x1, waiting for transfers between devices: 12.4 us -> 0.01 us  [body(): lax.all_to_all(jnp.broadcast_to(mean[None], (shards,) + mean.shape).resha...]
    all_to_all x1, waiting for transfers between devices: 11.7 us -> 0.5 us  [body(): lax.all_to_all(jnp.broadcast_to(partial[None], (chips,) + partial.shape)....]
    ppermute x3 -> x4, waiting for transfers between devices: 9.36 us -> 14.9 us  [halve(): got = lax.ppermute(give_rows, 'dp', [(i, i ^ bit) for i in range(groups)])]
    all_to_all x1, starting transfers between devices: 10.1 us -> 4.88 us  [body(): lax.all_to_all(jnp.broadcast_to(mean[None], (shards,) + mean.shape).resha...]
    all_to_all x1, waiting for transfers between devices: 10.9 us -> 6.63 us  [body(): lax.all_to_all(half, both, split_axis=0, concat_axis=0, tiled=True, axis_...]
    all_to_all x1, starting transfers between devices: 6.59 us -> 3.39 us  [body(): lax.all_to_all(jnp.broadcast_to(partial[None], (chips,) + partial.shape)....]
    ppermute x1, starting transfers between devices: 1.91 us -> 4.69 us  [body(): other_half = lax.ppermute(mine_half, 'dp', swap)]
  transfers between devices with their start and end apart: 10 -> 11, of which waited for: 8 -> 8; matrix products, arithmetic and copies ran while one was open for 2% -> 4% of each run, Pallas kernels for 7% -> 8%
where the time goes in v4:
time: 149 us; the launch traced here: 148 us
  starting transfers between devices  56 us (38%)
  waiting for transfers between devices  42.9 us (29%)
  blocking collectives  19.2 us (13%)
  Pallas kernels  18.8 us (13%)
  other arithmetic  5.39 us (4%)
  local copies, waits for them, and re-layouts  4.64 us (3%)
    all_to_all x1, blocking collectives, body(): lax.all_to_all(wanted, 'table', split_axis=0, concat_axis=0, tiled=True)  19.2 us
    ppermute x4, starting transfers between devices, halve(): got = lax.ppermute(give_rows, 'dp', [(i, i ^ bit) for i in range(groups)])  15.8 us
    ppermute x4, waiting for transfers between devices, halve(): got = lax.ppermute(give_rows, 'dp', [(i, i ^ bit) for i in range(groups)])  14.9 us
    all_to_all x1, waiting for transfers between devices, body(): lax.all_to_all(slot_grads, 'table', split_axis=0, concat_axis=0, tiled=True)  14.3 us
    all_to_all x1, starting transfers between devices, body(): lax.all_to_all(half, both, split_axis=0, concat_axis=0, tiled=True, axis_...  12.7 us
    pallas_call x1, Pallas kernels, body(): pl.pallas_call(prepare_kernel, out_shape=(shaped((slots, kinds * nodes),...  8.43 us
    all_to_all x1, waiting for transfers between devices, body(): lax.all_to_all(half, both, split_axis=0, concat_axis=0, tiled=True, axis_...  6.63 us
    ppermute x1, starting transfers between devices, body(): other = lax.ppermute(send, 'dp', swap)  6.6 us
  transfers between devices with their start and end apart: 11, of which 8 were waited for; matrix products, arithmetic and copies ran while one was open for 4% of the time, Pallas kernels for 8%

profile of v4, /device:TPU:1, one launch (start us, length us, event | category | flops | bytes accessed | tf_op | source)
XLA Modules:
  0.0 147.9 jit_solution(18348835462307389272)
XLA Ops:
  0.6 19.2 %all_to_all.55 = s32[32,1,32]{2,1,0:T(1,128)S(1)} all-to-all(s32[32,1,32]{2,1,0:T(1,128)} %bitcast.51), channel_id=1, replica_groups=mesh['dp'=16,'table'=32] {'table'}, dimensions={0} | all-to-all | bytes 8192 | tf_op jit(solution)/shard_map/all_to_all | solution.py:258
  19.8 0.9 copy-done.4
  20.8 0.0 copy-start.8
  20.8 0.0 copy-start.9
  20.8 1.3 gather.1
  22.1 4.0 %all-to-all-start.1 = ((bf16[32,32,256]{2,1,0:T(8,128)(2,1)}), bf16[32,32,256]{2,1,0:T(8,128)(2,1)S(1)}, u32[]{:S(2)}, u32[]{:S(2)}) async-start(bf16[32,32,256]{2,1,0:T(8,128)(2,1)} %bitcast.4), calls=%async_computation.1 | async-start | bytes 1048576 | tf_op jit(solution)/shard_map/all_to_all | solution.py:300
  26.2 0.0 copy-done.11
  26.2 0.0 copy-done.3
  26.2 0.0 copy-done.5
  26.2 0.0 copy-done.6
  26.2 0.0 copy-done.8
  26.3 0.0 copy-start.2
  26.3 1.4 copy-done.2
  27.7 8.4 %prepare.1 = (bf16[1024,1536]{1,0:T(8,128)(2,1)}, bf16[256,768]{1,0:T(8,128)(2,1)S(1)}, bf16[2,6,256,256]{3,2,1,0:T(8,128)(2,1)S(1)}, f32[256,256]{1,0:T(8,128)S(1)}, f32[256,8]{1,0:T(8,128)S(1)}) custom-call(s32[1,256]{1,0:T(1,128)S(1)} %bitcast.46, s32[5,4,256]{2,1,0:T(4,128)S(1)} %bitcast.42, s32[5,256]{1,0:T(8,128)S(1)} %bitcast.38, ...), custom_call_target="tpu_custom_call" | custom-call | tf_op jit(solution)/shard_map/prepare/pallas_call | solution.py:263
  36.1 4.7 %all-to-all-done.1 = bf16[32,32,256]{2,1,0:T(8,128)(2,1)S(1)} async-done(((bf16[32,32,256]{2,1,0:T(8,128)(2,1)}), bf16[32,32,256]{2,1,0:T(8,128)(2,1)S(1)}, u32[]{:S(2)}, u32[]{:S(2)}) %all-to-all-start.1) | async-done | bytes 524320 | tf_op jit(solution)/shard_map/all_to_all | solution.py:300
  40.8 6.0 %step.1 = (bf16[128,256]{1,0:T(8,128)(2,1)}, bf16[256,256]{1,0:T(8,128)(2,1)S(1)}, f32[6,256,256]{2,1,0:T(8,128)S(1)}, bf16[6,256,256]{2,1,0:T(8,128)(2,1)}) custom-call(s32[1,32]{1,0:T(1,128)S(1)} %bitcast.44, s32[1]{0:T(128)} %bitcast.1.core_ref, bf16[1024,256]{1,0:T(8,128)(2,1)S(1)} %bitcast.34, bf16[1024,1536]{1,0:T(8,128)(2,1)} %get-tuple-element.20.m1_ref, ...), custom_call_target="tpu_custom_call" | custom-call | tf_op jit(solution)/shard_map/step/pallas_call | solution.py:302
  46.8 6.6 %collective-permute-start = (bf16[6,256,256]{2,1,0:T(8,128)(2,1)}, bf16[6,256,256]{2,1,0:T(8,128)(2,1)S(1)}, u32[]{:S(2)}, u32[]{:S(2)}) collective-permute-start(bf16[6,256,256]{2,1,0:T(8,128)(2,1)} %get-tuple-element.26), channel_id=1, source_target_pairs={{0,32},{32,0},{64,96},{96,64},{128,160},{160,128},{192,224},{224,1... | collective-permute-start | bytes 2359304 | tf_op jit(solution)/shard_map/ppermute | solution.py:331
  53.5 2.6 %slots.1 = bf16[1024,256]{1,0:T(8,128)(2,1)} custom-call(s32[1,32]{1,0:T(1,128)S(1)} %bitcast.45, bf16[256,256]{1,0:T(8,128)(2,1)S(1)} %get-tuple-element.27.grad_ref, bf16[1024,1536]{1,0:T(8,128)(2,1)S(1)} %copy-done, bf16[2,6,256,256]{3,2,1,0:T(8,128)(2,1)S(1)} %get-tuple-element.22.wt_ref, f32[256,8]{1,0:T(8,128)S(1)} %get-tuple-element.28.column_ref), custom_call_target="tpu_custom_call" | custom-call | tf_op jit(solution)/shard_map/slots/pallas_call | solution.py:332
  56.1 3.9 %all-to-all-start.2 = ((bf16[32,32,256]{2,1,0:T(8,128)(2,1)}), bf16[32,32,256]{2,1,0:T(8,128)(2,1)S(1)}, u32[]{:S(2)}, u32[]{:S(2)}) async-start(bf16[32,32,256]{2,1,0:T(8,128)(2,1)} %bitcast.15), calls=%async_computation.2 | async-start | bytes 1048576 | tf_op jit(solution)/shard_map/all_to_all | solution.py:345
  60.0 0.0 collective-permute-done
  60.0 2.5 %add_convert_fusion = bf16[6,256,256]{2,1,0:T(8,128)(2,1)} fusion(f32[6,256,256]{2,1,0:T(8,128)} %copy-done.1, bf16[6,256,256]{2,1,0:T(8,128)(2,1)S(1)} %collective-permute-done), kind=kLoop, calls=%fused_computation.1 | loop fusion | flops 1179648 | bytes 3145728 | tf_op jit(solution)/shard_map/convert_element_type | solution.py:346
  62.4 14.3 %all-to-all-done.2 = bf16[32,32,256]{2,1,0:T(8,128)(2,1)S(1)} async-done(((bf16[32,32,256]{2,1,0:T(8,128)(2,1)}), bf16[32,32,256]{2,1,0:T(8,128)(2,1)S(1)}, u32[]{:S(2)}, u32[]{:S(2)}) %all-to-all-start.2) | async-done | bytes 524320 | tf_op jit(solution)/shard_map/all_to_all | solution.py:345
  76.7 12.7 %all-to-all-start.3 = ((bf16[32,48,256]{2,1,0:T(8,128)(2,1)}), bf16[32,48,256]{2,1,0:T(8,128)(2,1)S(1)}, u32[]{:S(2)}, u32[]{:S(2)}) async-start(bf16[32,48,256]{2,1,0:T(8,128)(2,1)} %bitcast.17), calls=%async_computation.3 | async-start | bytes 1572864 | tf_op jit(solution)/shard_map/all_to_all | solution.py:363
  89.5 0.5 broadcast.7
  90.0 0.7 reduce.5
  90.7 0.1 reshape.49.asked_ref
  90.8 0.4 scatter.1
  91.2 1.9 %collective-permute-start.1 = (f32[256,256]{1,0:T(8,128)S(1)}, f32[256,256]{1,0:T(8,128)S(1)}, u32[]{:S(2)}, u32[]{:S(2)}) collective-permute-start(f32[256,256]{1,0:T(8,128)S(1)} %get-tuple-element.32), channel_id=1, source_target_pairs={{0,32},{32,0},{64,96},{96,64},{128,160},{160,128},{192,224},{224,1... | collective-permute-start | bytes 786440 | tf_op jit(solution)/shard_map/ppermute | solution.py:360
  93.1 1.5 %collective-permute-done.1 = f32[256,256]{1,0:T(8,128)S(1)} collective-permute-done((f32[256,256]{1,0:T(8,128)S(1)}, f32[256,256]{1,0:T(8,128)S(1)}, u32[]{:S(2)}, u32[]{:S(2)}) %collective-permute-start.1) | collective-permute-done | bytes 262176 | tf_op jit(solution)/shard_map/ppermute | solution.py:360
  94.7 3.1 %collective-permute-start.2 = (f32[128,256]{1,0:T(8,128)S(1)}, f32[128,256]{1,0:T(8,128)S(1)}, u32[]{:S(2)}, u32[]{:S(2)}) collective-permute-start(f32[128,256]{1,0:T(8,128)S(1)} %slice.25), channel_id=1, source_target_pairs={{0,64},{32,96},{64,0},{96,32},{128,192},{160,224},{192,128},{224,1... | collective-permute-start | bytes 393224 | tf_op jit(solution)/shard_map/ppermute | solution.py:360
  97.8 6.6 %all-to-all-done.3 = bf16[32,48,256]{2,1,0:T(8,128)(2,1)S(1)} async-done(((bf16[32,48,256]{2,1,0:T(8,128)(2,1)}), bf16[32,48,256]{2,1,0:T(8,128)(2,1)S(1)}, u32[]{:S(2)}, u32[]{:S(2)}) %all-to-all-start.3) | async-done | bytes 786464 | tf_op jit(solution)/shard_map/all_to_all | solution.py:363
  104.5 0.1 reduce_sum.21
  104.6 0.7 broadcast_in_dim.9
  105.3 3.4 %all-to-all-start.4 = ((bf16[8,48,256]{2,1,0:T(8,128)(2,1)}), bf16[8,48,256]{2,1,0:T(8,128)(2,1)S(1)}, u32[]{:S(2)}, u32[]{:S(2)}) async-start(bf16[8,48,256]{2,1,0:T(8,128)(2,1)} %broadcast_in_dim.9), calls=%async_computation.4 | async-start | bytes 393216 | tf_op jit(solution)/shard_map/all_to_all | solution.py:369
  108.7 0.0 collective-permute-done.2
  108.7 3.7 %collective-permute-start.3 = (f32[64,256]{1,0:T(8,128)S(1)}, f32[64,256]{1,0:T(8,128)S(1)}, u32[]{:S(2)}, u32[]{:S(2)}) collective-permute-start(f32[64,256]{1,0:T(8,128)S(1)} %slice.27), channel_id=1, source_target_pairs={{0,128},{32,160},{64,192},{96,224},{128,0},{160,32},{192,64},{224,... | collective-permute-start | bytes 196616 | tf_op jit(solution)/shard_map/ppermute | solution.py:360
  112.4 4.3 %collective-permute-done.3 = f32[64,256]{1,0:T(8,128)S(1)} collective-permute-done((f32[64,256]{1,0:T(8,128)S(1)}, f32[64,256]{1,0:T(8,128)S(1)}, u32[]{:S(2)}, u32[]{:S(2)}) %collective-permute-start.3) | collective-permute-done | bytes 65568 | tf_op jit(solution)/shard_map/ppermute | solution.py:360
  116.7 0.5 all-to-all-done.4
  117.3 0.9 broadcast_in_dim.20
  118.2 4.9 %all-to-all-start.5 = ((bf16[32,48,256]{2,1,0:T(8,128)(2,1)}), bf16[32,48,256]{2,1,0:T(8,128)(2,1)S(1)}, u32[]{:S(2)}, u32[]{:S(2)}) async-start(bf16[32,48,256]{2,1,0:T(8,128)(2,1)} %broadcast_in_dim.20), calls=%async_computation.5 | async-start | bytes 1572864 | tf_op jit(solution)/shard_map/all_to_all | solution.py:382
  123.1 7.1 %collective-permute-start.4 = (f32[32,256]{1,0:T(8,128)S(1)}, f32[32,256]{1,0:T(8,128)S(1)}, u32[]{:S(2)}, u32[]{:S(2)}) collective-permute-start(f32[32,256]{1,0:T(8,128)S(1)} %slice.23), channel_id=1, source_target_pairs={{0,256},{32,288},{64,320},{96,352},{128,384},{160,416},{192,448},{... | collective-permute-start | bytes 98312 | tf_op jit(solution)/shard_map/ppermute | solution.py:360
  130.2 9.1 %collective-permute-done.4 = f32[32,256]{1,0:T(8,128)S(1)} collective-permute-done((f32[32,256]{1,0:T(8,128)S(1)}, f32[32,256]{1,0:T(8,128)S(1)}, u32[]{:S(2)}, u32[]{:S(2)}) %collective-permute-start.4) | collective-permute-done | bytes 32800 | tf_op jit(solution)/shard_map/ppermute | solution.py:360
  139.3 0.6 slice_add_fusion.2
  139.9 0.0 all-to-all-done.5
  139.9 4.7 %collective-permute-start.5 = (bf16[6,256,256]{2,1,0:T(8,128)(2,1)S(1)}, bf16[6,256,256]{2,1,0:T(8,128)(2,1)S(1)}, u32[]{:S(2)}, u32[]{:S(2)}) collective-permute-start(bf16[6,256,256]{2,1,0:T(8,128)(2,1)S(1)} %bitcast.48), channel_id=1, source_target_pairs={{0,32},{32,0},{64,96},{96,64},{128,160},{160,128},{192,224},{224,1... | collective-permute-start | bytes 2359304 | tf_op jit(solution)/shard_map/ppermute | solution.py:392
  144.6 1.9 %collective-permute-done.5 = bf16[6,256,256]{2,1,0:T(8,128)(2,1)S(1)} collective-permute-done((bf16[6,256,256]{2,1,0:T(8,128)(2,1)S(1)}, bf16[6,256,256]{2,1,0:T(8,128)(2,1)S(1)}, u32[]{:S(2)}, u32[]{:S(2)}) %collective-permute-start.5) | collective-permute-done | bytes 786464 | tf_op jit(solution)/shard_map/ppermute | solution.py:392
  146.5 0.1 select_bitcast_fusion.1
  146.6 1.3 pad_maximum_fusion
  (24 shorter events, 0.2 us)
Async XLA Ops:
  0.6 25.6 %copy-start.3 = (bf16[1,1,128,256]{3,2,1,0:T(8,128)(2,1)S(1)}, bf16[1,1,128,256]{3,2,1,0:T(8,128)(2,1)}, u32[]{:S(2)}) copy-start(bf16[1,1,128,256]{3,2,1,0:T(8,128)(2,1)} %param.21) | copy-start | bytes 196612
  19.8 1.0 copy-start.4
  20.7 5.4 %copy-start.11 = (s32[1,1,5,128]{3,1,2,0:T(1,128)S(1)}, s32[1,1,5,128]{3,1,2,0:T(1,128)}, u32[]{:S(2)}) copy-start(s32[1,1,5,128]{3,1,2,0:T(1,128)} %param.20) | copy-start | bytes 7684
  20.7 5.4 %copy-start.10 = (s32[1,1,5,256]{3,1,2,0:T(1,128)S(1)}, s32[1,1,5,256]{3,1,2,0:T(1,128)}, u32[]{:S(2)}) copy-start(s32[1,1,5,256]{3,1,2,0:T(1,128)} %param.17) | copy-start | bytes 15364
  20.7 5.5 %copy-start.5 = (s32[1,1,5,256,4]{3,4,2,1,0:T(4,128)S(1)}, s32[1,1,5,256,4]{3,4,2,1,0:T(4,128)}, u32[]{:S(2)}) copy-start(s32[1,1,5,256,4]{3,4,2,1,0:T(4,128)} %param.16) | copy-start | bytes 61444
  20.7 5.5 %copy-start.6 = (s32[1,1,5,128,4]{3,4,2,1,0:T(4,128)S(1)}, s32[1,1,5,128,4]{3,4,2,1,0:T(4,128)}, u32[]{:S(2)}) copy-start(s32[1,1,5,128,4]{3,4,2,1,0:T(4,128)} %param.19) | copy-start | bytes 30724
  20.8 5.5 %copy-start.8 = (s32[1,1,256]{2,1,0:T(1,128)S(1)}, s32[1,1,256]{2,1,0:T(1,128)}, u32[]{:S(2)}) copy-start(s32[1,1,256]{2,1,0:T(1,128)} %param.15) | copy-start | bytes 3076
  20.8 5.5 %copy-start.9 = (s32[1,1,128]{2,1,0:T(1,128)S(1)}, s32[1,1,128]{2,1,0:T(1,128)}, u32[]{:S(2)}) copy-start(s32[1,1,128]{2,1,0:T(1,128)} %param.18) | copy-start | bytes 1540
  22.1 18.7 %copy-start.7 = (s32[1,1,32]{2,1,0:T(1,128)S(1)}, s32[1,1,32]{2,1,0:T(1,128)}, u32[]{:S(2)}) copy-start(s32[1,1,32]{2,1,0:T(1,128)} %param.14) | copy-start | bytes 388
  22.1 18.7 %all-to-all-start.1 = ((bf16[32,32,256]{2,1,0:T(8,128)(2,1)}), bf16[32,32,256]{2,1,0:T(8,128)(2,1)S(1)}, u32[]{:S(2)}, u32[]{:S(2)}) async-start(bf16[32,32,256]{2,1,0:T(8,128)(2,1)} %bitcast.4), calls=%async_computation.1 | async-start | bytes 1048576 | tf_op jit(solution)/shard_map/all_to_all | solution.py:300
  26.3 1.4 copy-start.2
  40.8 12.6 %copy-start = (bf16[1024,1536]{1,0:T(8,128)(2,1)S(1)}, bf16[1024,1536]{1,0:T(8,128)(2,1)}, u32[]{:S(2)}) copy-start(bf16[1024,1536]{1,0:T(8,128)(2,1)} %get-tuple-element.20.m1_ref) | copy-start | bytes 9437188
  46.8 9.2 %copy-start.1 = (f32[6,256,256]{2,1,0:T(8,128)}, f32[6,256,256]{2,1,0:T(8,128)S(1)}, u32[]{:S(2)}) copy-start(f32[6,256,256]{2,1,0:T(8,128)S(1)} %get-tuple-element.25) | copy-start | bytes 4718596
  46.8 13.1 %collective-permute-start = (bf16[6,256,256]{2,1,0:T(8,128)(2,1)}, bf16[6,256,256]{2,1,0:T(8,128)(2,1)S(1)}, u32[]{:S(2)}, u32[]{:S(2)}) collective-permute-start(bf16[6,256,256]{2,1,0:T(8,128)(2,1)} %get-tuple-element.26), channel_id=1, source_target_pairs={{0,32},{32,0},{64,96},{96,64},{128,160},{160,128},{192,224},{224,1... | collective-permute-start | bytes 2359304 | tf_op jit(solution)/shard_map/ppermute | solution.py:331
  56.1 20.7 %all-to-all-start.2 = ((bf16[32,32,256]{2,1,0:T(8,128)(2,1)}), bf16[32,32,256]{2,1,0:T(8,128)(2,1)S(1)}, u32[]{:S(2)}, u32[]{:S(2)}) async-start(bf16[32,32,256]{2,1,0:T(8,128)(2,1)} %bitcast.15), calls=%async_computation.2 | async-start | bytes 1048576 | tf_op jit(solution)/shard_map/all_to_all | solution.py:345
  76.7 27.7 %all-to-all-start.3 = ((bf16[32,48,256]{2,1,0:T(8,128)(2,1)}), bf16[32,48,256]{2,1,0:T(8,128)(2,1)S(1)}, u32[]{:S(2)}, u32[]{:S(2)}) async-start(bf16[32,48,256]{2,1,0:T(8,128)(2,1)} %bitcast.17), calls=%async_computation.3 | async-start | bytes 1572864 | tf_op jit(solution)/shard_map/all_to_all | solution.py:363
  91.2 3.4 %collective-permute-start.1 = (f32[256,256]{1,0:T(8,128)S(1)}, f32[256,256]{1,0:T(8,128)S(1)}, u32[]{:S(2)}, u32[]{:S(2)}) collective-permute-start(f32[256,256]{1,0:T(8,128)S(1)} %get-tuple-element.32), channel_id=1, source_target_pairs={{0,32},{32,0},{64,96},{96,64},{128,160},{160,128},{192,224},{224,1... | collective-permute-start | bytes 786440 | tf_op jit(solution)/shard_map/ppermute | solution.py:360
  94.7 14.0 %collective-permute-start.2 = (f32[128,256]{1,0:T(8,128)S(1)}, f32[128,256]{1,0:T(8,128)S(1)}, u32[]{:S(2)}, u32[]{:S(2)}) collective-permute-start(f32[128,256]{1,0:T(8,128)S(1)} %slice.25), channel_id=1, source_target_pairs={{0,64},{32,96},{64,0},{96,32},{128,192},{160,224},{192,128},{224,1... | collective-permute-start | bytes 393224 | tf_op jit(solution)/shard_map/ppermute | solution.py:360
  105.3 11.9 %all-to-all-start.4 = ((bf16[8,48,256]{2,1,0:T(8,128)(2,1)}), bf16[8,48,256]{2,1,0:T(8,128)(2,1)S(1)}, u32[]{:S(2)}, u32[]{:S(2)}) async-start(bf16[8,48,256]{2,1,0:T(8,128)(2,1)} %broadcast_in_dim.9), calls=%async_computation.4 | async-start | bytes 393216 | tf_op jit(solution)/shard_map/all_to_all | solution.py:369
  108.7 8.0 %collective-permute-start.3 = (f32[64,256]{1,0:T(8,128)S(1)}, f32[64,256]{1,0:T(8,128)S(1)}, u32[]{:S(2)}, u32[]{:S(2)}) collective-permute-start(f32[64,256]{1,0:T(8,128)S(1)} %slice.27), channel_id=1, source_target_pairs={{0,128},{32,160},{64,192},{96,224},{128,0},{160,32},{192,64},{224,... | collective-permute-start | bytes 196616 | tf_op jit(solution)/shard_map/ppermute | solution.py:360
  118.2 21.7 %all-to-all-start.5 = ((bf16[32,48,256]{2,1,0:T(8,128)(2,1)}), bf16[32,48,256]{2,1,0:T(8,128)(2,1)S(1)}, u32[]{:S(2)}, u32[]{:S(2)}) async-start(bf16[32,48,256]{2,1,0:T(8,128)(2,1)} %broadcast_in_dim.20), calls=%async_computation.5 | async-start | bytes 1572864 | tf_op jit(solution)/shard_map/all_to_all | solution.py:382
  123.1 16.2 %collective-permute-start.4 = (f32[32,256]{1,0:T(8,128)S(1)}, f32[32,256]{1,0:T(8,128)S(1)}, u32[]{:S(2)}, u32[]{:S(2)}) collective-permute-start(f32[32,256]{1,0:T(8,128)S(1)} %slice.23), channel_id=1, source_target_pairs={{0,256},{32,288},{64,320},{96,352},{128,384},{160,416},{192,448},{... | collective-permute-start | bytes 98312 | tf_op jit(solution)/shard_map/ppermute | solution.py:360
  139.9 6.6 %collective-permute-start.5 = (bf16[6,256,256]{2,1,0:T(8,128)(2,1)S(1)}, bf16[6,256,256]{2,1,0:T(8,128)(2,1)S(1)}, u32[]{:S(2)}, u32[]{:S(2)}) collective-permute-start(bf16[6,256,256]{2,1,0:T(8,128)(2,1)S(1)} %bitcast.48), channel_id=1, source_target_pairs={{0,32},{32,0},{64,96},{96,64},{128,160},{160,128},{192,224},{224,1... | collective-permute-start | bytes 2359304 | tf_op jit(solution)/shard_map/ppermute | solution.py:392

commit v5 on v4

--- a/solution.py
+++ b/solution.py
@@ -7,7 +7,7 @@
 
 BF = jnp.bfloat16
 F32 = jnp.float32
-PARAMS = pltpu.CompilerParams(vmem_limit_bytes=48 * 1024 * 1024)
+PARAMS = pltpu.CompilerParams(vmem_limit_bytes=20 * 1024 * 1024)
 
 
 def dot(a, b):
@@ -23,16 +23,19 @@
     return high, (x - high.astype(F32)).astype(BF)
 
 
-def gather_kernel(asked_ref, table_ref, out_ref, hot_ref):
+def gather_kernel(asked_ref, table_ref, out_ref, hot_ref, near_ref, sem):
+    copy = pltpu.make_async_copy(table_ref, near_ref, sem)
+    copy.start()
     groups, width = asked_ref.shape
-    rows = table_ref.shape[0]
+    rows = near_ref.shape[0]
     columns = jnp.transpose(asked_ref[...].astype(F32))
     lanes = lax.broadcasted_iota(jnp.int32, (width, rows), 1).astype(F32)
     for j in range(groups):
         hot_ref[pl.ds(j * width, width), :] = jnp.where(
             lanes == columns[:, j : j + 1], 1.0, 0.0
         ).astype(BF)
-    out_ref[...] = dot(hot_ref[...], table_ref[...]).astype(BF)
+    copy.wait()
+    out_ref[...] = dot(hot_ref[...], near_ref[...]).astype(BF)
 
 
 def counts_of(selfs, edges_ref, degree_ref, out_ref, height):
@@ -94,90 +97,46 @@
     back_ref[...] = jnp.transpose(dot(m2, high_ref[...]) + dot(m2, low_ref[...]))
 
 
-def main_kernel(
+def step_kernel(
     count_ref,
-    core_ref,
     x_ref,
     m1_ref,
-    m2_ref,
     wt_ref,
     back_ref,
-    degree1_ref,
-    degree2_ref,
-    cot_ref,
-    node_ref,
+    column_ref,
+    degree_ref,
+    slot_ref,
+    agg_ref,
+    hidden_ref,
     grad_ref,
-    keep_ref,
-    send_ref,
     live_ref,
-    agg_ref,
-    agg2_ref,
+    spread_ref,
 ):
     shards = count_ref.shape[1]
     slots, feature = x_ref.shape
     width = slots // shards
     kinds = wt_ref.shape[1]
-    nodes = degree1_ref.shape[1]
-    seeds = degree2_ref.shape[1]
+    nodes = degree_ref.shape[1]
     position = lax.broadcasted_iota(jnp.int32, (width, feature), 0)
     for k in range(shards):
         rows = x_ref[pl.ds(k * width, width), :].astype(F32)
         live_ref[pl.ds(k * width, width), :] = jnp.where(position < count_ref[0, k], rows, 0.0)
     xt = jnp.transpose(live_ref[...]).astype(BF)
-    inverse1 = 1.0 / degree1_ref[...].astype(F32)
-    inverse2 = 1.0 / degree2_ref[...].astype(F32)
+    inverse = 1.0 / degree_ref[...].astype(F32)
     pre = None
     for r in range(kinds):
         part = dot(xt, m1_ref[:, r * nodes : (r + 1) * nodes])
         if r > 0:
-            part = part * inverse1[r - 1 : r, :]
+            part = part * inverse[r - 1 : r, :]
         part = part.astype(BF)
         agg_ref[:, r * nodes : (r + 1) * nodes] = part
         term = dot(wt_ref[0, r], part)
         pre = term if pre is None else pre + term
     logistic = 1.0 / (1.0 + jnp.exp(-pre))
-    hidden = (pre * logistic).astype(BF)
+    hidden_ref[...] = (pre * logistic).astype(BF)
     slope = logistic * (1.0 + pre * (1.0 - logistic))
     grad_pre = jnp.transpose(back_ref[...] * slope).astype(BF)
-    out = None
-    for r in range(kinds):
-        part = dot(hidden, m2_ref[:, r * seeds : (r + 1) * seeds])
-        if r > 0:
-            part = part * inverse2[r - 1 : r, :]
-        part = part.astype(BF)
-        agg2_ref[:, r * seeds : (r + 1) * seeds] = part
-        term = dot(wt_ref[1, r], part)
-        out = term if out is None else out + term
-    node_ref[...] = jnp.transpose(out).astype(BF)
     grad_ref[...] = grad_pre
-
-    def bottom(r):
-        return dot(agg_ref[:, r * nodes : (r + 1) * nodes], grad_pre)
-
-    def top(r):
-        return dot(agg2_ref[:, r * seeds : (r + 1) * seeds], cot_ref[...])
-
-    @pl.when(core_ref[0] == 0)
-    def first():
-        for r in range(kinds):
-            keep_ref[r] = bottom(r)
-            send_ref[r] = top(r).astype(BF)
-
-    @pl.when(core_ref[0] != 0)
-    def second():
-        for r in range(kinds):
-            keep_ref[r] = top(r)
-            send_ref[r] = bottom(r).astype(BF)
-
-
-def slots_kernel(count_ref, grad_ref, m1_ref, wt_ref, column_ref, slot_ref, spread_ref, live_ref):
-    shards = count_ref.shape[1]
-    slots, feature = slot_ref.shape
-    width = slots // shards
-    kinds = wt_ref.shape[1]
-    nodes = grad_ref.shape[0]
-    position = lax.broadcasted_iota(jnp.int32, (width, feature), 0)
-    grad_pre = grad_ref[...]
     for r in range(kinds):
         part = dot(grad_pre, wt_ref[0, r])
         if r > 0:
@@ -189,6 +148,63 @@
         slot_ref[pl.ds(k * width, width), :] = jnp.where(
             position < count_ref[0, k], rows, 0.0
         ).astype(BF)
+
+
+def grads_kernel(
+    core_ref,
+    agg_ref,
+    hidden_ref,
+    grad_ref,
+    m2_ref,
+    wt_ref,
+    degree_ref,
+    cot_ref,
+    node_ref,
+    keep_ref,
+    send_ref,
+    send2_ref,
+    agg2_ref,
+):
+    kinds = wt_ref.shape[1]
+    nodes = grad_ref.shape[0]
+    seeds = cot_ref.shape[0]
+    inverse = 1.0 / degree_ref[...].astype(F32)
+    hidden = hidden_ref[...]
+    out = None
+    for r in range(kinds):
+        part = dot(hidden, m2_ref[:, r * seeds : (r + 1) * seeds])
+        if r > 0:
+            part = part * inverse[r - 1 : r, :]
+        part = part.astype(BF)
+        agg2_ref[:, r * seeds : (r + 1) * seeds] = part
+        term = dot(wt_ref[1, r], part)
+        out = term if out is None else out + term
+    node_ref[...] = jnp.transpose(out).astype(BF)
+
+    def bottom(r):
+        return dot(agg_ref[:, r * nodes : (r + 1) * nodes], grad_ref[...])
+
+    def top(r):
+        return dot(agg2_ref[:, r * seeds : (r + 1) * seeds], cot_ref[...])
+
+    def send(r, value):
+        half = send_ref.shape[0]
+        if r < half:
+            send_ref[r] = value
+        else:
+            send2_ref[r - half] = value
+
+    @pl.when(core_ref[0] == 0)
+    def first():
+        for r in range(kinds):
+            keep_ref[r] = bottom(r)
+            send(r, top(r).astype(BF))
+
+    @pl.when(core_ref[0] != 0)
+    def second():
+        for r in range(kinds):
+            keep_ref[r] = top(r)
+            send(r, bottom(r).astype(BF))
 
 
 def scatter_kernel(me_ref, asked_ref, grads_ref, keep_ref, give_ref, hot_ref):
@@ -291,58 +307,52 @@
     found = pl.pallas_call(
         gather_kernel,
         out_shape=shaped((slots, feature), BF),
-        in_specs=whole(2),
+        in_specs=whole(1) + [pl.BlockSpec(memory_space=pltpu.MemorySpace.HBM)],
         out_specs=whole(1)[0],
-        scratch_shapes=[pltpu.VMEM((slots, rows), BF)],
+        scratch_shapes=[
+            pltpu.VMEM((slots, rows), BF),
+            pltpu.VMEM((rows, feature), BF),
+            pltpu.SemaphoreType.DMA,
+        ],
         compiler_params=PARAMS,
         name="gather",
     )(asked, table)
     inputs = lax.all_to_all(found, "table", split_axis=0, concat_axis=0, tiled=True)
 
-    node_out, grad_pre, keep, send = pl.pallas_call(
-        main_kernel,
+    slot_grads, agg, hidden, grad_pre = pl.pallas_call(
+        step_kernel,
         out_shape=(
-            shaped((seeds, feature), BF),
+            shaped((slots, feature), BF),
+            shaped((feature, kinds * nodes), BF),
+            shaped((feature, nodes), BF),
             shaped((nodes, feature), BF),
-            shaped((kinds, feature, feature), F32),
-            shaped((kinds, feature, feature), BF),
         ),
-        in_specs=[smem, smem] + whole(8),
+        in_specs=[smem] + whole(6),
         out_specs=tuple(whole(4)),
         scratch_shapes=[
             pltpu.VMEM((slots, feature), F32),
-            pltpu.VMEM((feature, kinds * nodes), BF),
-            pltpu.VMEM((feature, kinds * seeds), BF),
+            pltpu.VMEM((kinds * nodes, feature), BF),
         ],
         compiler_params=PARAMS,
         name="step",
-    )(
-        fetch_count[0],
-        core.reshape(1),
-        inputs,
-        m1,
-        m2,
-        wt,
-        back,
-        degree1,
-        degree2,
-        cot,
-    )
-    other = lax.ppermute(send, "dp", swap)
-    slot_grads = pl.pallas_call(
-        slots_kernel,
-        out_shape=shaped((slots, feature), BF),
-        in_specs=[smem] + whole(4),
-        out_specs=whole(1)[0],
-        scratch_shapes=[
-            pltpu.VMEM((kinds * nodes, feature), BF),
-            pltpu.VMEM((slots, feature), F32),
-        ],
+    )(fetch_count[0], inputs, m1, wt, back, column, degree1)
+    returned = lax.all_to_all(slot_grads, "table", split_axis=0, concat_axis=0, tiled=True)
+
+    node_out, keep, send, send2 = pl.pallas_call(
+        grads_kernel,
+        out_shape=(
+            shaped((seeds, feature), BF),
+            shaped((kinds, feature, feature), F32),
+            shaped((kinds // 2, feature, feature), BF),
+            shaped((kinds // 2, feature, feature), BF),
+        ),
+        in_specs=[smem] + whole(7),
+        out_specs=tuple(whole(4)),
+        scratch_shapes=[pltpu.VMEM((feature, kinds * seeds), BF)],
         compiler_params=PARAMS,
-        name="slots",
-    )(fetch_count[0], grad_pre, m1, wt, column)
-
-    returned = lax.all_to_all(slot_grads, "table", split_axis=0, concat_axis=0, tiled=True)
+        name="grads",
+    )(core.reshape(1), agg, hidden, grad_pre, m2, wt, degree2, cot)
+    other = jnp.concatenate([lax.ppermute(send, "dp", swap), lax.ppermute(send2, "dp", swap)])
     half = (keep + other.astype(F32)).astype(BF).reshape(-1, feature)
     half, returned = lax.optimization_barrier((half, returned))
     share = rows // groups

time: 149 us -> 147 us (0.987)
  waiting for transfers between devices: 42.9 us -> 28.8 us
  local copies, waits for them, and re-layouts: 4.64 us -> 16.3 us
  starting transfers between devices: 56 us -> 61.5 us
  Pallas kernels: 18.8 us -> 15.2 us
    all_to_all x1, waiting for transfers between devices: 14.3 us -> 0.01 us  [body(): lax.all_to_all(slot_grads, 'table', split_axis=0, concat_axis=0, tiled=True)]
    unnamed x26 -> x48, local copies, waits for them, and re-layouts: 2.4 us -> 14 us
    all_to_all x1, starting transfers between devices: 3.39 us -> 6.37 us  [body(): lax.all_to_all(jnp.broadcast_to(partial[None], (chips,) + partial.shape)....]
    all_to_all x1, starting transfers between devices: 3.89 us -> 6.48 us  [body(): lax.all_to_all(slot_grads, 'table', split_axis=0, concat_axis=0, tiled=True)]
    pallas_call x2, Pallas kernels: 8.63 us -> 6.36 us  [the longest x1 4.22 us: body(): pl.pallas_call(step_kernel, out_shape=(shaped((slots, feature), BF), shap...]
    ppermute x1 -> x2, waiting for transfers between devices: 0.01 us -> 1.68 us  [the longest x1 1.68 us: body(): lax.ppermute(send2, 'dp', swap)]
    pallas_call x1, Pallas kernels: 8.43 us -> 6.78 us  [body(): pl.pallas_call(prepare_kernel, out_shape=(shaped((slots, kinds * nodes),...]
    ppermute x1 -> x2, starting transfers between devices: 6.6 us -> 6.16 us  [the longest x1 4.24 us: body(): lax.ppermute(send, 'dp', swap)]
  transfers between devices with their start and end apart: 11 -> 12, of which waited for: 8 -> 8; matrix products, arithmetic and copies ran while one was open for 4% -> 3% of each run, Pallas kernels for 8% -> 6%
where the time goes in v5:
time: 147 us; the launch traced here: 146 us
  starting transfers between devices  61.5 us (42%)
  waiting for transfers between devices  28.8 us (20%)
  blocking collectives  19.2 us (13%)
  local copies, waits for them, and re-layouts  16.3 us (11%)
  Pallas kernels  15.2 us (10%)
  other arithmetic  4.06 us (3%)
    all_to_all x1, blocking collectives, body(): lax.all_to_all(wanted, 'table', split_axis=0, concat_axis=0, tiled=True)  19.2 us
    ppermute x4, starting transfers between devices, halve(): got = lax.ppermute(give_rows, 'dp', [(i, i ^ bit) for i in range(groups)])  15.9 us
    unnamed x48, local copies, waits for them, and re-layouts  14 us
    ppermute x4, waiting for transfers between devices, halve(): got = lax.ppermute(give_rows, 'dp', [(i, i ^ bit) for i in range(groups)])  13.8 us
    all_to_all x1, starting transfers between devices, body(): lax.all_to_all(half, both, split_axis=0, concat_axis=0, tiled=True, axis_...  13 us
    pallas_call x1, Pallas kernels, body(): pl.pallas_call(prepare_kernel, out_shape=(shaped((slots, kinds * nodes),...  6.78 us
    all_to_all x1, starting transfers between devices, body(): lax.all_to_all(slot_grads, 'table', split_axis=0, concat_axis=0, tiled=True)  6.48 us
    all_to_all x1, waiting for transfers between devices, body(): lax.all_to_all(half, both, split_axis=0, concat_axis=0, tiled=True, axis_...  6.42 us
  transfers between devices with their start and end apart: 12, of which 8 were waited for; matrix products, arithmetic and copies ran while one was open for 3% of the time, Pallas kernels for 6%

profile of v5, /device:TPU:1, one launch (start us, length us, event | category | flops | bytes accessed | tf_op | source)
XLA Modules:
  0.0 146.0 jit_solution(10849930191851624143)
XLA Ops:
  0.7 19.2 %all_to_all.55 = s32[32,1,32]{2,1,0:T(1,128)S(1)} all-to-all(s32[32,1,32]{2,1,0:T(1,128)} %bitcast.50), channel_id=1, replica_groups=mesh['dp'=16,'table'=32] {'table'}, dimensions={0} | all-to-all | bytes 8192 | tf_op jit(solution)/shard_map/all_to_all | solution.py:274
  19.8 0.9 copy-done.3
  20.8 1.6 %gather.1 = bf16[1024,256]{1,0:T(8,128)(2,1)} custom-call(s32[32,32]{1,0:T(8,128)S(1)} %bitcast.37, bf16[512,256]{1,0:T(8,128)(2,1)S(1)} %copy-done.3), custom_call_target="tpu_custom_call" | custom-call | tf_op jit(solution)/shard_map/gather/pallas_call | solution.py:307
  22.4 3.9 %all-to-all-start.1 = ((bf16[32,32,256]{2,1,0:T(8,128)(2,1)}), bf16[32,32,256]{2,1,0:T(8,128)(2,1)S(1)}, u32[]{:S(2)}, u32[]{:S(2)}) async-start(bf16[32,32,256]{2,1,0:T(8,128)(2,1)} %bitcast.4), calls=%async_computation.1 | async-start | bytes 1048576 | tf_op jit(solution)/shard_map/all_to_all | solution.py:320
  26.4 0.6 copy-done.14
  27.0 1.4 copy-done.2
  28.4 6.8 %prepare.1 = (bf16[1024,1536]{1,0:T(8,128)(2,1)S(1)}, bf16[256,768]{1,0:T(8,128)(2,1)S(1)}, bf16[2,6,256,256]{3,2,1,0:T(8,128)(2,1)S(1)}, f32[256,256]{1,0:T(8,128)S(1)}, f32[256,8]{1,0:T(8,128)S(1)}) custom-call(s32[1,256]{1,0:T(1,128)S(1)} %bitcast.44, s32[5,4,256]{2,1,0:T(4,128)S(1)} %bitcast.42, s32[5,256]{1,0:T(8,128)S(1)} %bitcast.38, ...), custom_call_target="tpu_custom_call" | custom-call | tf_op jit(solution)/shard_map/prepare/pallas_call | solution.py:279
  35.2 1.6 %copy-done = bf16[1024,1536]{1,0:T(8,128)(2,1)} copy-done((bf16[1024,1536]{1,0:T(8,128)(2,1)}, bf16[1024,1536]{1,0:T(8,128)(2,1)S(1)}, u32[]{:S(2)}) %copy-start) | copy-done | bytes 3145752
  36.8 0.7 copy-done.10
  37.5 3.5 %all-to-all-done.1 = bf16[32,32,256]{2,1,0:T(8,128)(2,1)S(1)} async-done(((bf16[32,32,256]{2,1,0:T(8,128)(2,1)}), bf16[32,32,256]{2,1,0:T(8,128)(2,1)S(1)}, u32[]{:S(2)}, u32[]{:S(2)}) %all-to-all-start.1) | async-done | bytes 524320 | tf_op jit(solution)/shard_map/all_to_all | solution.py:320
  41.0 1.9 %copy-done.1 = bf16[1024,1536]{1,0:T(8,128)(2,1)S(1)} copy-done((bf16[1024,1536]{1,0:T(8,128)(2,1)S(1)}, bf16[1024,1536]{1,0:T(8,128)(2,1)}, u32[]{:S(2)}) %copy-start.1) | copy-done | bytes 3145752
  42.8 0.9 copy-done.11
  43.8 0.7 copy-done.13
  44.5 0.7 copy-done.20
  45.1 4.2 %step.1 = (bf16[1024,256]{1,0:T(8,128)(2,1)}, bf16[256,1536]{1,0:T(8,128)(2,1)S(1)}, bf16[256,256]{1,0:T(8,128)(2,1)S(1)}, bf16[256,256]{1,0:T(8,128)(2,1)S(1)}) custom-call(s32[1,32]{1,0:T(1,128)S(1)} %bitcast.46, bf16[1024,256]{1,0:T(8,128)(2,1)S(1)} %bitcast.33, bf16[1024,1536]{1,0:T(8,128)(2,1)S(1)} %copy-done.1, ...), custom_call_target="tpu_custom_call" | custom-call | tf_op jit(solution)/shard_map/step/pallas_call | solution.py:322
  49.3 0.7 copy-done.6
  50.0 0.6 copy-done.8
  50.6 6.5 %all-to-all-start.2 = ((bf16[32,32,256]{2,1,0:T(8,128)(2,1)}), bf16[32,32,256]{2,1,0:T(8,128)(2,1)S(1)}, u32[]{:S(2)}, u32[]{:S(2)}) async-start(bf16[32,32,256]{2,1,0:T(8,128)(2,1)} %bitcast.15), calls=%async_computation.2 | async-start | bytes 1048576 | tf_op jit(solution)/shard_map/all_to_all | solution.py:339
  57.1 0.8 copy-done.5
  58.0 0.9 copy-done.7
  58.9 0.9 copy-done.9
  59.8 0.7 copy-done.15
  60.5 2.1 %grads.1 = (bf16[128,256]{1,0:T(8,128)(2,1)}, f32[6,256,256]{2,1,0:T(8,128)S(1)}, bf16[3,256,256]{2,1,0:T(8,128)(2,1)S(1)}, bf16[3,256,256]{2,1,0:T(8,128)(2,1)S(1)}) custom-call(s32[1]{0:T(128)} %bitcast.core_ref, bf16[256,1536]{1,0:T(8,128)(2,1)S(1)} %get-tuple-element.28.agg_ref, bf16[256,256]{1,0:T(8,128)(2,1)S(1)} %copy-done.7, ...), custom_call_target="tpu_custom_call" | custom-call | tf_op jit(solution)/shard_map/grads/pallas_call | solution.py:341
  62.6 4.2 %collective-permute-start = (bf16[3,256,256]{2,1,0:T(8,128)(2,1)S(1)}, bf16[3,256,256]{2,1,0:T(8,128)(2,1)S(1)}, u32[]{:S(2)}, u32[]{:S(2)}) collective-permute-start(bf16[3,256,256]{2,1,0:T(8,128)(2,1)S(1)} %get-tuple-element.34), channel_id=1, source_target_pairs={{0,32},{32,0},{64,96},{96,64},{128,160},{160,128},{192,224},{224,1... | collective-permute-start | bytes 1179656 | tf_op jit(solution)/shard_map/ppermute | solution.py:355
  66.9 1.9 %collective-permute-start.1 = (bf16[3,256,256]{2,1,0:T(8,128)(2,1)S(1)}, bf16[3,256,256]{2,1,0:T(8,128)(2,1)S(1)}, u32[]{:S(2)}, u32[]{:S(2)}) collective-permute-start(bf16[3,256,256]{2,1,0:T(8,128)(2,1)S(1)} %get-tuple-element.35), channel_id=1, source_target_pairs={{0,32},{32,0},{64,96},{96,64},{128,160},{160,128},{192,224},{224,1... | collective-permute-start | bytes 1179656 | tf_op jit(solution)/shard_map/ppermute | solution.py:355
  68.8 1.7 %collective-permute-done.1 = bf16[3,256,256]{2,1,0:T(8,128)(2,1)S(1)} collective-permute-done((bf16[3,256,256]{2,1,0:T(8,128)(2,1)S(1)}, bf16[3,256,256]{2,1,0:T(8,128)(2,1)S(1)}, u32[]{:S(2)}, u32[]{:S(2)}) %collective-permute-start.1) | collective-permute-done | bytes 393248 | tf_op jit(solution)/shard_map/ppermute | solution.py:355
  70.5 1.1 add_convert_fusion
  71.6 13.0 %all-to-all-start.3 = ((bf16[32,48,256]{2,1,0:T(8,128)(2,1)}), bf16[32,48,256]{2,1,0:T(8,128)(2,1)S(1)}, u32[]{:S(2)}, u32[]{:S(2)}) async-start(bf16[32,48,256]{2,1,0:T(8,128)(2,1)} %bitcast.17), calls=%async_computation.3 | async-start | bytes 1572864 | tf_op jit(solution)/shard_map/all_to_all | solution.py:373
  84.6 0.6 broadcast.7
  85.2 0.7 reduce.5
  86.0 0.4 scatter.1
  86.4 1.9 %collective-permute-start.2 = (f32[256,256]{1,0:T(8,128)S(1)}, f32[256,256]{1,0:T(8,128)S(1)}, u32[]{:S(2)}, u32[]{:S(2)}) collective-permute-start(f32[256,256]{1,0:T(8,128)S(1)} %get-tuple-element.40), channel_id=1, source_target_pairs={{0,32},{32,0},{64,96},{96,64},{128,160},{160,128},{192,224},{224,1... | collective-permute-start | bytes 786440 | tf_op jit(solution)/shard_map/ppermute | solution.py:370
  88.3 1.5 %collective-permute-done.2 = f32[256,256]{1,0:T(8,128)S(1)} collective-permute-done((f32[256,256]{1,0:T(8,128)S(1)}, f32[256,256]{1,0:T(8,128)S(1)}, u32[]{:S(2)}, u32[]{:S(2)}) %collective-permute-start.2) | collective-permute-done | bytes 262176 | tf_op jit(solution)/shard_map/ppermute | solution.py:370
  89.9 3.1 %collective-permute-start.3 = (f32[128,256]{1,0:T(8,128)S(1)}, f32[128,256]{1,0:T(8,128)S(1)}, u32[]{:S(2)}, u32[]{:S(2)}) collective-permute-start(f32[128,256]{1,0:T(8,128)S(1)} %slice.25), channel_id=1, source_target_pairs={{0,64},{32,96},{64,0},{96,32},{128,192},{160,224},{192,128},{224,1... | collective-permute-start | bytes 393224 | tf_op jit(solution)/shard_map/ppermute | solution.py:370
  93.0 6.4 %all-to-all-done.3 = bf16[32,48,256]{2,1,0:T(8,128)(2,1)S(1)} async-done(((bf16[32,48,256]{2,1,0:T(8,128)(2,1)}), bf16[32,48,256]{2,1,0:T(8,128)(2,1)S(1)}, u32[]{:S(2)}, u32[]{:S(2)}) %all-to-all-start.3) | async-done | bytes 786464 | tf_op jit(solution)/shard_map/all_to_all | solution.py:373
  99.6 0.7 broadcast_in_dim.9
  100.3 6.4 %all-to-all-start.4 = ((bf16[8,48,256]{2,1,0:T(8,128)(2,1)}), bf16[8,48,256]{2,1,0:T(8,128)(2,1)S(1)}, u32[]{:S(2)}, u32[]{:S(2)}) async-start(bf16[8,48,256]{2,1,0:T(8,128)(2,1)} %broadcast_in_dim.9), calls=%async_computation.4 | async-start | bytes 393216 | tf_op jit(solution)/shard_map/all_to_all | solution.py:379
  106.7 3.8 %collective-permute-start.4 = (f32[64,256]{1,0:T(8,128)S(1)}, f32[64,256]{1,0:T(8,128)S(1)}, u32[]{:S(2)}, u32[]{:S(2)}) collective-permute-start(f32[64,256]{1,0:T(8,128)S(1)} %slice.27), channel_id=1, source_target_pairs={{0,128},{32,160},{64,192},{96,224},{128,0},{160,32},{192,64},{224,... | collective-permute-start | bytes 196616 | tf_op jit(solution)/shard_map/ppermute | solution.py:370
  110.5 3.3 %collective-permute-done.4 = f32[64,256]{1,0:T(8,128)S(1)} collective-permute-done((f32[64,256]{1,0:T(8,128)S(1)}, f32[64,256]{1,0:T(8,128)S(1)}, u32[]{:S(2)}, u32[]{:S(2)}) %collective-permute-start.4) | collective-permute-done | bytes 65568 | tf_op jit(solution)/shard_map/ppermute | solution.py:370
  113.8 1.5 %all-to-all-done.4 = bf16[8,48,256]{2,1,0:T(8,128)(2,1)S(1)} async-done(((bf16[8,48,256]{2,1,0:T(8,128)(2,1)}), bf16[8,48,256]{2,1,0:T(8,128)(2,1)S(1)}, u32[]{:S(2)}, u32[]{:S(2)}) %all-to-all-start.4) | async-done | bytes 196640 | tf_op jit(solution)/shard_map/all_to_all | solution.py:379
  115.3 0.9 broadcast_in_dim.20
  116.3 4.7 %all-to-all-start.5 = ((bf16[32,48,256]{2,1,0:T(8,128)(2,1)}), bf16[32,48,256]{2,1,0:T(8,128)(2,1)S(1)}, u32[]{:S(2)}, u32[]{:S(2)}) async-start(bf16[32,48,256]{2,1,0:T(8,128)(2,1)} %broadcast_in_dim.20), calls=%async_computation.5 | async-start | bytes 1572864 | tf_op jit(solution)/shard_map/all_to_all | solution.py:392
  121.0 7.1 %collective-permute-start.5 = (f32[32,256]{1,0:T(8,128)S(1)}, f32[32,256]{1,0:T(8,128)S(1)}, u32[]{:S(2)}, u32[]{:S(2)}) collective-permute-start(f32[32,256]{1,0:T(8,128)S(1)} %slice.23), channel_id=1, source_target_pairs={{0,256},{32,288},{64,320},{96,352},{128,384},{160,416},{192,448},{... | collective-permute-start | bytes 98312 | tf_op jit(solution)/shard_map/ppermute | solution.py:370
  128.1 9.1 %collective-permute-done.5 = f32[32,256]{1,0:T(8,128)S(1)} collective-permute-done((f32[32,256]{1,0:T(8,128)S(1)}, f32[32,256]{1,0:T(8,128)S(1)}, u32[]{:S(2)}, u32[]{:S(2)}) %collective-permute-start.5) | collective-permute-done | bytes 32800 | tf_op jit(solution)/shard_map/ppermute | solution.py:370
  137.1 0.6 slice_add_fusion.2
  137.8 4.9 %collective-permute-start.6 = (bf16[6,256,256]{2,1,0:T(8,128)(2,1)S(1)}, bf16[6,256,256]{2,1,0:T(8,128)(2,1)S(1)}, u32[]{:S(2)}, u32[]{:S(2)}) collective-permute-start(bf16[6,256,256]{2,1,0:T(8,128)(2,1)S(1)} %bitcast.47), channel_id=1, source_target_pairs={{0,32},{32,0},{64,96},{96,64},{128,160},{160,128},{192,224},{224,1... | collective-permute-start | bytes 2359304 | tf_op jit(solution)/shard_map/ppermute | solution.py:402
  142.7 1.9 %collective-permute-done.6 = bf16[6,256,256]{2,1,0:T(8,128)(2,1)S(1)} collective-permute-done((bf16[6,256,256]{2,1,0:T(8,128)(2,1)S(1)}, bf16[6,256,256]{2,1,0:T(8,128)(2,1)S(1)}, u32[]{:S(2)}, u32[]{:S(2)}) %collective-permute-start.6) | collective-permute-done | bytes 786464 | tf_op jit(solution)/shard_map/ppermute | solution.py:402
  144.7 1.3 pad_maximum_fusion
  (48 shorter events, 0.5 us)
Async XLA Ops:
  0.6 25.7 %copy-start.22 = (s32[1,1,5,128]{3,1,2,0:T(1,128)S(1)}, s32[1,1,5,128]{3,1,2,0:T(1,128)}, u32[]{:S(2)}) copy-start(s32[1,1,5,128]{3,1,2,0:T(1,128)} %param.20) | copy-start | bytes 7684
  0.6 26.3 %copy-start.17 = (s32[1,1,5,128,4]{3,4,2,1,0:T(4,128)S(1)}, s32[1,1,5,128,4]{3,4,2,1,0:T(4,128)}, u32[]{:S(2)}) copy-start(s32[1,1,5,128,4]{3,4,2,1,0:T(4,128)} %param.19) | copy-start | bytes 30724
  0.7 26.3 %copy-start.19 = (s32[1,1,128]{2,1,0:T(1,128)S(1)}, s32[1,1,128]{2,1,0:T(1,128)}, u32[]{:S(2)}) copy-start(s32[1,1,128]{2,1,0:T(1,128)} %param.18) | copy-start | bytes 1540
  0.7 26.3 %copy-start.16 = (s32[1,1,5,256,4]{3,4,2,1,0:T(4,128)S(1)}, s32[1,1,5,256,4]{3,4,2,1,0:T(4,128)}, u32[]{:S(2)}) copy-start(s32[1,1,5,256,4]{3,4,2,1,0:T(4,128)} %param.16) | copy-start | bytes 61444
  0.7 26.3 %copy-start.18 = (s32[1,1,256]{2,1,0:T(1,128)S(1)}, s32[1,1,256]{2,1,0:T(1,128)}, u32[]{:S(2)}) copy-start(s32[1,1,256]{2,1,0:T(1,128)} %param.15) | copy-start | bytes 3076
  19.8 1.0 copy-start.3
  20.8 5.5 %copy-start.21 = (s32[1,1,5,256]{3,1,2,0:T(1,128)S(1)}, s32[1,1,5,256]{3,1,2,0:T(1,128)}, u32[]{:S(2)}) copy-start(s32[1,1,5,256]{3,1,2,0:T(1,128)} %param.17) | copy-start | bytes 15364
  20.8 6.2 %copy-start.4 = (bf16[1,1,128,256]{3,2,1,0:T(8,128)(2,1)S(1)}, bf16[1,1,128,256]{3,2,1,0:T(8,128)(2,1)}, u32[]{:S(2)}) copy-start(bf16[1,1,128,256]{3,2,1,0:T(8,128)(2,1)} %param.21) | copy-start | bytes 196612
  22.4 18.6 %all-to-all-start.1 = ((bf16[32,32,256]{2,1,0:T(8,128)(2,1)}), bf16[32,32,256]{2,1,0:T(8,128)(2,1)S(1)}, u32[]{:S(2)}, u32[]{:S(2)}) async-start(bf16[32,32,256]{2,1,0:T(8,128)(2,1)} %bitcast.4), calls=%async_computation.1 | async-start | bytes 1048576 | tf_op jit(solution)/shard_map/all_to_all | solution.py:320
  26.3 0.6 copy-start.14
  26.4 0.6 copy-start.12
  27.0 1.4 copy-start.2
  35.2 1.6 %copy-start = (bf16[1024,1536]{1,0:T(8,128)(2,1)}, bf16[1024,1536]{1,0:T(8,128)(2,1)S(1)}, u32[]{:S(2)}) copy-start(bf16[1024,1536]{1,0:T(8,128)(2,1)S(1)} %get-tuple-element.24.m1_ref) | copy-start | bytes 9437188
  36.8 0.7 copy-start.10
  41.0 1.9 %copy-start.1 = (bf16[1024,1536]{1,0:T(8,128)(2,1)S(1)}, bf16[1024,1536]{1,0:T(8,128)(2,1)}, u32[]{:S(2)}) copy-start(bf16[1024,1536]{1,0:T(8,128)(2,1)} %copy-done) | copy-start | bytes 9437188
  42.8 0.9 copy-start.11
  43.8 0.7 copy-start.13
  44.4 0.7 copy-start.20
  49.3 0.7 copy-start.6
  50.0 0.6 copy-start.8
  50.6 21.0 %all-to-all-start.2 = ((bf16[32,32,256]{2,1,0:T(8,128)(2,1)}), bf16[32,32,256]{2,1,0:T(8,128)(2,1)S(1)}, u32[]{:S(2)}, u32[]{:S(2)}) async-start(bf16[32,32,256]{2,1,0:T(8,128)(2,1)} %bitcast.15), calls=%async_computation.2 | async-start | bytes 1048576 | tf_op jit(solution)/shard_map/all_to_all | solution.py:339
  57.1 0.8 copy-start.5
  58.0 0.9 copy-start.7
  58.9 0.9 copy-start.9
  59.8 0.7 copy-start.15
  62.6 6.2 %collective-permute-start = (bf16[3,256,256]{2,1,0:T(8,128)(2,1)S(1)}, bf16[3,256,256]{2,1,0:T(8,128)(2,1)S(1)}, u32[]{:S(2)}, u32[]{:S(2)}) collective-permute-start(bf16[3,256,256]{2,1,0:T(8,128)(2,1)S(1)} %get-tuple-element.34), channel_id=1, source_target_pairs={{0,32},{32,0},{64,96},{96,64},{128,160},{160,128},{192,224},{224,1... | collective-permute-start | bytes 1179656 | tf_op jit(solution)/shard_map/ppermute | solution.py:355
  66.9 3.6 %collective-permute-start.1 = (bf16[3,256,256]{2,1,0:T(8,128)(2,1)S(1)}, bf16[3,256,256]{2,1,0:T(8,128)(2,1)S(1)}, u32[]{:S(2)}, u32[]{:S(2)}) collective-permute-start(bf16[3,256,256]{2,1,0:T(8,128)(2,1)S(1)} %get-tuple-element.35), channel_id=1, source_target_pairs={{0,32},{32,0},{64,96},{96,64},{128,160},{160,128},{192,224},{224,1... | collective-permute-start | bytes 1179656 | tf_op jit(solution)/shard_map/ppermute | solution.py:355
  71.6 27.9 %all-to-all-start.3 = ((bf16[32,48,256]{2,1,0:T(8,128)(2,1)}), bf16[32,48,256]{2,1,0:T(8,128)(2,1)S(1)}, u32[]{:S(2)}, u32[]{:S(2)}) async-start(bf16[32,48,256]{2,1,0:T(8,128)(2,1)} %bitcast.17), calls=%async_computation.3 | async-start | bytes 1572864 | tf_op jit(solution)/shard_map/all_to_all | solution.py:373
  86.4 3.4 %collective-permute-start.2 = (f32[256,256]{1,0:T(8,128)S(1)}, f32[256,256]{1,0:T(8,128)S(1)}, u32[]{:S(2)}, u32[]{:S(2)}) collective-permute-start(f32[256,256]{1,0:T(8,128)S(1)} %get-tuple-element.40), channel_id=1, source_target_pairs={{0,32},{32,0},{64,96},{96,64},{128,160},{160,128},{192,224},{224,1... | collective-permute-start | bytes 786440 | tf_op jit(solution)/shard_map/ppermute | solution.py:370
  89.9 16.8 %collective-permute-start.3 = (f32[128,256]{1,0:T(8,128)S(1)}, f32[128,256]{1,0:T(8,128)S(1)}, u32[]{:S(2)}, u32[]{:S(2)}) collective-permute-start(f32[128,256]{1,0:T(8,128)S(1)} %slice.25), channel_id=1, source_target_pairs={{0,64},{32,96},{64,0},{96,32},{128,192},{160,224},{192,128},{224,1... | collective-permute-start | bytes 393224 | tf_op jit(solution)/shard_map/ppermute | solution.py:370
  100.3 15.0 %all-to-all-start.4 = ((bf16[8,48,256]{2,1,0:T(8,128)(2,1)}), bf16[8,48,256]{2,1,0:T(8,128)(2,1)S(1)}, u32[]{:S(2)}, u32[]{:S(2)}) async-start(bf16[8,48,256]{2,1,0:T(8,128)(2,1)} %broadcast_in_dim.9), calls=%async_computation.4 | async-start | bytes 393216 | tf_op jit(solution)/shard_map/all_to_all | solution.py:379
  106.7 7.1 %collective-permute-start.4 = (f32[64,256]{1,0:T(8,128)S(1)}, f32[64,256]{1,0:T(8,128)S(1)}, u32[]{:S(2)}, u32[]{:S(2)}) collective-permute-start(f32[64,256]{1,0:T(8,128)S(1)} %slice.27), channel_id=1, source_target_pairs={{0,128},{32,160},{64,192},{96,224},{128,0},{160,32},{192,64},{224,... | collective-permute-start | bytes 196616 | tf_op jit(solution)/shard_map/ppermute | solution.py:370
  116.3 21.5 %all-to-all-start.5 = ((bf16[32,48,256]{2,1,0:T(8,128)(2,1)}), bf16[32,48,256]{2,1,0:T(8,128)(2,1)S(1)}, u32[]{:S(2)}, u32[]{:S(2)}) async-start(bf16[32,48,256]{2,1,0:T(8,128)(2,1)} %broadcast_in_dim.20), calls=%async_computation.5 | async-start | bytes 1572864 | tf_op jit(solution)/shard_map/all_to_all | solution.py:392
  121.0 16.1 %collective-permute-start.5 = (f32[32,256]{1,0:T(8,128)S(1)}, f32[32,256]{1,0:T(8,128)S(1)}, u32[]{:S(2)}, u32[]{:S(2)}) collective-permute-start(f32[32,256]{1,0:T(8,128)S(1)} %slice.23), channel_id=1, source_target_pairs={{0,256},{32,288},{64,320},{96,352},{128,384},{160,416},{192,448},{... | collective-permute-start | bytes 98312 | tf_op jit(solution)/shard_map/ppermute | solution.py:370
  137.8 6.8 %collective-permute-start.6 = (bf16[6,256,256]{2,1,0:T(8,128)(2,1)S(1)}, bf16[6,256,256]{2,1,0:T(8,128)(2,1)S(1)}, u32[]{:S(2)}, u32[]{:S(2)}) collective-permute-start(bf16[6,256,256]{2,1,0:T(8,128)(2,1)S(1)} %bitcast.47), channel_id=1, source_target_pairs={{0,32},{32,0},{64,96},{96,64},{128,160},{160,128},{192,224},{224,1... | collective-permute-start | bytes 2359304 | tf_op jit(solution)/shard_map/ppermute | solution.py:402

commit v6 on v5

--- a/solution.py
+++ b/solution.py
@@ -7,7 +7,8 @@
 
 BF = jnp.bfloat16
 F32 = jnp.float32
-PARAMS = pltpu.CompilerParams(vmem_limit_bytes=20 * 1024 * 1024)
+PARAMS = pltpu.CompilerParams(vmem_limit_bytes=58 * 1024 * 1024)
+ROOMY = pltpu.CompilerParams(vmem_limit_bytes=52 * 1024 * 1024)
 
 
 def dot(a, b):
@@ -43,7 +44,7 @@
     slots = lax.broadcasted_iota(jnp.int32, (height, nodes), 0)
     out_ref[:, 0:nodes] = jnp.where(slots == selfs, 1.0, 0.0).astype(BF)
     for r in range(relations):
-        degree = degree_ref[r : r + 1, :]
+        degree = degree_ref[:, r * nodes : (r + 1) * nodes]
         total = None
         for f in range(fan):
             edge = jnp.where(degree > f, edges_ref[r, f : f + 1, :], -1)
@@ -52,11 +53,13 @@
         out_ref[:, (r + 1) * nodes : (r + 2) * nodes] = total.astype(BF)
 
 
-def inverse_columns(degree_ref):
-    relations, nodes = degree_ref.shape
+def inverse_columns(degree_ref, relations):
+    nodes = degree_ref.shape[1] // relations
     inverse = 1.0 / degree_ref[...].astype(F32)
-    padded = jnp.concatenate([inverse, jnp.ones((8 - relations, nodes), F32)], axis=0)
-    return jnp.transpose(padded)
+    rows = [inverse[:, r * nodes : (r + 1) * nodes] for r in range(relations)]
+    return jnp.transpose(
+        jnp.concatenate(rows + [jnp.ones((8 - relations, nodes), F32)], axis=0)
+    )
 
 
 def prepare_kernel(
@@ -82,8 +85,8 @@
     for layer in range(layers):
         for r in range(kinds):
             wt_ref[layer, r] = jnp.transpose(weights_ref[layer, r].astype(F32)).astype(BF)
-    column_ref[...] = inverse_columns(degree1_ref)
-    column2 = inverse_columns(degree2_ref)
+    column_ref[...] = inverse_columns(degree1_ref, edges1_ref.shape[0])
+    column2 = inverse_columns(degree2_ref, edges2_ref.shape[0])
     seeds = cot_ref.shape[0]
     cot = cot_ref[...]
     for r in range(kinds):
@@ -100,8 +103,8 @@
 def step_kernel(
     count_ref,
     x_ref,
-    m1_ref,
-    wt_ref,
+    m1_far,
+    wt_far,
     back_ref,
     column_ref,
     degree_ref,
@@ -111,23 +114,34 @@
     grad_ref,
     live_ref,
     spread_ref,
+    m1_ref,
+    wt_ref,
+    sems,
 ):
+    copies = [
+        pltpu.make_async_copy(m1_far, m1_ref, sems.at[0]),
+        pltpu.make_async_copy(wt_far.at[pl.ds(0, 1)], wt_ref, sems.at[1]),
+    ]
+    for copy in copies:
+        copy.start()
     shards = count_ref.shape[1]
     slots, feature = x_ref.shape
     width = slots // shards
     kinds = wt_ref.shape[1]
-    nodes = degree_ref.shape[1]
+    nodes = grad_ref.shape[0]
     position = lax.broadcasted_iota(jnp.int32, (width, feature), 0)
     for k in range(shards):
         rows = x_ref[pl.ds(k * width, width), :].astype(F32)
         live_ref[pl.ds(k * width, width), :] = jnp.where(position < count_ref[0, k], rows, 0.0)
     xt = jnp.transpose(live_ref[...]).astype(BF)
     inverse = 1.0 / degree_ref[...].astype(F32)
+    for copy in copies:
+        copy.wait()
     pre = None
     for r in range(kinds):
         part = dot(xt, m1_ref[:, r * nodes : (r + 1) * nodes])
         if r > 0:
-            part = part * inverse[r - 1 : r, :]
+            part = part * inverse[:, (r - 1) * nodes : r * nodes]
         part = part.astype(BF)
         agg_ref[:, r * nodes : (r + 1) * nodes] = part
         term = dot(wt_ref[0, r], part)
@@ -174,7 +188,7 @@
     for r in range(kinds):
         part = dot(hidden, m2_ref[:, r * seeds : (r + 1) * seeds])
         if r > 0:
-            part = part * inverse[r - 1 : r, :]
+            part = part * inverse[:, (r - 1) * seeds : r * seeds]
         part = part.astype(BF)
         agg2_ref[:, r * seeds : (r + 1) * seeds] = part
         term = dot(wt_ref[1, r], part)
@@ -269,12 +283,13 @@
     lines = [
         [device(z, 0, y, x) for z in range(chips)] for y in range(down) for x in range(across)
     ] + [[device(z, 1, y, x) for y in range(down)] for z in range(chips) for x in range(across)]
+    far = pl.BlockSpec(memory_space=pl.ANY)
     smem = pl.BlockSpec(memory_space=pltpu.SMEM)
 
     asked = lax.all_to_all(wanted, "table", split_axis=0, concat_axis=0, tiled=True)
 
-    degree1 = first_degree[0, 0]
-    degree2 = second_degree[0, 0]
+    degree1 = first_degree.reshape(1, -1)
+    degree2 = second_degree.reshape(1, -1)
     cot = cotangent[0, 0]
     m1, m2, wt, back, column = pl.pallas_call(
         prepare_kernel,
@@ -307,7 +322,7 @@
     found = pl.pallas_call(
         gather_kernel,
         out_shape=shaped((slots, feature), BF),
-        in_specs=whole(1) + [pl.BlockSpec(memory_space=pltpu.MemorySpace.HBM)],
+        in_specs=whole(1) + [far],
         out_specs=whole(1)[0],
         scratch_shapes=[
             pltpu.VMEM((slots, rows), BF),
@@ -327,11 +342,14 @@
             shaped((feature, nodes), BF),
             shaped((nodes, feature), BF),
         ),
-        in_specs=[smem] + whole(6),
+        in_specs=[smem] + whole(1) + [far] * 2 + whole(3),
         out_specs=tuple(whole(4)),
         scratch_shapes=[
             pltpu.VMEM((slots, feature), F32),
             pltpu.VMEM((kinds * nodes, feature), BF),
+            pltpu.VMEM((slots, kinds * nodes), BF),
+            pltpu.VMEM((1, kinds, feature, feature), BF),
+            pltpu.SemaphoreType.DMA((2,)),
         ],
         compiler_params=PARAMS,
         name="step",
@@ -362,7 +380,7 @@
         in_specs=[smem] + whole(2),
         out_specs=tuple(whole(2)),
         scratch_shapes=[pltpu.VMEM((rows, slots), BF)],
-        compiler_params=PARAMS,
+        compiler_params=ROOMY,
         name="scatter",
     )(lax.axis_index("dp").reshape(1), asked.reshape(1, slots), returned)
 

time: 147 us -> 147 us (level)
  local copies, waits for them, and re-layouts: 16.3 us -> 3.12 us
  Pallas kernels: 15.2 us -> 25.1 us
  waiting for transfers between devices: 28.8 us -> 30.5 us
    unnamed x48 -> x4, local copies, waits for them, and re-layouts: 14 us -> 0.82 us
    pallas_call x1, Pallas kernels: 6.78 us -> 9.93 us  [body(): pl.pallas_call(prepare_kernel, out_shape=(shaped((slots, kinds * nodes),...]
    pallas_call x1, Pallas kernels: 4.22 us -> 6.98 us  [body(): pl.pallas_call(step_kernel, out_shape=(shaped((slots, feature), BF), shap...]
    pallas_call x1, Pallas kernels: 2.14 us -> 4.82 us  [body(): pl.pallas_call(grads_kernel, out_shape=(shaped((seeds, feature), BF), sha...]
    all_to_all x1, waiting for transfers between devices: 3.48 us -> 5 us  [body(): lax.all_to_all(found, 'table', split_axis=0, concat_axis=0, tiled=True)]
  transfers between devices with their start and end apart: 12 -> 12, of which waited for: 8 -> 8; matrix products, arithmetic and copies ran while one was open for 3% -> 4% of each run, Pallas kernels for 6% -> 10%
where the time goes in v6:
time: 147 us; the launch traced here: 146 us
  starting transfers between devices  61.4 us (42%)
  waiting for transfers between devices  30.5 us (21%)
  Pallas kernels  25.1 us (17%)
  blocking collectives  19.1 us (13%)
  other arithmetic  5.42 us (4%)
  local copies, waits for them, and re-layouts  3.12 us (2%)
    all_to_all x1, blocking collectives, body(): lax.all_to_all(wanted, 'table', split_axis=0, concat_axis=0, tiled=True)  19.1 us
    ppermute x4, starting transfers between devices, halve(): got = lax.ppermute(give_rows, 'dp', [(i, i ^ bit) for i in range(groups)])  15.9 us
    ppermute x4, waiting for transfers between devices, halve(): got = lax.ppermute(give_rows, 'dp', [(i, i ^ bit) for i in range(groups)])  13.8 us
    all_to_all x1, starting transfers between devices, body(): lax.all_to_all(half, both, split_axis=0, concat_axis=0, tiled=True, axis_...  13.1 us
    pallas_call x1, Pallas kernels, body(): pl.pallas_call(prepare_kernel, out_shape=(shaped((slots, kinds * nodes),...  9.93 us
    pallas_call x1, Pallas kernels, body(): pl.pallas_call(step_kernel, out_shape=(shaped((slots, feature), BF), shap...  6.98 us
    all_to_all x1, waiting for transfers between devices, body(): lax.all_to_all(half, both, split_axis=0, concat_axis=0, tiled=True, axis_...  6.46 us
    all_to_all x1, starting transfers between devices, body(): lax.all_to_all(slot_grads, 'table', split_axis=0, concat_axis=0, tiled=True)  6.44 us
  transfers between devices with their start and end apart: 12, of which 8 were waited for; matrix products, arithmetic and copies ran while one was open for 4% of the time, Pallas kernels for 10%

profile of v6, /device:TPU:1, one launch (start us, length us, event | category | flops | bytes accessed | tf_op | source)
XLA Modules:
  0.0 145.5 jit_solution(7370232000907731849)
XLA Ops:
  0.6 19.1 %all_to_all.55 = s32[32,1,32]{2,1,0:T(1,128)} all-to-all(s32[32,1,32]{2,1,0:T(1,128)} %bitcast.42), channel_id=1, replica_groups=mesh['dp'=16,'table'=32] {'table'}, dimensions={0} | all-to-all | bytes 8192 | tf_op jit(solution)/shard_map/all_to_all | solution.py:289
  19.8 2.9 %gather.1 = bf16[1024,256]{1,0:T(8,128)(2,1)} custom-call(s32[32,32]{1,0:T(8,128)} %bitcast.37, bf16[512,256]{1,0:T(8,128)(2,1)} %table_ref.1), custom_call_target="tpu_custom_call" | custom-call | tf_op jit(solution)/shard_map/gather/pallas_call | solution.py:322
  22.7 3.9 %all-to-all-start.1 = ((bf16[32,32,256]{2,1,0:T(8,128)(2,1)}), bf16[32,32,256]{2,1,0:T(8,128)(2,1)S(1)}, u32[]{:S(2)}, u32[]{:S(2)}) async-start(bf16[32,32,256]{2,1,0:T(8,128)(2,1)} %bitcast.32), calls=%async_computation.1 | async-start | bytes 1048576 | tf_op jit(solution)/shard_map/all_to_all | solution.py:335
  26.6 9.9 %prepare.1 = (bf16[1024,1536]{1,0:T(8,128)(2,1)}, bf16[256,768]{1,0:T(8,128)(2,1)}, bf16[2,6,256,256]{3,2,1,0:T(8,128)(2,1)}, f32[256,256]{1,0:T(8,128)}, f32[256,8]{1,0:T(8,128)}) custom-call(s32[1,256]{1,0:T(1,128)} %bitcast.46, s32[5,4,256]{2,1,0:T(4,128)} %bitcast.39, s32[1,1280]{1,0:T(1,128)} %bitcast.40, s32[1,128]{1,0:T(1,128)} %bitcast.47, ...), custom_call_target="tpu_custom_call" | custom-call | tf_op jit(solution)/shard_map/prepare/pallas_call | solution.py:294
  36.5 5.0 %all-to-all-done.1 = bf16[32,32,256]{2,1,0:T(8,128)(2,1)S(1)} async-done(((bf16[32,32,256]{2,1,0:T(8,128)(2,1)}), bf16[32,32,256]{2,1,0:T(8,128)(2,1)S(1)}, u32[]{:S(2)}, u32[]{:S(2)}) %all-to-all-start.1) | async-done | bytes 524320 | tf_op jit(solution)/shard_map/all_to_all | solution.py:335
  41.5 0.0 copy-start
  41.5 0.8 copy-done
  42.3 7.0 %step.1 = (bf16[1024,256]{1,0:T(8,128)(2,1)}, bf16[256,1536]{1,0:T(8,128)(2,1)}, bf16[256,256]{1,0:T(8,128)(2,1)}, bf16[256,256]{1,0:T(8,128)(2,1)}) custom-call(s32[1,32]{1,0:T(1,128)} %bitcast.48, bf16[1024,256]{1,0:T(8,128)(2,1)} %bitcast.33, bf16[1024,1536]{1,0:T(8,128)(2,1)} %get-tuple-element.24.m1_far, ...), custom_call_target="tpu_custom_call" | custom-call | tf_op jit(solution)/shard_map/step/pallas_call | solution.py:337
  49.3 6.4 %all-to-all-start.2 = ((bf16[32,32,256]{2,1,0:T(8,128)(2,1)}), bf16[32,32,256]{2,1,0:T(8,128)(2,1)S(1)}, u32[]{:S(2)}, u32[]{:S(2)}) async-start(bf16[32,32,256]{2,1,0:T(8,128)(2,1)} %bitcast.34), calls=%async_computation.2 | async-start | bytes 1048576 | tf_op jit(solution)/shard_map/all_to_all | solution.py:357
  55.8 4.8 %grads.1 = (bf16[128,256]{1,0:T(8,128)(2,1)}, f32[6,256,256]{2,1,0:T(8,128)}, bf16[3,256,256]{2,1,0:T(8,128)(2,1)}, bf16[3,256,256]{2,1,0:T(8,128)(2,1)}) custom-call(s32[1]{0:T(128)} %bitcast.core_ref, bf16[256,1536]{1,0:T(8,128)(2,1)} %get-tuple-element.28.agg_ref, bf16[256,256]{1,0:T(8,128)(2,1)} %get-tuple-element.29.hidden_ref, ...), custom_call_target="tpu_custom_call" | custom-call | tf_op jit(solution)/shard_map/grads/pallas_call | solution.py:359
  60.6 4.0 %collective-permute-start = (bf16[3,256,256]{2,1,0:T(8,128)(2,1)}, bf16[3,256,256]{2,1,0:T(8,128)(2,1)S(1)}, u32[]{:S(2)}, u32[]{:S(2)}) collective-permute-start(bf16[3,256,256]{2,1,0:T(8,128)(2,1)} %get-tuple-element.34), channel_id=1, source_target_pairs={{0,32},{32,0},{64,96},{96,64},{128,160},{160,128},{192,224},{224,1... | collective-permute-start | bytes 1179656 | tf_op jit(solution)/shard_map/ppermute | solution.py:373
  64.6 1.9 %collective-permute-start.1 = (bf16[3,256,256]{2,1,0:T(8,128)(2,1)}, bf16[3,256,256]{2,1,0:T(8,128)(2,1)S(1)}, u32[]{:S(2)}, u32[]{:S(2)}) collective-permute-start(bf16[3,256,256]{2,1,0:T(8,128)(2,1)} %get-tuple-element.35), channel_id=1, source_target_pairs={{0,32},{32,0},{64,96},{96,64},{128,160},{160,128},{192,224},{224,1... | collective-permute-start | bytes 1179656 | tf_op jit(solution)/shard_map/ppermute | solution.py:373
  66.6 0.0 collective-permute-done
  66.6 1.9 %collective-permute-done.1 = bf16[3,256,256]{2,1,0:T(8,128)(2,1)S(1)} collective-permute-done((bf16[3,256,256]{2,1,0:T(8,128)(2,1)}, bf16[3,256,256]{2,1,0:T(8,128)(2,1)S(1)}, u32[]{:S(2)}, u32[]{:S(2)}) %collective-permute-start.1) | collective-permute-done | bytes 393248 | tf_op jit(solution)/shard_map/ppermute | solution.py:373
  68.5 2.5 %add_convert_fusion = bf16[6,256,256]{2,1,0:T(8,128)(2,1)} fusion(f32[6,256,256]{2,1,0:T(8,128)} %get-tuple-element.33, bf16[3,256,256]{2,1,0:T(8,128)(2,1)S(1)} %collective-permute-done.1, bf16[3,256,256]{2,1,0:T(8,128)(2,1)S(1)} %collective-permute-done), kind=kLoop, calls=%fused_computation.1 | loop fusion | flops 1572864 | bytes 3145728 | tf_op jit(solution)/shard_map/convert_element_type | solution.py:374
  71.0 0.0 copy-start.1
  71.0 0.0 all-to-all-done.2
  71.0 13.1 %all-to-all-start.3 = ((bf16[32,48,256]{2,1,0:T(8,128)(2,1)}), bf16[32,48,256]{2,1,0:T(8,128)(2,1)S(1)}, u32[]{:S(2)}, u32[]{:S(2)}) async-start(bf16[32,48,256]{2,1,0:T(8,128)(2,1)} %bitcast.19), calls=%async_computation.3 | async-start | bytes 1572864 | tf_op jit(solution)/shard_map/all_to_all | solution.py:391
  84.1 0.6 broadcast.7
  84.7 0.0 copy-done.1
  84.7 0.7 reduce.5
  85.4 0.1 reshape.57.asked_ref
  85.5 0.4 scatter.1
  85.9 1.9 %collective-permute-start.2 = (f32[256,256]{1,0:T(8,128)S(1)}, f32[256,256]{1,0:T(8,128)S(1)}, u32[]{:S(2)}, u32[]{:S(2)}) collective-permute-start(f32[256,256]{1,0:T(8,128)S(1)} %get-tuple-element.40), channel_id=1, source_target_pairs={{0,32},{32,0},{64,96},{96,64},{128,160},{160,128},{192,224},{224,1... | collective-permute-start | bytes 786440 | tf_op jit(solution)/shard_map/ppermute | solution.py:388
  87.8 1.5 %collective-permute-done.2 = f32[256,256]{1,0:T(8,128)S(1)} collective-permute-done((f32[256,256]{1,0:T(8,128)S(1)}, f32[256,256]{1,0:T(8,128)S(1)}, u32[]{:S(2)}, u32[]{:S(2)}) %collective-permute-start.2) | collective-permute-done | bytes 262176 | tf_op jit(solution)/shard_map/ppermute | solution.py:388
  89.4 3.1 %collective-permute-start.3 = (f32[128,256]{1,0:T(8,128)S(1)}, f32[128,256]{1,0:T(8,128)S(1)}, u32[]{:S(2)}, u32[]{:S(2)}) collective-permute-start(f32[128,256]{1,0:T(8,128)S(1)} %slice.25), channel_id=1, source_target_pairs={{0,64},{32,96},{64,0},{96,32},{128,192},{160,224},{192,128},{224,1... | collective-permute-start | bytes 393224 | tf_op jit(solution)/shard_map/ppermute | solution.py:388
  92.5 6.5 %all-to-all-done.3 = bf16[32,48,256]{2,1,0:T(8,128)(2,1)S(1)} async-done(((bf16[32,48,256]{2,1,0:T(8,128)(2,1)}), bf16[32,48,256]{2,1,0:T(8,128)(2,1)S(1)}, u32[]{:S(2)}, u32[]{:S(2)}) %all-to-all-start.3) | async-done | bytes 786464 | tf_op jit(solution)/shard_map/all_to_all | solution.py:391
  99.0 0.1 reduce_sum.21
  99.1 0.7 broadcast_in_dim.9
  99.8 6.4 %all-to-all-start.4 = ((bf16[8,48,256]{2,1,0:T(8,128)(2,1)}), bf16[8,48,256]{2,1,0:T(8,128)(2,1)S(1)}, u32[]{:S(2)}, u32[]{:S(2)}) async-start(bf16[8,48,256]{2,1,0:T(8,128)(2,1)} %broadcast_in_dim.9), calls=%async_computation.4 | async-start | bytes 393216 | tf_op jit(solution)/shard_map/all_to_all | solution.py:397
  106.2 0.0 collective-permute-done.3
  106.2 3.8 %collective-permute-start.4 = (f32[64,256]{1,0:T(8,128)S(1)}, f32[64,256]{1,0:T(8,128)S(1)}, u32[]{:S(2)}, u32[]{:S(2)}) collective-permute-start(f32[64,256]{1,0:T(8,128)S(1)} %slice.27), channel_id=1, source_target_pairs={{0,128},{32,160},{64,192},{96,224},{128,0},{160,32},{192,64},{224,... | collective-permute-start | bytes 196616 | tf_op jit(solution)/shard_map/ppermute | solution.py:388
  110.0 3.3 %collective-permute-done.4 = f32[64,256]{1,0:T(8,128)S(1)} collective-permute-done((f32[64,256]{1,0:T(8,128)S(1)}, f32[64,256]{1,0:T(8,128)S(1)}, u32[]{:S(2)}, u32[]{:S(2)}) %collective-permute-start.4) | collective-permute-done | bytes 65568 | tf_op jit(solution)/shard_map/ppermute | solution.py:388
  113.3 1.5 %all-to-all-done.4 = bf16[8,48,256]{2,1,0:T(8,128)(2,1)S(1)} async-done(((bf16[8,48,256]{2,1,0:T(8,128)(2,1)}), bf16[8,48,256]{2,1,0:T(8,128)(2,1)S(1)}, u32[]{:S(2)}, u32[]{:S(2)}) %all-to-all-start.4) | async-done | bytes 196640 | tf_op jit(solution)/shard_map/all_to_all | solution.py:397
  114.9 0.9 broadcast_in_dim.20
  115.8 4.7 %all-to-all-start.5 = ((bf16[32,48,256]{2,1,0:T(8,128)(2,1)}), bf16[32,48,256]{2,1,0:T(8,128)(2,1)S(1)}, u32[]{:S(2)}, u32[]{:S(2)}) async-start(bf16[32,48,256]{2,1,0:T(8,128)(2,1)} %broadcast_in_dim.20), calls=%async_computation.5 | async-start | bytes 1572864 | tf_op jit(solution)/shard_map/all_to_all | solution.py:410
  120.5 7.1 %collective-permute-start.5 = (f32[32,256]{1,0:T(8,128)S(1)}, f32[32,256]{1,0:T(8,128)S(1)}, u32[]{:S(2)}, u32[]{:S(2)}) collective-permute-start(f32[32,256]{1,0:T(8,128)S(1)} %slice.23), channel_id=1, source_target_pairs={{0,256},{32,288},{64,320},{96,352},{128,384},{160,416},{192,448},{... | collective-permute-start | bytes 98312 | tf_op jit(solution)/shard_map/ppermute | solution.py:388
  127.6 9.1 %collective-permute-done.5 = f32[32,256]{1,0:T(8,128)S(1)} collective-permute-done((f32[32,256]{1,0:T(8,128)S(1)}, f32[32,256]{1,0:T(8,128)S(1)}, u32[]{:S(2)}, u32[]{:S(2)}) %collective-permute-start.5) | collective-permute-done | bytes 32800 | tf_op jit(solution)/shard_map/ppermute | solution.py:388
  136.7 0.6 slice_add_fusion.2
  137.3 0.0 all-to-all-done.5
  137.3 4.9 %collective-permute-start.6 = (bf16[6,256,256]{2,1,0:T(8,128)(2,1)S(1)}, bf16[6,256,256]{2,1,0:T(8,128)(2,1)S(1)}, u32[]{:S(2)}, u32[]{:S(2)}) collective-permute-start(bf16[6,256,256]{2,1,0:T(8,128)(2,1)S(1)} %bitcast.30), channel_id=1, source_target_pairs={{0,32},{32,0},{64,96},{96,64},{128,160},{160,128},{192,224},{224,1... | collective-permute-start | bytes 2359304 | tf_op jit(solution)/shard_map/ppermute | solution.py:420
  142.2 1.9 %collective-permute-done.6 = bf16[6,256,256]{2,1,0:T(8,128)(2,1)S(1)} collective-permute-done((bf16[6,256,256]{2,1,0:T(8,128)(2,1)S(1)}, bf16[6,256,256]{2,1,0:T(8,128)(2,1)S(1)}, u32[]{:S(2)}, u32[]{:S(2)}) %collective-permute-start.6) | collective-permute-done | bytes 786464 | tf_op jit(solution)/shard_map/ppermute | solution.py:420
  144.1 0.1 select_bitcast_fusion.1
  144.2 1.3 pad_maximum_fusion
  (8 shorter events, 0.1 us)
Async XLA Ops:
  22.7 18.8 %all-to-all-start.1 = ((bf16[32,32,256]{2,1,0:T(8,128)(2,1)}), bf16[32,32,256]{2,1,0:T(8,128)(2,1)S(1)}, u32[]{:S(2)}, u32[]{:S(2)}) async-start(bf16[32,32,256]{2,1,0:T(8,128)(2,1)} %bitcast.32), calls=%async_computation.1 | async-start | bytes 1048576 | tf_op jit(solution)/shard_map/all_to_all | solution.py:335
  41.5 0.8 copy-start
  49.3 21.7 %all-to-all-start.2 = ((bf16[32,32,256]{2,1,0:T(8,128)(2,1)}), bf16[32,32,256]{2,1,0:T(8,128)(2,1)S(1)}, u32[]{:S(2)}, u32[]{:S(2)}) async-start(bf16[32,32,256]{2,1,0:T(8,128)(2,1)} %bitcast.34), calls=%async_computation.2 | async-start | bytes 1048576 | tf_op jit(solution)/shard_map/all_to_all | solution.py:357
  60.6 6.0 %collective-permute-start = (bf16[3,256,256]{2,1,0:T(8,128)(2,1)}, bf16[3,256,256]{2,1,0:T(8,128)(2,1)S(1)}, u32[]{:S(2)}, u32[]{:S(2)}) collective-permute-start(bf16[3,256,256]{2,1,0:T(8,128)(2,1)} %get-tuple-element.34), channel_id=1, source_target_pairs={{0,32},{32,0},{64,96},{96,64},{128,160},{160,128},{192,224},{224,1... | collective-permute-start | bytes 1179656 | tf_op jit(solution)/shard_map/ppermute | solution.py:373
  64.6 3.8 %collective-permute-start.1 = (bf16[3,256,256]{2,1,0:T(8,128)(2,1)}, bf16[3,256,256]{2,1,0:T(8,128)(2,1)S(1)}, u32[]{:S(2)}, u32[]{:S(2)}) collective-permute-start(bf16[3,256,256]{2,1,0:T(8,128)(2,1)} %get-tuple-element.35), channel_id=1, source_target_pairs={{0,32},{32,0},{64,96},{96,64},{128,160},{160,128},{192,224},{224,1... | collective-permute-start | bytes 1179656 | tf_op jit(solution)/shard_map/ppermute | solution.py:373
  71.0 13.7 %copy-start.1 = (s32[32,1,32]{2,1,0:T(1,128)S(1)}, s32[32,1,32]{2,1,0:T(1,128)}, u32[]{:S(2)}) copy-start(s32[32,1,32]{2,1,0:T(1,128)} %all_to_all.55) | copy-start | bytes 12292
  71.0 28.0 %all-to-all-start.3 = ((bf16[32,48,256]{2,1,0:T(8,128)(2,1)}), bf16[32,48,256]{2,1,0:T(8,128)(2,1)S(1)}, u32[]{:S(2)}, u32[]{:S(2)}) async-start(bf16[32,48,256]{2,1,0:T(8,128)(2,1)} %bitcast.19), calls=%async_computation.3 | async-start | bytes 1572864 | tf_op jit(solution)/shard_map/all_to_all | solution.py:391
  85.9 3.4 %collective-permute-start.2 = (f32[256,256]{1,0:T(8,128)S(1)}, f32[256,256]{1,0:T(8,128)S(1)}, u32[]{:S(2)}, u32[]{:S(2)}) collective-permute-start(f32[256,256]{1,0:T(8,128)S(1)} %get-tuple-element.40), channel_id=1, source_target_pairs={{0,32},{32,0},{64,96},{96,64},{128,160},{160,128},{192,224},{224,1... | collective-permute-start | bytes 786440 | tf_op jit(solution)/shard_map/ppermute | solution.py:388
  89.4 16.8 %collective-permute-start.3 = (f32[128,256]{1,0:T(8,128)S(1)}, f32[128,256]{1,0:T(8,128)S(1)}, u32[]{:S(2)}, u32[]{:S(2)}) collective-permute-start(f32[128,256]{1,0:T(8,128)S(1)} %slice.25), channel_id=1, source_target_pairs={{0,64},{32,96},{64,0},{96,32},{128,192},{160,224},{192,128},{224,1... | collective-permute-start | bytes 393224 | tf_op jit(solution)/shard_map/ppermute | solution.py:388
  99.8 15.0 %all-to-all-start.4 = ((bf16[8,48,256]{2,1,0:T(8,128)(2,1)}), bf16[8,48,256]{2,1,0:T(8,128)(2,1)S(1)}, u32[]{:S(2)}, u32[]{:S(2)}) async-start(bf16[8,48,256]{2,1,0:T(8,128)(2,1)} %broadcast_in_dim.9), calls=%async_computation.4 | async-start | bytes 393216 | tf_op jit(solution)/shard_map/all_to_all | solution.py:397
  106.2 7.1 %collective-permute-start.4 = (f32[64,256]{1,0:T(8,128)S(1)}, f32[64,256]{1,0:T(8,128)S(1)}, u32[]{:S(2)}, u32[]{:S(2)}) collective-permute-start(f32[64,256]{1,0:T(8,128)S(1)} %slice.27), channel_id=1, source_target_pairs={{0,128},{32,160},{64,192},{96,224},{128,0},{160,32},{192,64},{224,... | collective-permute-start | bytes 196616 | tf_op jit(solution)/shard_map/ppermute | solution.py:388
  115.8 21.5 %all-to-all-start.5 = ((bf16[32,48,256]{2,1,0:T(8,128)(2,1)}), bf16[32,48,256]{2,1,0:T(8,128)(2,1)S(1)}, u32[]{:S(2)}, u32[]{:S(2)}) async-start(bf16[32,48,256]{2,1,0:T(8,128)(2,1)} %broadcast_in_dim.20), calls=%async_computation.5 | async-start | bytes 1572864 | tf_op jit(solution)/shard_map/all_to_all | solution.py:410
  120.5 16.1 %collective-permute-start.5 = (f32[32,256]{1,0:T(8,128)S(1)}, f32[32,256]{1,0:T(8,128)S(1)}, u32[]{:S(2)}, u32[]{:S(2)}) collective-permute-start(f32[32,256]{1,0:T(8,128)S(1)} %slice.23), channel_id=1, source_target_pairs={{0,256},{32,288},{64,320},{96,352},{128,384},{160,416},{192,448},{... | collective-permute-start | bytes 98312 | tf_op jit(solution)/shard_map/ppermute | solution.py:388
  137.3 6.8 %collective-permute-start.6 = (bf16[6,256,256]{2,1,0:T(8,128)(2,1)S(1)}, bf16[6,256,256]{2,1,0:T(8,128)(2,1)S(1)}, u32[]{:S(2)}, u32[]{:S(2)}) collective-permute-start(bf16[6,256,256]{2,1,0:T(8,128)(2,1)S(1)} %bitcast.30), channel_id=1, source_target_pairs={{0,32},{32,0},{64,96},{96,64},{128,160},{160,128},{192,224},{224,1... | collective-permute-start | bytes 2359304 | tf_op jit(solution)/shard_map/ppermute | solution.py:420

commit v7 on v6

--- a/solution.py
+++ b/solution.py
@@ -7,6 +7,7 @@
 
 BF = jnp.bfloat16
 F32 = jnp.float32
+PIECES = 4
 PARAMS = pltpu.CompilerParams(vmem_limit_bytes=58 * 1024 * 1024)
 ROOMY = pltpu.CompilerParams(vmem_limit_bytes=52 * 1024 * 1024)
 
@@ -24,19 +25,27 @@
     return high, (x - high.astype(F32)).astype(BF)
 
 
-def gather_kernel(asked_ref, table_ref, out_ref, hot_ref, near_ref, sem):
-    copy = pltpu.make_async_copy(table_ref, near_ref, sem)
-    copy.start()
+def gather_kernel(asked_ref, table_far, out_far, hot_ref, table_ref, out_ref, sems):
+    load = pltpu.make_async_copy(table_far, table_ref, sems.at[0])
+    load.start()
     groups, width = asked_ref.shape
-    rows = near_ref.shape[0]
+    slots, rows = hot_ref.shape
     columns = jnp.transpose(asked_ref[...].astype(F32))
     lanes = lax.broadcasted_iota(jnp.int32, (width, rows), 1).astype(F32)
     for j in range(groups):
         hot_ref[pl.ds(j * width, width), :] = jnp.where(
             lanes == columns[:, j : j + 1], 1.0, 0.0
         ).astype(BF)
-    copy.wait()
-    out_ref[...] = dot(hot_ref[...], near_ref[...]).astype(BF)
+    load.wait()
+    size = slots // PIECES
+    stores = []
+    for n in range(PIECES):
+        part = pl.ds(n * size, size)
+        out_ref[part, :] = dot(hot_ref[part, :], table_ref[...]).astype(BF)
+        stores.append(pltpu.make_async_copy(out_ref.at[part], out_far.at[part], sems.at[1 + n]))
+        stores[n].start()
+    for store in stores:
+        store.wait()
 
 
 def counts_of(selfs, edges_ref, degree_ref, out_ref, height):
@@ -102,9 +111,19 @@
 
 def step_kernel(
     count_ref,
-    x_ref,
+    x_far,
     m1_far,
     wt_far,
+    back_far,
+    column_far,
+    degree_far,
+    slot_far,
+    agg_far,
+    hidden_far,
+    grad_far,
+    x_ref,
+    m1_ref,
+    wt_ref,
     back_ref,
     column_ref,
     degree_ref,
@@ -112,31 +131,50 @@
     agg_ref,
     hidden_ref,
     grad_ref,
-    live_ref,
+    xt_ref,
     spread_ref,
-    m1_ref,
-    wt_ref,
     sems,
 ):
-    copies = [
-        pltpu.make_async_copy(m1_far, m1_ref, sems.at[0]),
-        pltpu.make_async_copy(wt_far.at[pl.ds(0, 1)], wt_ref, sems.at[1]),
-    ]
-    for copy in copies:
-        copy.start()
     shards = count_ref.shape[1]
     slots, feature = x_ref.shape
     width = slots // shards
     kinds = wt_ref.shape[1]
     nodes = grad_ref.shape[0]
+    size = slots // PIECES
+    pieces = [pl.ds(n * size, size) for n in range(PIECES)]
+    x_loads = [
+        pltpu.make_async_copy(x_far.at[part], x_ref.at[part], sems.at[n])
+        for n, part in enumerate(pieces)
+    ]
+    used = PIECES
+    loads = [
+        pltpu.make_async_copy(source, target, sems.at[used + n])
+        for n, (source, target) in enumerate(
+            [
+                (m1_far, m1_ref),
+                (wt_far.at[pl.ds(0, 1)], wt_ref),
+                (degree_far, degree_ref),
+                (back_far, back_ref),
+                (column_far, column_ref),
+            ]
+        )
+    ]
+    used += len(loads)
+    for load in x_loads + loads:
+        load.start()
     position = lax.broadcasted_iota(jnp.int32, (width, feature), 0)
-    for k in range(shards):
-        rows = x_ref[pl.ds(k * width, width), :].astype(F32)
-        live_ref[pl.ds(k * width, width), :] = jnp.where(position < count_ref[0, k], rows, 0.0)
-    xt = jnp.transpose(live_ref[...]).astype(BF)
+    per_piece = shards // PIECES
+    for n in range(PIECES):
+        x_loads[n].wait()
+        rows = []
+        for k in range(n * per_piece, (n + 1) * per_piece):
+            block = x_ref[pl.ds(k * width, width), :].astype(F32)
+            rows.append(jnp.where(position < count_ref[0, k], block, 0.0))
+        xt_ref[:, pieces[n]] = jnp.transpose(jnp.concatenate(rows, axis=0)).astype(BF)
+    for load in loads:
+        load.wait()
+    xt = xt_ref[...]
     inverse = 1.0 / degree_ref[...].astype(F32)
-    for copy in copies:
-        copy.wait()
     pre = None
     for r in range(kinds):
         part = dot(xt, m1_ref[:, r * nodes : (r + 1) * nodes])
@@ -146,22 +184,37 @@
         agg_ref[:, r * nodes : (r + 1) * nodes] = part
         term = dot(wt_ref[0, r], part)
         pre = term if pre is None else pre + term
+    stores = [pltpu.make_async_copy(agg_ref, agg_far, sems.at[used])]
     logistic = 1.0 / (1.0 + jnp.exp(-pre))
     hidden_ref[...] = (pre * logistic).astype(BF)
+    stores.append(pltpu.make_async_copy(hidden_ref, hidden_far, sems.at[used + 1]))
     slope = logistic * (1.0 + pre * (1.0 - logistic))
     grad_pre = jnp.transpose(back_ref[...] * slope).astype(BF)
     grad_ref[...] = grad_pre
+    stores.append(pltpu.make_async_copy(grad_ref, grad_far, sems.at[used + 2]))
+    for store in stores:
+        store.start()
+    used += len(stores)
     for r in range(kinds):
         part = dot(grad_pre, wt_ref[0, r])
         if r > 0:
             part = part * column_ref[:, r - 1 : r]
         spread_ref[pl.ds(r * nodes, nodes), :] = part.astype(BF)
-    live_ref[...] = dot(m1_ref[...], spread_ref[...])
-    for k in range(shards):
-        rows = live_ref[pl.ds(k * width, width), :]
-        slot_ref[pl.ds(k * width, width), :] = jnp.where(
-            position < count_ref[0, k], rows, 0.0
-        ).astype(BF)
+    spread = spread_ref[...]
+    for n in range(PIECES):
+        grads = dot(m1_ref[pieces[n], :], spread)
+        for k in range(n * per_piece, (n + 1) * per_piece):
+            first = (k - n * per_piece) * width
+            slot_ref[pl.ds(k * width, width), :] = jnp.where(
+                position < count_ref[0, k], grads[first : first + width, :], 0.0
+            ).astype(BF)
+        store = pltpu.make_async_copy(
+            slot_ref.at[pieces[n]], slot_far.at[pieces[n]], sems.at[used + n]
+        )
+        store.start()
+        stores.append(store)
+    for store in stores:
+        store.wait()
 
 
 def grads_kernel(
@@ -237,6 +290,16 @@
     keep_ref[...] = dot(hot_ref[:half, :], grads)
 
 
+def place_kernel(layer_ref, half_far, out_far, sem):
+    copy = pltpu.make_async_copy(half_far, out_far.at[layer_ref[0]], sem)
+    copy.start()
+    copy.wait()
+
+
+def place_other_kernel(layer_ref, half_far, rest_far, out_far, sem):
+    place_kernel(layer_ref, half_far, out_far, sem)
+
+
 def whole(n):
     return [pl.BlockSpec(memory_space=pltpu.VMEM)] * n
 
@@ -323,11 +386,12 @@
         gather_kernel,
         out_shape=shaped((slots, feature), BF),
         in_specs=whole(1) + [far],
-        out_specs=whole(1)[0],
+        out_specs=far,
         scratch_shapes=[
             pltpu.VMEM((slots, rows), BF),
             pltpu.VMEM((rows, feature), BF),
-            pltpu.SemaphoreType.DMA,
+            pltpu.VMEM((slots, feature), BF),
+            pltpu.SemaphoreType.DMA((1 + PIECES,)),
         ],
         compiler_params=PARAMS,
         name="gather",
@@ -342,14 +406,22 @@
             shaped((feature, nodes), BF),
             shaped((nodes, feature), BF),
         ),
-        in_specs=[smem] + whole(1) + [far] * 2 + whole(3),
-        out_specs=tuple(whole(4)),
+        in_specs=[smem] + [far] * 6,
+        out_specs=(far,) * 4,
         scratch_shapes=[
-            pltpu.VMEM((slots, feature), F32),
-            pltpu.VMEM((kinds * nodes, feature), BF),
+            pltpu.VMEM((slots, feature), BF),
             pltpu.VMEM((slots, kinds * nodes), BF),
             pltpu.VMEM((1, kinds, feature, feature), BF),
-            pltpu.SemaphoreType.DMA((2,)),
+            pltpu.VMEM((feature, nodes), F32),
+            pltpu.VMEM((nodes, 8), F32),
+            pltpu.VMEM(degree1.shape, jnp.int32),
+            pltpu.VMEM((slots, feature), BF),
+            pltpu.VMEM((feature, kinds * nodes), BF),
+            pltpu.VMEM((feature, nodes), BF),
+            pltpu.VMEM((nodes, feature), BF),
+            pltpu.VMEM((feature, slots), BF),
+            pltpu.VMEM((kinds * nodes, feature), BF),
+            pltpu.SemaphoreType.DMA((2 * PIECES + 8,)),
         ],
         compiler_params=PARAMS,
         name="step",
@@ -418,12 +490,25 @@
     table_part = halve(rest[:share], rest[share:], 8)
     mine_half, table_part = lax.optimization_barrier((mine_half, table_part))
     other_half = lax.ppermute(mine_half, "dp", swap)
-    weight_grad = jnp.stack(
-        [
-            jnp.where(core == 0, mine_half, other_half),
-            jnp.where(core == 0, other_half, mine_half),
-        ]
-    )
+    weight_grad = pl.pallas_call(
+        place_kernel,
+        out_shape=shaped(weights.shape, BF),
+        in_specs=[smem, far],
+        out_specs=far,
+        scratch_shapes=[pltpu.SemaphoreType.DMA],
+        compiler_params=PARAMS,
+        name="place_mine",
+    )(core.reshape(1), mine_half)
+    weight_grad = pl.pallas_call(
+        place_other_kernel,
+        out_shape=shaped(weights.shape, BF),
+        in_specs=[smem, far, far],
+        out_specs=far,
+        scratch_shapes=[pltpu.SemaphoreType.DMA],
+        input_output_aliases={2: 0},
+        compiler_params=PARAMS,
+        name="place_other",
+    )(1 - core.reshape(1), other_half, weight_grad)
     return (node_out[None, None], weight_grad, table_part[None])
 
 

time: 147 us -> 194 us (1.32)
  Pallas kernels: 25.1 us -> 74.7 us
  waiting for transfers between devices: 30.5 us -> 28.2 us
    pallas_call x0 -> x2, Pallas kernels: none -> 49.9 us  [the longest x1 24.9 us: body(): pl.pallas_call(place_kernel, out_shape=shaped(weights.shape, BF), in_spec...]
  transfers between devices with their start and end apart: 12 -> 12, of which waited for: 8 -> 7; matrix products, arithmetic and copies ran while one was open for 4% -> 3% of each run, Pallas kernels for 10% -> 21%
where the time goes in v7:
time: 194 us; the launch traced here: 193 us
  Pallas kernels  74.7 us (39%)
  starting transfers between devices  61.8 us (32%)
  waiting for transfers between devices  28.2 us (15%)
  blocking collectives  19 us (10%)
  other arithmetic  4.07 us (2%)
  local copies, waits for them, and re-layouts  4.01 us (2%)
    pallas_call x1, Pallas kernels, body(): pl.pallas_call(place_kernel, out_shape=shaped(weights.shape, BF), in_spec...  24.9 us
    pallas_call x1, Pallas kernels, body(): pl.pallas_call(place_other_kernel, out_shape=shaped(weights.shape, BF), i...  24.9 us
    all_to_all x1, blocking collectives, body(): lax.all_to_all(wanted, 'table', split_axis=0, concat_axis=0, tiled=True)  19 us
    ppermute x4, starting transfers between devices, halve(): got = lax.ppermute(give_rows, 'dp', [(i, i ^ bit) for i in range(groups)])  15.9 us
    ppermute x4, waiting for transfers between devices, halve(): got = lax.ppermute(give_rows, 'dp', [(i, i ^ bit) for i in range(groups)])  13.8 us
    all_to_all x1, starting transfers between devices, body(): lax.all_to_all(half, both, split_axis=0, concat_axis=0, tiled=True, axis_...  13.1 us
    pallas_call x1, Pallas kernels, body(): pl.pallas_call(prepare_kernel, out_shape=(shaped((slots, kinds * nodes),...  9.95 us
    pallas_call x1, Pallas kernels, body(): pl.pallas_call(step_kernel, out_shape=(shaped((slots, feature), BF), shap...  6.75 us
  transfers between devices with their start and end apart: 12, of which 7 were waited for; matrix products, arithmetic and copies ran while one was open for 3% of the time, Pallas kernels for 21%

profile of v7, /device:TPU:1, one launch (start us, length us, event | category | flops | bytes accessed | tf_op | source)
XLA Modules:
  0.0 192.7 jit_solution(1670877175620026546)
XLA Ops:
  0.6 19.0 %all_to_all.55 = s32[32,1,32]{2,1,0:T(1,128)} all-to-all(s32[32,1,32]{2,1,0:T(1,128)} %bitcast.38), channel_id=1, replica_groups=mesh['dp'=16,'table'=32] {'table'}, dimensions={0} | all-to-all | bytes 8192 | tf_op jit(solution)/shard_map/all_to_all | solution.py:352
  19.6 2.8 %gather.1 = bf16[1024,256]{1,0:T(8,128)(2,1)} custom-call(s32[32,32]{1,0:T(8,128)} %bitcast.33, bf16[512,256]{1,0:T(8,128)(2,1)} %table_far.1), custom_call_target="tpu_custom_call" | custom-call | tf_op jit(solution)/shard_map/gather/pallas_call | solution.py:385
  22.5 3.9 %all-to-all-start.1 = ((bf16[32,32,256]{2,1,0:T(8,128)(2,1)}), bf16[32,32,256]{2,1,0:T(8,128)(2,1)S(1)}, u32[]{:S(2)}, u32[]{:S(2)}) async-start(bf16[32,32,256]{2,1,0:T(8,128)(2,1)} %bitcast.28), calls=%async_computation.1 | async-start | bytes 1048576 | tf_op jit(solution)/shard_map/all_to_all | solution.py:399
  26.4 9.9 %prepare.1 = (bf16[1024,1536]{1,0:T(8,128)(2,1)}, bf16[256,768]{1,0:T(8,128)(2,1)}, bf16[2,6,256,256]{3,2,1,0:T(8,128)(2,1)}, f32[256,256]{1,0:T(8,128)}, f32[256,8]{1,0:T(8,128)}) custom-call(s32[1,256]{1,0:T(1,128)} %bitcast.42, s32[5,4,256]{2,1,0:T(4,128)} %bitcast.35, s32[1,1280]{1,0:T(1,128)} %bitcast.36, s32[1,128]{1,0:T(1,128)} %bitcast.43, ...), custom_call_target="tpu_custom_call" | custom-call | tf_op jit(solution)/shard_map/prepare/pallas_call | solution.py:357
  36.3 4.6 %all-to-all-done.1 = bf16[32,32,256]{2,1,0:T(8,128)(2,1)S(1)} async-done(((bf16[32,32,256]{2,1,0:T(8,128)(2,1)}), bf16[32,32,256]{2,1,0:T(8,128)(2,1)S(1)}, u32[]{:S(2)}, u32[]{:S(2)}) %all-to-all-start.1) | async-done | bytes 524320 | tf_op jit(solution)/shard_map/all_to_all | solution.py:399
  40.9 0.0 copy-start.1
  40.9 0.8 copy-done.1
  41.7 6.7 %step.1 = (bf16[1024,256]{1,0:T(8,128)(2,1)}, bf16[256,1536]{1,0:T(8,128)(2,1)}, bf16[256,256]{1,0:T(8,128)(2,1)}, bf16[256,256]{1,0:T(8,128)(2,1)}) custom-call(s32[1,32]{1,0:T(1,128)} %bitcast.44, bf16[1024,256]{1,0:T(8,128)(2,1)} %bitcast.29, bf16[1024,1536]{1,0:T(8,128)(2,1)} %get-tuple-element.24.m1_far, ...), custom_call_target="tpu_custom_call" | custom-call | tf_op jit(solution)/shard_map/step/pallas_call | solution.py:401
  48.4 6.4 %all-to-all-start.2 = ((bf16[32,32,256]{2,1,0:T(8,128)(2,1)}), bf16[32,32,256]{2,1,0:T(8,128)(2,1)S(1)}, u32[]{:S(2)}, u32[]{:S(2)}) async-start(bf16[32,32,256]{2,1,0:T(8,128)(2,1)} %bitcast.30), calls=%async_computation.2 | async-start | bytes 1048576 | tf_op jit(solution)/shard_map/all_to_all | solution.py:429
  54.9 4.8 %grads.1 = (bf16[128,256]{1,0:T(8,128)(2,1)}, f32[6,256,256]{2,1,0:T(8,128)}, bf16[3,256,256]{2,1,0:T(8,128)(2,1)}, bf16[3,256,256]{2,1,0:T(8,128)(2,1)}) custom-call(s32[1]{0:T(128)} %bitcast.core_ref.layer_ref, bf16[256,1536]{1,0:T(8,128)(2,1)} %get-tuple-element.28.agg_ref, bf16[256,256]{1,0:T(8,128)(2,1)} %get-tuple-element.29.hidden_ref, ...), custom_call_target="tpu_custom_call" | custom-call | tf_op jit(solution)/shard_map/grads/pallas_call | solution.py:431
  59.7 4.5 %collective-permute-start = (bf16[3,256,256]{2,1,0:T(8,128)(2,1)}, bf16[3,256,256]{2,1,0:T(8,128)(2,1)S(1)}, u32[]{:S(2)}, u32[]{:S(2)}) collective-permute-start(bf16[3,256,256]{2,1,0:T(8,128)(2,1)} %get-tuple-element.34), channel_id=1, source_target_pairs={{0,32},{32,0},{64,96},{96,64},{128,160},{160,128},{192,224},{224,1... | collective-permute-start | bytes 1179656 | tf_op jit(solution)/shard_map/ppermute | solution.py:445
  64.2 1.9 collective-permute-start.1
  66.1 0.0 collective-permute-done
  66.1 1.9 collective-permute-done.1
  68.0 2.5 %add_convert_fusion = bf16[6,256,256]{2,1,0:T(8,128)(2,1)} fusion(f32[6,256,256]{2,1,0:T(8,128)} %get-tuple-element.33, bf16[3,256,256]{2,1,0:T(8,128)(2,1)S(1)} %collective-permute-done.1, bf16[3,256,256]{2,1,0:T(8,128)(2,1)S(1)} %collective-permute-done), kind=kLoop, calls=%fused_computation | loop fusion | flops 1572864 | bytes 3145728 | tf_op jit(solution)/shard_map/convert_element_type | solution.py:446
  70.5 0.0 copy-start.3
  70.5 0.0 all-to-all-done.2
  70.5 13.1 %all-to-all-start.3 = ((bf16[32,48,256]{2,1,0:T(8,128)(2,1)}), bf16[32,48,256]{2,1,0:T(8,128)(2,1)S(1)}, u32[]{:S(2)}, u32[]{:S(2)}) async-start(bf16[32,48,256]{2,1,0:T(8,128)(2,1)} %bitcast.19), calls=%async_computation.3 | async-start | bytes 1572864 | tf_op jit(solution)/shard_map/all_to_all | solution.py:463
  83.7 0.6 broadcast.7
  84.2 0.0 copy-done.3
  84.2 0.7 reduce.5
  85.0 0.1 reshape.59.asked_ref
  85.0 0.4 scatter.1
  85.5 1.9 collective-permute-start.2
  87.4 1.5 collective-permute-done.2
  89.0 3.1 %collective-permute-start.3 = (f32[128,256]{1,0:T(8,128)S(1)}, f32[128,256]{1,0:T(8,128)S(1)}, u32[]{:S(2)}, u32[]{:S(2)}) collective-permute-start(f32[128,256]{1,0:T(8,128)S(1)} %slice.25), channel_id=1, source_target_pairs={{0,64},{32,96},{64,0},{96,32},{128,192},{160,224},{192,128},{224,1... | collective-permute-start | bytes 393224 | tf_op jit(solution)/shard_map/ppermute | solution.py:460
  92.1 6.4 %all-to-all-done.3 = bf16[32,48,256]{2,1,0:T(8,128)(2,1)S(1)} async-done(((bf16[32,48,256]{2,1,0:T(8,128)(2,1)}), bf16[32,48,256]{2,1,0:T(8,128)(2,1)S(1)}, u32[]{:S(2)}, u32[]{:S(2)}) %all-to-all-start.3) | async-done | bytes 786464 | tf_op jit(solution)/shard_map/all_to_all | solution.py:463
  98.5 0.1 reduce_sum.21
  98.7 0.7 broadcast_in_dim.9
  99.3 6.4 %all-to-all-start.4 = ((bf16[8,48,256]{2,1,0:T(8,128)(2,1)}), bf16[8,48,256]{2,1,0:T(8,128)(2,1)S(1)}, u32[]{:S(2)}, u32[]{:S(2)}) async-start(bf16[8,48,256]{2,1,0:T(8,128)(2,1)} %broadcast_in_dim.9), calls=%async_computation.4 | async-start | bytes 393216 | tf_op jit(solution)/shard_map/all_to_all | solution.py:469
  105.7 0.0 collective-permute-done.3
  105.8 3.8 %collective-permute-start.4 = (f32[64,256]{1,0:T(8,128)S(1)}, f32[64,256]{1,0:T(8,128)S(1)}, u32[]{:S(2)}, u32[]{:S(2)}) collective-permute-start(f32[64,256]{1,0:T(8,128)S(1)} %slice.27), channel_id=1, source_target_pairs={{0,128},{32,160},{64,192},{96,224},{128,0},{160,32},{192,64},{224,... | collective-permute-start | bytes 196616 | tf_op jit(solution)/shard_map/ppermute | solution.py:460
  109.6 3.3 %collective-permute-done.4 = f32[64,256]{1,0:T(8,128)S(1)} collective-permute-done((f32[64,256]{1,0:T(8,128)S(1)}, f32[64,256]{1,0:T(8,128)S(1)}, u32[]{:S(2)}, u32[]{:S(2)}) %collective-permute-start.4) | collective-permute-done | bytes 65568 | tf_op jit(solution)/shard_map/ppermute | solution.py:460
  112.9 1.5 all-to-all-done.4
  114.4 0.9 broadcast_in_dim.20
  115.3 4.7 %all-to-all-start.5 = ((bf16[32,48,256]{2,1,0:T(8,128)(2,1)}), bf16[32,48,256]{2,1,0:T(8,128)(2,1)S(1)}, u32[]{:S(2)}, u32[]{:S(2)}) async-start(bf16[32,48,256]{2,1,0:T(8,128)(2,1)} %broadcast_in_dim.20), calls=%async_computation.5 | async-start | bytes 1572864 | tf_op jit(solution)/shard_map/all_to_all | solution.py:482
  120.1 7.1 %collective-permute-start.5 = (f32[32,256]{1,0:T(8,128)S(1)}, f32[32,256]{1,0:T(8,128)S(1)}, u32[]{:S(2)}, u32[]{:S(2)}) collective-permute-start(f32[32,256]{1,0:T(8,128)S(1)} %slice.23), channel_id=1, source_target_pairs={{0,256},{32,288},{64,320},{96,352},{128,384},{160,416},{192,448},{... | collective-permute-start | bytes 98312 | tf_op jit(solution)/shard_map/ppermute | solution.py:460
  127.2 9.1 %collective-permute-done.5 = f32[32,256]{1,0:T(8,128)S(1)} collective-permute-done((f32[32,256]{1,0:T(8,128)S(1)}, f32[32,256]{1,0:T(8,128)S(1)}, u32[]{:S(2)}, u32[]{:S(2)}) %collective-permute-start.5) | collective-permute-done | bytes 32800 | tf_op jit(solution)/shard_map/ppermute | solution.py:460
  136.2 0.6 slice_add_fusion.2
  136.8 0.0 all-to-all-done.5
  136.8 0.0 copy-start
  136.8 4.9 %collective-permute-start.6 = (bf16[6,256,256]{2,1,0:T(8,128)(2,1)S(1)}, bf16[6,256,256]{2,1,0:T(8,128)(2,1)S(1)}, u32[]{:S(2)}, u32[]{:S(2)}) collective-permute-start(bf16[6,256,256]{2,1,0:T(8,128)(2,1)S(1)} %bitcast.26), channel_id=1, source_target_pairs={{0,32},{32,0},{64,96},{96,64},{128,160},{160,128},{192,224},{224,1... | collective-permute-start | bytes 2359304 | tf_op jit(solution)/shard_map/ppermute | solution.py:492
  141.8 0.0 copy-done
  141.8 24.9 %place_mine.1.rest_far = bf16[2,6,256,256]{3,2,1,0:T(8,128)(2,1)} custom-call(s32[1]{0:T(128)} %bitcast.core_ref.layer_ref, bf16[6,256,256]{2,1,0:T(8,128)(2,1)} %bitcast.27), custom_call_target="tpu_custom_call" | custom-call | tf_op jit(solution)/shard_map/place_mine/pallas_call | solution.py:493
  166.7 0.0 collective-permute-done.6.half_far
  166.7 0.0 copy-start.2
  166.8 0.9 copy-done.2
  167.6 24.9 %place_other.1 = bf16[2,6,256,256]{3,2,1,0:T(8,128)(2,1)} custom-call(s32[1]{0:T(128)S(6)} %sub.3.layer_ref, bf16[6,256,256]{2,1,0:T(8,128)(2,1)} %copy-done.2, bf16[2,6,256,256]{3,2,1,0:T(8,128)(2,1)} %place_mine.1.rest_far), custom_call_target="tpu_custom_call", output_to_operand_aliasing={{}: (2, {})} | custom-call | tf_op jit(solution)/shard_map/place_other/pallas_call | solution.py:502
  (8 shorter events, 0.1 us)
Async XLA Ops:
  22.5 18.4 %all-to-all-start.1 = ((bf16[32,32,256]{2,1,0:T(8,128)(2,1)}), bf16[32,32,256]{2,1,0:T(8,128)(2,1)S(1)}, u32[]{:S(2)}, u32[]{:S(2)}) async-start(bf16[32,32,256]{2,1,0:T(8,128)(2,1)} %bitcast.28), calls=%async_computation.1 | async-start | bytes 1048576 | tf_op jit(solution)/shard_map/all_to_all | solution.py:399
  40.9 0.8 copy-start.1
  48.4 22.1 %all-to-all-start.2 = ((bf16[32,32,256]{2,1,0:T(8,128)(2,1)}), bf16[32,32,256]{2,1,0:T(8,128)(2,1)S(1)}, u32[]{:S(2)}, u32[]{:S(2)}) async-start(bf16[32,32,256]{2,1,0:T(8,128)(2,1)} %bitcast.30), calls=%async_computation.2 | async-start | bytes 1048576 | tf_op jit(solution)/shard_map/all_to_all | solution.py:429
  59.7 6.4 %collective-permute-start = (bf16[3,256,256]{2,1,0:T(8,128)(2,1)}, bf16[3,256,256]{2,1,0:T(8,128)(2,1)S(1)}, u32[]{:S(2)}, u32[]{:S(2)}) collective-permute-start(bf16[3,256,256]{2,1,0:T(8,128)(2,1)} %get-tuple-element.34), channel_id=1, source_target_pairs={{0,32},{32,0},{64,96},{96,64},{128,160},{160,128},{192,224},{224,1... | collective-permute-start | bytes 1179656 | tf_op jit(solution)/shard_map/ppermute | solution.py:445
  64.2 3.8 %collective-permute-start.1 = (bf16[3,256,256]{2,1,0:T(8,128)(2,1)}, bf16[3,256,256]{2,1,0:T(8,128)(2,1)S(1)}, u32[]{:S(2)}, u32[]{:S(2)}) collective-permute-start(bf16[3,256,256]{2,1,0:T(8,128)(2,1)} %get-tuple-element.35), channel_id=1, source_target_pairs={{0,32},{32,0},{64,96},{96,64},{128,160},{160,128},{192,224},{224,1... | collective-permute-start | bytes 1179656 | tf_op jit(solution)/shard_map/ppermute | solution.py:445
  70.5 13.7 %copy-start.3 = (s32[32,1,32]{2,1,0:T(1,128)S(1)}, s32[32,1,32]{2,1,0:T(1,128)}, u32[]{:S(2)}) copy-start(s32[32,1,32]{2,1,0:T(1,128)} %all_to_all.55) | copy-start | bytes 12292
  70.5 28.0 %all-to-all-start.3 = ((bf16[32,48,256]{2,1,0:T(8,128)(2,1)}), bf16[32,48,256]{2,1,0:T(8,128)(2,1)S(1)}, u32[]{:S(2)}, u32[]{:S(2)}) async-start(bf16[32,48,256]{2,1,0:T(8,128)(2,1)} %bitcast.19), calls=%async_computation.3 | async-start | bytes 1572864 | tf_op jit(solution)/shard_map/all_to_all | solution.py:463
  85.5 3.4 %collective-permute-start.2 = (f32[256,256]{1,0:T(8,128)S(1)}, f32[256,256]{1,0:T(8,128)S(1)}, u32[]{:S(2)}, u32[]{:S(2)}) collective-permute-start(f32[256,256]{1,0:T(8,128)S(1)} %get-tuple-element.40), channel_id=1, source_target_pairs={{0,32},{32,0},{64,96},{96,64},{128,160},{160,128},{192,224},{224,1... | collective-permute-start | bytes 786440 | tf_op jit(solution)/shard_map/ppermute | solution.py:460
  89.0 16.8 %collective-permute-start.3 = (f32[128,256]{1,0:T(8,128)S(1)}, f32[128,256]{1,0:T(8,128)S(1)}, u32[]{:S(2)}, u32[]{:S(2)}) collective-permute-start(f32[128,256]{1,0:T(8,128)S(1)} %slice.25), channel_id=1, source_target_pairs={{0,64},{32,96},{64,0},{96,32},{128,192},{160,224},{192,128},{224,1... | collective-permute-start | bytes 393224 | tf_op jit(solution)/shard_map/ppermute | solution.py:460
  99.3 15.0 %all-to-all-start.4 = ((bf16[8,48,256]{2,1,0:T(8,128)(2,1)}), bf16[8,48,256]{2,1,0:T(8,128)(2,1)S(1)}, u32[]{:S(2)}, u32[]{:S(2)}) async-start(bf16[8,48,256]{2,1,0:T(8,128)(2,1)} %broadcast_in_dim.9), calls=%async_computation.4 | async-start | bytes 393216 | tf_op jit(solution)/shard_map/all_to_all | solution.py:469
  105.8 7.1 %collective-permute-start.4 = (f32[64,256]{1,0:T(8,128)S(1)}, f32[64,256]{1,0:T(8,128)S(1)}, u32[]{:S(2)}, u32[]{:S(2)}) collective-permute-start(f32[64,256]{1,0:T(8,128)S(1)} %slice.27), channel_id=1, source_target_pairs={{0,128},{32,160},{64,192},{96,224},{128,0},{160,32},{192,64},{224,... | collective-permute-start | bytes 196616 | tf_op jit(solution)/shard_map/ppermute | solution.py:460
  115.3 21.5 %all-to-all-start.5 = ((bf16[32,48,256]{2,1,0:T(8,128)(2,1)}), bf16[32,48,256]{2,1,0:T(8,128)(2,1)S(1)}, u32[]{:S(2)}, u32[]{:S(2)}) async-start(bf16[32,48,256]{2,1,0:T(8,128)(2,1)} %broadcast_in_dim.20), calls=%async_computation.5 | async-start | bytes 1572864 | tf_op jit(solution)/shard_map/all_to_all | solution.py:482
  120.1 16.1 %collective-permute-start.5 = (f32[32,256]{1,0:T(8,128)S(1)}, f32[32,256]{1,0:T(8,128)S(1)}, u32[]{:S(2)}, u32[]{:S(2)}) collective-permute-start(f32[32,256]{1,0:T(8,128)S(1)} %slice.23), channel_id=1, source_target_pairs={{0,256},{32,288},{64,320},{96,352},{128,384},{160,416},{192,448},{... | collective-permute-start | bytes 98312 | tf_op jit(solution)/shard_map/ppermute | solution.py:460
  136.8 4.9 %copy-start = (bf16[32,48,256]{2,1,0:T(8,128)(2,1)}, bf16[32,48,256]{2,1,0:T(8,128)(2,1)S(1)}, u32[]{:S(2)}) copy-start(bf16[32,48,256]{2,1,0:T(8,128)(2,1)S(1)} %all-to-all-done.5) | copy-start | bytes 2359300
  136.8 29.9 %collective-permute-start.6 = (bf16[6,256,256]{2,1,0:T(8,128)(2,1)S(1)}, bf16[6,256,256]{2,1,0:T(8,128)(2,1)S(1)}, u32[]{:S(2)}, u32[]{:S(2)}) collective-permute-start(bf16[6,256,256]{2,1,0:T(8,128)(2,1)S(1)} %bitcast.26), channel_id=1, source_target_pairs={{0,32},{32,0},{64,96},{96,64},{128,160},{160,128},{192,224},{224,1... | collective-permute-start | bytes 2359304 | tf_op jit(solution)/shard_map/ppermute | solution.py:492
  166.7 0.9 copy-start.2

commit v8 on v7

--- a/solution.py
+++ b/solution.py
@@ -25,27 +25,16 @@
     return high, (x - high.astype(F32)).astype(BF)
 
 
-def gather_kernel(asked_ref, table_far, out_far, hot_ref, table_ref, out_ref, sems):
-    load = pltpu.make_async_copy(table_far, table_ref, sems.at[0])
-    load.start()
+def gather_kernel(asked_ref, table_ref, out_ref, hot_ref):
     groups, width = asked_ref.shape
-    slots, rows = hot_ref.shape
+    rows = table_ref.shape[0]
     columns = jnp.transpose(asked_ref[...].astype(F32))
     lanes = lax.broadcasted_iota(jnp.int32, (width, rows), 1).astype(F32)
     for j in range(groups):
         hot_ref[pl.ds(j * width, width), :] = jnp.where(
             lanes == columns[:, j : j + 1], 1.0, 0.0
         ).astype(BF)
-    load.wait()
-    size = slots // PIECES
-    stores = []
-    for n in range(PIECES):
-        part = pl.ds(n * size, size)
-        out_ref[part, :] = dot(hot_ref[part, :], table_ref[...]).astype(BF)
-        stores.append(pltpu.make_async_copy(out_ref.at[part], out_far.at[part], sems.at[1 + n]))
-        stores[n].start()
-    for store in stores:
-        store.wait()
+    out_ref[...] = dot(hot_ref[...], table_ref[...]).astype(BF)
 
 
 def counts_of(selfs, edges_ref, degree_ref, out_ref, height):
@@ -147,11 +136,16 @@
         for n, part in enumerate(pieces)
     ]
     used = PIECES
+    blocks = [pl.ds(r * nodes, nodes) for r in range(kinds)]
+    m1_loads = [
+        pltpu.make_async_copy(m1_far.at[:, block], m1_ref.at[:, block], sems.at[used + r])
+        for r, block in enumerate(blocks)
+    ]
+    used += kinds
     loads = [
         pltpu.make_async_copy(source, target, sems.at[used + n])
         for n, (source, target) in enumerate(
             [
-                (m1_far, m1_ref),
                 (wt_far.at[pl.ds(0, 1)], wt_ref),
                 (degree_far, degree_ref),
                 (back_far, back_ref),
@@ -160,7 +154,7 @@
         )
     ]
     used += len(loads)
-    for load in x_loads + loads:
+    for load in x_loads + m1_loads[:1] + loads + m1_loads[1:]:
         load.start()
     position = lax.broadcasted_iota(jnp.int32, (width, feature), 0)
     per_piece = shards // PIECES
@@ -177,6 +171,7 @@
     inverse = 1.0 / degree_ref[...].astype(F32)
     pre = None
     for r in range(kinds):
+        m1_loads[r].wait()
         part = dot(xt, m1_ref[:, r * nodes : (r + 1) * nodes])
         if r > 0:
             part = part * inverse[:, (r - 1) * nodes : r * nodes]
@@ -290,16 +285,6 @@
     keep_ref[...] = dot(hot_ref[:half, :], grads)
 
 
-def place_kernel(layer_ref, half_far, out_far, sem):
-    copy = pltpu.make_async_copy(half_far, out_far.at[layer_ref[0]], sem)
-    copy.start()
-    copy.wait()
-
-
-def place_other_kernel(layer_ref, half_far, rest_far, out_far, sem):
-    place_kernel(layer_ref, half_far, out_far, sem)
-
-
 def whole(n):
     return [pl.BlockSpec(memory_space=pltpu.VMEM)] * n
 
@@ -385,15 +370,10 @@
     found = pl.pallas_call(
         gather_kernel,
         out_shape=shaped((slots, feature), BF),
-        in_specs=whole(1) + [far],
-        out_specs=far,
-        scratch_shapes=[
-            pltpu.VMEM((slots, rows), BF),
-            pltpu.VMEM((rows, feature), BF),
-            pltpu.VMEM((slots, feature), BF),
-            pltpu.SemaphoreType.DMA((1 + PIECES,)),
-        ],
-        compiler_params=PARAMS,
+        in_specs=whole(2),
+        out_specs=whole(1)[0],
+        scratch_shapes=[pltpu.VMEM((slots, rows), BF)],
+        compiler_params=ROOMY,
         name="gather",
     )(asked, table)
     inputs = lax.all_to_all(found, "table", split_axis=0, concat_axis=0, tiled=True)
@@ -421,7 +401,7 @@
             pltpu.VMEM((nodes, feature), BF),
             pltpu.VMEM((feature, slots), BF),
             pltpu.VMEM((kinds * nodes, feature), BF),
-            pltpu.SemaphoreType.DMA((2 * PIECES + 8,)),
+            pltpu.SemaphoreType.DMA((2 * PIECES + kinds + 7,)),
         ],
         compiler_params=PARAMS,
         name="step",
@@ -490,25 +470,12 @@
     table_part = halve(rest[:share], rest[share:], 8)
     mine_half, table_part = lax.optimization_barrier((mine_half, table_part))
     other_half = lax.ppermute(mine_half, "dp", swap)
-    weight_grad = pl.pallas_call(
-        place_kernel,
-        out_shape=shaped(weights.shape, BF),
-        in_specs=[smem, far],
-        out_specs=far,
-        scratch_shapes=[pltpu.SemaphoreType.DMA],
-        compiler_params=PARAMS,
-        name="place_mine",
-    )(core.reshape(1), mine_half)
-    weight_grad = pl.pallas_call(
-        place_other_kernel,
-        out_shape=shaped(weights.shape, BF),
-        in_specs=[smem, far, far],
-        out_specs=far,
-        scratch_shapes=[pltpu.SemaphoreType.DMA],
-        input_output_aliases={2: 0},
-        compiler_params=PARAMS,
-        name="place_other",
-    )(1 - core.reshape(1), other_half, weight_grad)
+    weight_grad = jnp.stack(
+        [
+            jnp.where(core == 0, mine_half, other_half),
+            jnp.where(core == 0, other_half, mine_half),
+        ]
+    )
     return (node_out[None, None], weight_grad, table_part[None])
 
 

time: 194 us -> 146 us (0.75)
  Pallas kernels: 74.7 us -> 24.1 us
  waiting for transfers between devices: 28.2 us -> 30.3 us
    pallas_call x2 -> x0, Pallas kernels: 49.9 us -> none  [the longest x1 24.9 us: body(): pl.pallas_call(place_kernel, out_shape=shaped(weights.shape, BF), in_spec...]
  transfers between devices with their start and end apart: 12 -> 12, of which waited for: 7 -> 8; matrix products, arithmetic and copies ran while one was open for 3% -> 4% of each run, Pallas kernels for 21% -> 10%
where the time goes in v8:
time: 146 us; the launch traced here: 145 us
  starting transfers between devices  61.5 us (42%)
  waiting for transfers between devices  30.3 us (21%)
  Pallas kernels  24.1 us (17%)
  blocking collectives  19 us (13%)
  other arithmetic  5.4 us (4%)
  local copies, waits for them, and re-layouts  4.06 us (3%)
    all_to_all x1, blocking collectives, body(): lax.all_to_all(wanted, 'table', split_axis=0, concat_axis=0, tiled=True)  19 us
    ppermute x4, starting transfers between devices, halve(): got = lax.ppermute(give_rows, 'dp', [(i, i ^ bit) for i in range(groups)])  15.9 us
    ppermute x4, waiting for transfers between devices, halve(): got = lax.ppermute(give_rows, 'dp', [(i, i ^ bit) for i in range(groups)])  13.8 us
    all_to_all x1, starting transfers between devices, body(): lax.all_to_all(half, both, split_axis=0, concat_axis=0, tiled=True, axis_...  13 us
    pallas_call x1, Pallas kernels, body(): pl.pallas_call(prepare_kernel, out_shape=(shaped((slots, kinds * nodes),...  9.93 us
    pallas_call x1, Pallas kernels, body(): pl.pallas_call(step_kernel, out_shape=(shaped((slots, feature), BF), shap...  7.59 us
    all_to_all x1, starting transfers between devices, body(): lax.all_to_all(slot_grads, 'table', split_axis=0, concat_axis=0, tiled=True)  6.48 us
    all_to_all x1, waiting for transfers between devices, body(): lax.all_to_all(half, both, split_axis=0, concat_axis=0, tiled=True, axis_...  6.48 us
  transfers between devices with their start and end apart: 12, of which 8 were waited for; matrix products, arithmetic and copies ran while one was open for 4% of the time, Pallas kernels for 10%

profile of v8, /device:TPU:1, one launch (start us, length us, event | category | flops | bytes accessed | tf_op | source)
XLA Modules:
  0.0 145.2 jit_solution(15836797866529987480)
XLA Ops:
  0.6 19.0 %all_to_all.55 = s32[32,1,32]{2,1,0:T(1,128)S(1)} all-to-all(s32[32,1,32]{2,1,0:T(1,128)} %bitcast.41), channel_id=1, replica_groups=mesh['dp'=16,'table'=32] {'table'}, dimensions={0} | all-to-all | bytes 8192 | tf_op jit(solution)/shard_map/all_to_all | solution.py:337
  19.6 0.0 copy-start
  19.7 0.9 copy-done
  20.6 1.4 gather.1
  22.0 3.9 %all-to-all-start.1 = ((bf16[32,32,256]{2,1,0:T(8,128)(2,1)}), bf16[32,32,256]{2,1,0:T(8,128)(2,1)S(1)}, u32[]{:S(2)}, u32[]{:S(2)}) async-start(bf16[32,32,256]{2,1,0:T(8,128)(2,1)} %bitcast.4), calls=%async_computation.1 | async-start | bytes 1048576 | tf_op jit(solution)/shard_map/all_to_all | solution.py:379
  25.8 9.9 %prepare.1 = (bf16[1024,1536]{1,0:T(8,128)(2,1)}, bf16[256,768]{1,0:T(8,128)(2,1)}, bf16[2,6,256,256]{3,2,1,0:T(8,128)(2,1)}, f32[256,256]{1,0:T(8,128)}, f32[256,8]{1,0:T(8,128)}) custom-call(s32[1,256]{1,0:T(1,128)} %bitcast.45, s32[5,4,256]{2,1,0:T(4,128)} %bitcast.38, s32[1,1280]{1,0:T(1,128)} %bitcast.39, s32[1,128]{1,0:T(1,128)} %bitcast.46, ...), custom_call_target="tpu_custom_call" | custom-call | tf_op jit(solution)/shard_map/prepare/pallas_call | solution.py:342
  35.8 4.7 %all-to-all-done.1 = bf16[32,32,256]{2,1,0:T(8,128)(2,1)S(1)} async-done(((bf16[32,32,256]{2,1,0:T(8,128)(2,1)}), bf16[32,32,256]{2,1,0:T(8,128)(2,1)S(1)}, u32[]{:S(2)}, u32[]{:S(2)}) %all-to-all-start.1) | async-done | bytes 524320 | tf_op jit(solution)/shard_map/all_to_all | solution.py:379
  40.5 0.0 copy-start.1
  40.5 0.8 copy-done.1
  41.3 7.6 %step.1 = (bf16[1024,256]{1,0:T(8,128)(2,1)}, bf16[256,1536]{1,0:T(8,128)(2,1)}, bf16[256,256]{1,0:T(8,128)(2,1)}, bf16[256,256]{1,0:T(8,128)(2,1)}) custom-call(s32[1,32]{1,0:T(1,128)} %bitcast.47, bf16[1024,256]{1,0:T(8,128)(2,1)} %bitcast.33, bf16[1024,1536]{1,0:T(8,128)(2,1)} %get-tuple-element.24.m1_far, ...), custom_call_target="tpu_custom_call" | custom-call | tf_op jit(solution)/shard_map/step/pallas_call | solution.py:381
  48.9 6.5 %all-to-all-start.2 = ((bf16[32,32,256]{2,1,0:T(8,128)(2,1)}), bf16[32,32,256]{2,1,0:T(8,128)(2,1)S(1)}, u32[]{:S(2)}, u32[]{:S(2)}) async-start(bf16[32,32,256]{2,1,0:T(8,128)(2,1)} %bitcast.34), calls=%async_computation.2 | async-start | bytes 1048576 | tf_op jit(solution)/shard_map/all_to_all | solution.py:409
  55.4 4.8 %grads.1 = (bf16[128,256]{1,0:T(8,128)(2,1)}, f32[6,256,256]{2,1,0:T(8,128)}, bf16[3,256,256]{2,1,0:T(8,128)(2,1)}, bf16[3,256,256]{2,1,0:T(8,128)(2,1)}) custom-call(s32[1]{0:T(128)} %bitcast.core_ref, bf16[256,1536]{1,0:T(8,128)(2,1)} %get-tuple-element.28.agg_ref, bf16[256,256]{1,0:T(8,128)(2,1)} %get-tuple-element.29.hidden_ref, ...), custom_call_target="tpu_custom_call" | custom-call | tf_op jit(solution)/shard_map/grads/pallas_call | solution.py:411
  60.2 4.2 %collective-permute-start = (bf16[3,256,256]{2,1,0:T(8,128)(2,1)}, bf16[3,256,256]{2,1,0:T(8,128)(2,1)S(1)}, u32[]{:S(2)}, u32[]{:S(2)}) collective-permute-start(bf16[3,256,256]{2,1,0:T(8,128)(2,1)} %get-tuple-element.34), channel_id=1, source_target_pairs={{0,32},{32,0},{64,96},{96,64},{128,160},{160,128},{192,224},{224,1... | collective-permute-start | bytes 1179656 | tf_op jit(solution)/shard_map/ppermute | solution.py:425
  64.5 1.9 %collective-permute-start.1 = (bf16[3,256,256]{2,1,0:T(8,128)(2,1)}, bf16[3,256,256]{2,1,0:T(8,128)(2,1)S(1)}, u32[]{:S(2)}, u32[]{:S(2)}) collective-permute-start(bf16[3,256,256]{2,1,0:T(8,128)(2,1)} %get-tuple-element.35), channel_id=1, source_target_pairs={{0,32},{32,0},{64,96},{96,64},{128,160},{160,128},{192,224},{224,1... | collective-permute-start | bytes 1179656 | tf_op jit(solution)/shard_map/ppermute | solution.py:425
  66.4 0.0 collective-permute-done
  66.4 1.9 %collective-permute-done.1 = bf16[3,256,256]{2,1,0:T(8,128)(2,1)S(1)} collective-permute-done((bf16[3,256,256]{2,1,0:T(8,128)(2,1)}, bf16[3,256,256]{2,1,0:T(8,128)(2,1)S(1)}, u32[]{:S(2)}, u32[]{:S(2)}) %collective-permute-start.1) | collective-permute-done | bytes 393248 | tf_op jit(solution)/shard_map/ppermute | solution.py:425
  68.3 2.5 %add_convert_fusion = bf16[6,256,256]{2,1,0:T(8,128)(2,1)} fusion(f32[6,256,256]{2,1,0:T(8,128)} %get-tuple-element.33, bf16[3,256,256]{2,1,0:T(8,128)(2,1)S(1)} %collective-permute-done.1, bf16[3,256,256]{2,1,0:T(8,128)(2,1)S(1)} %collective-permute-done), kind=kLoop, calls=%fused_computation.1 | loop fusion | flops 1572864 | bytes 3145728 | tf_op jit(solution)/shard_map/convert_element_type | solution.py:426
  70.8 0.0 all-to-all-done.2
  70.8 13.0 %all-to-all-start.3 = ((bf16[32,48,256]{2,1,0:T(8,128)(2,1)}), bf16[32,48,256]{2,1,0:T(8,128)(2,1)S(1)}, u32[]{:S(2)}, u32[]{:S(2)}) async-start(bf16[32,48,256]{2,1,0:T(8,128)(2,1)} %bitcast.19), calls=%async_computation.3 | async-start | bytes 1572864 | tf_op jit(solution)/shard_map/all_to_all | solution.py:443
  83.8 0.6 broadcast.7
  84.4 0.7 reduce.5
  85.1 0.1 reshape.57.asked_ref
  85.2 0.4 scatter.1
  85.6 1.9 %collective-permute-start.2 = (f32[256,256]{1,0:T(8,128)S(1)}, f32[256,256]{1,0:T(8,128)S(1)}, u32[]{:S(2)}, u32[]{:S(2)}) collective-permute-start(f32[256,256]{1,0:T(8,128)S(1)} %get-tuple-element.40), channel_id=1, source_target_pairs={{0,32},{32,0},{64,96},{96,64},{128,160},{160,128},{192,224},{224,1... | collective-permute-start | bytes 786440 | tf_op jit(solution)/shard_map/ppermute | solution.py:440
  87.5 1.5 %collective-permute-done.2 = f32[256,256]{1,0:T(8,128)S(1)} collective-permute-done((f32[256,256]{1,0:T(8,128)S(1)}, f32[256,256]{1,0:T(8,128)S(1)}, u32[]{:S(2)}, u32[]{:S(2)}) %collective-permute-start.2) | collective-permute-done | bytes 262176 | tf_op jit(solution)/shard_map/ppermute | solution.py:440
  89.1 3.1 %collective-permute-start.3 = (f32[128,256]{1,0:T(8,128)S(1)}, f32[128,256]{1,0:T(8,128)S(1)}, u32[]{:S(2)}, u32[]{:S(2)}) collective-permute-start(f32[128,256]{1,0:T(8,128)S(1)} %slice.25), channel_id=1, source_target_pairs={{0,64},{32,96},{64,0},{96,32},{128,192},{160,224},{192,128},{224,1... | collective-permute-start | bytes 393224 | tf_op jit(solution)/shard_map/ppermute | solution.py:440
  92.2 6.5 %all-to-all-done.3 = bf16[32,48,256]{2,1,0:T(8,128)(2,1)S(1)} async-done(((bf16[32,48,256]{2,1,0:T(8,128)(2,1)}), bf16[32,48,256]{2,1,0:T(8,128)(2,1)S(1)}, u32[]{:S(2)}, u32[]{:S(2)}) %all-to-all-start.3) | async-done | bytes 786464 | tf_op jit(solution)/shard_map/all_to_all | solution.py:443
  98.7 0.1 reduce_sum.21
  98.8 0.7 broadcast_in_dim.9
  99.5 6.4 %all-to-all-start.4 = ((bf16[8,48,256]{2,1,0:T(8,128)(2,1)}), bf16[8,48,256]{2,1,0:T(8,128)(2,1)S(1)}, u32[]{:S(2)}, u32[]{:S(2)}) async-start(bf16[8,48,256]{2,1,0:T(8,128)(2,1)} %broadcast_in_dim.9), calls=%async_computation.4 | async-start | bytes 393216 | tf_op jit(solution)/shard_map/all_to_all | solution.py:449
  105.9 0.0 collective-permute-done.3
  106.0 3.8 %collective-permute-start.4 = (f32[64,256]{1,0:T(8,128)S(1)}, f32[64,256]{1,0:T(8,128)S(1)}, u32[]{:S(2)}, u32[]{:S(2)}) collective-permute-start(f32[64,256]{1,0:T(8,128)S(1)} %slice.27), channel_id=1, source_target_pairs={{0,128},{32,160},{64,192},{96,224},{128,0},{160,32},{192,64},{224,... | collective-permute-start | bytes 196616 | tf_op jit(solution)/shard_map/ppermute | solution.py:440
  109.8 3.3 %collective-permute-done.4 = f32[64,256]{1,0:T(8,128)S(1)} collective-permute-done((f32[64,256]{1,0:T(8,128)S(1)}, f32[64,256]{1,0:T(8,128)S(1)}, u32[]{:S(2)}, u32[]{:S(2)}) %collective-permute-start.4) | collective-permute-done | bytes 65568 | tf_op jit(solution)/shard_map/ppermute | solution.py:440
  113.1 1.5 %all-to-all-done.4 = bf16[8,48,256]{2,1,0:T(8,128)(2,1)S(1)} async-done(((bf16[8,48,256]{2,1,0:T(8,128)(2,1)}), bf16[8,48,256]{2,1,0:T(8,128)(2,1)S(1)}, u32[]{:S(2)}, u32[]{:S(2)}) %all-to-all-start.4) | async-done | bytes 196640 | tf_op jit(solution)/shard_map/all_to_all | solution.py:449
  114.6 0.9 broadcast_in_dim.20
  115.5 4.7 %all-to-all-start.5 = ((bf16[32,48,256]{2,1,0:T(8,128)(2,1)}), bf16[32,48,256]{2,1,0:T(8,128)(2,1)S(1)}, u32[]{:S(2)}, u32[]{:S(2)}) async-start(bf16[32,48,256]{2,1,0:T(8,128)(2,1)} %broadcast_in_dim.20), calls=%async_computation.5 | async-start | bytes 1572864 | tf_op jit(solution)/shard_map/all_to_all | solution.py:462
  120.3 7.1 %collective-permute-start.5 = (f32[32,256]{1,0:T(8,128)S(1)}, f32[32,256]{1,0:T(8,128)S(1)}, u32[]{:S(2)}, u32[]{:S(2)}) collective-permute-start(f32[32,256]{1,0:T(8,128)S(1)} %slice.23), channel_id=1, source_target_pairs={{0,256},{32,288},{64,320},{96,352},{128,384},{160,416},{192,448},{... | collective-permute-start | bytes 98312 | tf_op jit(solution)/shard_map/ppermute | solution.py:440
  127.3 9.1 %collective-permute-done.5 = f32[32,256]{1,0:T(8,128)S(1)} collective-permute-done((f32[32,256]{1,0:T(8,128)S(1)}, f32[32,256]{1,0:T(8,128)S(1)}, u32[]{:S(2)}, u32[]{:S(2)}) %collective-permute-start.5) | collective-permute-done | bytes 32800 | tf_op jit(solution)/shard_map/ppermute | solution.py:440
  136.4 0.6 slice_add_fusion.2
  137.0 0.0 all-to-all-done.5
  137.0 4.9 %collective-permute-start.6 = (bf16[6,256,256]{2,1,0:T(8,128)(2,1)S(1)}, bf16[6,256,256]{2,1,0:T(8,128)(2,1)S(1)}, u32[]{:S(2)}, u32[]{:S(2)}) collective-permute-start(bf16[6,256,256]{2,1,0:T(8,128)(2,1)S(1)} %bitcast.31), channel_id=1, source_target_pairs={{0,32},{32,0},{64,96},{96,64},{128,160},{160,128},{192,224},{224,1... | collective-permute-start | bytes 2359304 | tf_op jit(solution)/shard_map/ppermute | solution.py:472
  142.0 1.9 %collective-permute-done.6 = bf16[6,256,256]{2,1,0:T(8,128)(2,1)S(1)} collective-permute-done((bf16[6,256,256]{2,1,0:T(8,128)(2,1)S(1)}, bf16[6,256,256]{2,1,0:T(8,128)(2,1)S(1)}, u32[]{:S(2)}, u32[]{:S(2)}) %collective-permute-start.6) | collective-permute-done | bytes 786464 | tf_op jit(solution)/shard_map/ppermute | solution.py:472
  143.9 0.1 select_bitcast_fusion.1
  144.0 1.3 pad_maximum_fusion
  (8 shorter events, 0.1 us)
Async XLA Ops:
  19.6 1.0 copy-start
  22.0 18.5 %all-to-all-start.1 = ((bf16[32,32,256]{2,1,0:T(8,128)(2,1)}), bf16[32,32,256]{2,1,0:T(8,128)(2,1)S(1)}, u32[]{:S(2)}, u32[]{:S(2)}) async-start(bf16[32,32,256]{2,1,0:T(8,128)(2,1)} %bitcast.4), calls=%async_computation.1 | async-start | bytes 1048576 | tf_op jit(solution)/shard_map/all_to_all | solution.py:379
  40.5 0.8 copy-start.1
  48.9 21.9 %all-to-all-start.2 = ((bf16[32,32,256]{2,1,0:T(8,128)(2,1)}), bf16[32,32,256]{2,1,0:T(8,128)(2,1)S(1)}, u32[]{:S(2)}, u32[]{:S(2)}) async-start(bf16[32,32,256]{2,1,0:T(8,128)(2,1)} %bitcast.34), calls=%async_computation.2 | async-start | bytes 1048576 | tf_op jit(solution)/shard_map/all_to_all | solution.py:409
  60.2 6.2 %collective-permute-start = (bf16[3,256,256]{2,1,0:T(8,128)(2,1)}, bf16[3,256,256]{2,1,0:T(8,128)(2,1)S(1)}, u32[]{:S(2)}, u32[]{:S(2)}) collective-permute-start(bf16[3,256,256]{2,1,0:T(8,128)(2,1)} %get-tuple-element.34), channel_id=1, source_target_pairs={{0,32},{32,0},{64,96},{96,64},{128,160},{160,128},{192,224},{224,1... | collective-permute-start | bytes 1179656 | tf_op jit(solution)/shard_map/ppermute | solution.py:425
  64.5 3.8 %collective-permute-start.1 = (bf16[3,256,256]{2,1,0:T(8,128)(2,1)}, bf16[3,256,256]{2,1,0:T(8,128)(2,1)S(1)}, u32[]{:S(2)}, u32[]{:S(2)}) collective-permute-start(bf16[3,256,256]{2,1,0:T(8,128)(2,1)} %get-tuple-element.35), channel_id=1, source_target_pairs={{0,32},{32,0},{64,96},{96,64},{128,160},{160,128},{192,224},{224,1... | collective-permute-start | bytes 1179656 | tf_op jit(solution)/shard_map/ppermute | solution.py:425
  70.8 27.9 %all-to-all-start.3 = ((bf16[32,48,256]{2,1,0:T(8,128)(2,1)}), bf16[32,48,256]{2,1,0:T(8,128)(2,1)S(1)}, u32[]{:S(2)}, u32[]{:S(2)}) async-start(bf16[32,48,256]{2,1,0:T(8,128)(2,1)} %bitcast.19), calls=%async_computation.3 | async-start | bytes 1572864 | tf_op jit(solution)/shard_map/all_to_all | solution.py:443
  85.6 3.4 %collective-permute-start.2 = (f32[256,256]{1,0:T(8,128)S(1)}, f32[256,256]{1,0:T(8,128)S(1)}, u32[]{:S(2)}, u32[]{:S(2)}) collective-permute-start(f32[256,256]{1,0:T(8,128)S(1)} %get-tuple-element.40), channel_id=1, source_target_pairs={{0,32},{32,0},{64,96},{96,64},{128,160},{160,128},{192,224},{224,1... | collective-permute-start | bytes 786440 | tf_op jit(solution)/shard_map/ppermute | solution.py:440
  89.1 16.8 %collective-permute-start.3 = (f32[128,256]{1,0:T(8,128)S(1)}, f32[128,256]{1,0:T(8,128)S(1)}, u32[]{:S(2)}, u32[]{:S(2)}) collective-permute-start(f32[128,256]{1,0:T(8,128)S(1)} %slice.25), channel_id=1, source_target_pairs={{0,64},{32,96},{64,0},{96,32},{128,192},{160,224},{192,128},{224,1... | collective-permute-start | bytes 393224 | tf_op jit(solution)/shard_map/ppermute | solution.py:440
  99.5 15.0 %all-to-all-start.4 = ((bf16[8,48,256]{2,1,0:T(8,128)(2,1)}), bf16[8,48,256]{2,1,0:T(8,128)(2,1)S(1)}, u32[]{:S(2)}, u32[]{:S(2)}) async-start(bf16[8,48,256]{2,1,0:T(8,128)(2,1)} %broadcast_in_dim.9), calls=%async_computation.4 | async-start | bytes 393216 | tf_op jit(solution)/shard_map/all_to_all | solution.py:449
  106.0 7.1 %collective-permute-start.4 = (f32[64,256]{1,0:T(8,128)S(1)}, f32[64,256]{1,0:T(8,128)S(1)}, u32[]{:S(2)}, u32[]{:S(2)}) collective-permute-start(f32[64,256]{1,0:T(8,128)S(1)} %slice.27), channel_id=1, source_target_pairs={{0,128},{32,160},{64,192},{96,224},{128,0},{160,32},{192,64},{224,... | collective-permute-start | bytes 196616 | tf_op jit(solution)/shard_map/ppermute | solution.py:440
  115.5 21.5 %all-to-all-start.5 = ((bf16[32,48,256]{2,1,0:T(8,128)(2,1)}), bf16[32,48,256]{2,1,0:T(8,128)(2,1)S(1)}, u32[]{:S(2)}, u32[]{:S(2)}) async-start(bf16[32,48,256]{2,1,0:T(8,128)(2,1)} %broadcast_in_dim.20), calls=%async_computation.5 | async-start | bytes 1572864 | tf_op jit(solution)/shard_map/all_to_all | solution.py:462
  120.3 16.1 %collective-permute-start.5 = (f32[32,256]{1,0:T(8,128)S(1)}, f32[32,256]{1,0:T(8,128)S(1)}, u32[]{:S(2)}, u32[]{:S(2)}) collective-permute-start(f32[32,256]{1,0:T(8,128)S(1)} %slice.23), channel_id=1, source_target_pairs={{0,256},{32,288},{64,320},{96,352},{128,384},{160,416},{192,448},{... | collective-permute-start | bytes 98312 | tf_op jit(solution)/shard_map/ppermute | solution.py:440
  137.0 6.8 %collective-permute-start.6 = (bf16[6,256,256]{2,1,0:T(8,128)(2,1)S(1)}, bf16[6,256,256]{2,1,0:T(8,128)(2,1)S(1)}, u32[]{:S(2)}, u32[]{:S(2)}) collective-permute-start(bf16[6,256,256]{2,1,0:T(8,128)(2,1)S(1)} %bitcast.31), channel_id=1, source_target_pairs={{0,32},{32,0},{64,96},{96,64},{128,160},{160,128},{192,224},{224,1... | collective-permute-start | bytes 2359304 | tf_op jit(solution)/shard_map/ppermute | solution.py:472

commit v9 on v6

--- a/solution.py
+++ b/solution.py
@@ -7,8 +7,7 @@
 
 BF = jnp.bfloat16
 F32 = jnp.float32
-PARAMS = pltpu.CompilerParams(vmem_limit_bytes=58 * 1024 * 1024)
-ROOMY = pltpu.CompilerParams(vmem_limit_bytes=52 * 1024 * 1024)
+PARAMS = pltpu.CompilerParams(vmem_limit_bytes=52 * 1024 * 1024)
 
 
 def dot(a, b):
@@ -24,24 +23,20 @@
     return high, (x - high.astype(F32)).astype(BF)
 
 
-def gather_kernel(asked_ref, table_ref, out_ref, hot_ref, near_ref, sem):
-    copy = pltpu.make_async_copy(table_ref, near_ref, sem)
-    copy.start()
+def gather_kernel(asked_ref, table_ref, out_ref, hot_ref):
     groups, width = asked_ref.shape
-    rows = near_ref.shape[0]
+    rows = table_ref.shape[0]
     columns = jnp.transpose(asked_ref[...].astype(F32))
     lanes = lax.broadcasted_iota(jnp.int32, (width, rows), 1).astype(F32)
     for j in range(groups):
         hot_ref[pl.ds(j * width, width), :] = jnp.where(
             lanes == columns[:, j : j + 1], 1.0, 0.0
         ).astype(BF)
-    copy.wait()
-    out_ref[...] = dot(hot_ref[...], near_ref[...]).astype(BF)
-
-
-def counts_of(selfs, edges_ref, degree_ref, out_ref, height):
+    out_ref[...] = dot(hot_ref[...], table_ref[...]).astype(BF)
+
+
+def counts_of(selfs, edges_ref, degree_ref, out_ref, slots):
     relations, fan, nodes = edges_ref.shape
-    slots = lax.broadcasted_iota(jnp.int32, (height, nodes), 0)
     out_ref[:, 0:nodes] = jnp.where(slots == selfs, 1.0, 0.0).astype(BF)
     for r in range(relations):
         degree = degree_ref[:, r * nodes : (r + 1) * nodes]
@@ -53,16 +48,15 @@
         out_ref[:, (r + 1) * nodes : (r + 2) * nodes] = total.astype(BF)
 
 
-def inverse_columns(degree_ref, relations):
+def inverse_rows(degree_ref, relations):
     nodes = degree_ref.shape[1] // relations
     inverse = 1.0 / degree_ref[...].astype(F32)
     rows = [inverse[:, r * nodes : (r + 1) * nodes] for r in range(relations)]
-    return jnp.transpose(
-        jnp.concatenate(rows + [jnp.ones((8 - relations, nodes), F32)], axis=0)
-    )
+    return jnp.concatenate(rows + [jnp.ones((8 - relations, nodes), F32)], axis=0)
 
 
 def prepare_kernel(
+    count_ref,
     self1_ref,
     edges1_ref,
     degree1_ref,
@@ -74,19 +68,30 @@
     m1_ref,
     m2_ref,
     wt_ref,
-    back_ref,
-    column_ref,
+    extra_ref,
     high_ref,
     low_ref,
 ):
-    counts_of(self1_ref[...], edges1_ref, degree1_ref, m1_ref, m1_ref.shape[0])
-    counts_of(self2_ref[...], edges2_ref, degree2_ref, m2_ref, m2_ref.shape[0])
+    shards = count_ref.shape[1]
+    width = m1_ref.shape[0] // shards
+    nodes = self1_ref.shape[1]
+    position = lax.broadcasted_iota(jnp.int32, (width, nodes), 0)
+    live = [
+        jnp.where(position < count_ref[0, k], position + k * width, -2) for k in range(shards)
+    ]
+    counts_of(
+        self1_ref[...], edges1_ref, degree1_ref, m1_ref, jnp.concatenate(live, axis=0)
+    )
+    second = lax.broadcasted_iota(jnp.int32, (m2_ref.shape[0], self2_ref.shape[1]), 0)
+    counts_of(self2_ref[...], edges2_ref, degree2_ref, m2_ref, second)
     layers, kinds = weights_ref.shape[0], weights_ref.shape[1]
     for layer in range(layers):
         for r in range(kinds):
             wt_ref[layer, r] = jnp.transpose(weights_ref[layer, r].astype(F32)).astype(BF)
-    column_ref[...] = inverse_columns(degree1_ref, edges1_ref.shape[0])
-    column2 = inverse_columns(degree2_ref, edges2_ref.shape[0])
+    inverse1 = inverse_rows(degree1_ref, edges1_ref.shape[0])
+    extra_ref[nodes : nodes + 8, 0:nodes] = inverse1
+    extra_ref[0:nodes, nodes : nodes + 8] = jnp.transpose(inverse1)
+    column2 = jnp.transpose(inverse_rows(degree2_ref, edges2_ref.shape[0]))
     seeds = cot_ref.shape[0]
     cot = cot_ref[...]
     for r in range(kinds):
@@ -97,26 +102,11 @@
         high_ref[pl.ds(r * seeds, seeds), :] = high
         low_ref[pl.ds(r * seeds, seeds), :] = low
     m2 = m2_ref[...]
-    back_ref[...] = jnp.transpose(dot(m2, high_ref[...]) + dot(m2, low_ref[...]))
+    extra_ref[0:nodes, 0:nodes] = jnp.transpose(dot(m2, high_ref[...]) + dot(m2, low_ref[...]))
 
 
 def step_kernel(
-    count_ref,
-    x_ref,
-    m1_far,
-    wt_far,
-    back_ref,
-    column_ref,
-    degree_ref,
-    slot_ref,
-    agg_ref,
-    hidden_ref,
-    grad_ref,
-    live_ref,
-    spread_ref,
-    m1_ref,
-    wt_ref,
-    sems,
+    x_ref, m1_far, wt_far, extra_ref, slot_ref, all_ref, spread_ref, m1_ref, wt_ref, sems
 ):
     copies = [
         pltpu.make_async_copy(m1_far, m1_ref, sems.at[0]),
@@ -124,51 +114,36 @@
     ]
     for copy in copies:
         copy.start()
-    shards = count_ref.shape[1]
-    slots, feature = x_ref.shape
-    width = slots // shards
     kinds = wt_ref.shape[1]
-    nodes = grad_ref.shape[0]
-    position = lax.broadcasted_iota(jnp.int32, (width, feature), 0)
-    for k in range(shards):
-        rows = x_ref[pl.ds(k * width, width), :].astype(F32)
-        live_ref[pl.ds(k * width, width), :] = jnp.where(position < count_ref[0, k], rows, 0.0)
-    xt = jnp.transpose(live_ref[...]).astype(BF)
-    inverse = 1.0 / degree_ref[...].astype(F32)
+    nodes = all_ref.shape[0]
+    xt = jnp.transpose(x_ref[...])
     for copy in copies:
         copy.wait()
     pre = None
     for r in range(kinds):
         part = dot(xt, m1_ref[:, r * nodes : (r + 1) * nodes])
         if r > 0:
-            part = part * inverse[:, (r - 1) * nodes : r * nodes]
+            part = part * extra_ref[nodes + r - 1 : nodes + r, 0:nodes]
         part = part.astype(BF)
-        agg_ref[:, r * nodes : (r + 1) * nodes] = part
+        all_ref[:, r * nodes : (r + 1) * nodes] = part
         term = dot(wt_ref[0, r], part)
         pre = term if pre is None else pre + term
     logistic = 1.0 / (1.0 + jnp.exp(-pre))
-    hidden_ref[...] = (pre * logistic).astype(BF)
+    all_ref[:, kinds * nodes : (kinds + 1) * nodes] = (pre * logistic).astype(BF)
     slope = logistic * (1.0 + pre * (1.0 - logistic))
-    grad_pre = jnp.transpose(back_ref[...] * slope).astype(BF)
-    grad_ref[...] = grad_pre
+    grad_pre = jnp.transpose(extra_ref[0:nodes, 0:nodes] * slope).astype(BF)
+    all_ref[:, (kinds + 1) * nodes : (kinds + 2) * nodes] = grad_pre
     for r in range(kinds):
         part = dot(grad_pre, wt_ref[0, r])
         if r > 0:
-            part = part * column_ref[:, r - 1 : r]
+            part = part * extra_ref[0:nodes, nodes + r - 1 : nodes + r]
         spread_ref[pl.ds(r * nodes, nodes), :] = part.astype(BF)
-    live_ref[...] = dot(m1_ref[...], spread_ref[...])
-    for k in range(shards):
-        rows = live_ref[pl.ds(k * width, width), :]
-        slot_ref[pl.ds(k * width, width), :] = jnp.where(
-            position < count_ref[0, k], rows, 0.0
-        ).astype(BF)
+    slot_ref[...] = dot(m1_ref[...], spread_ref[...]).astype(BF)
 
 
 def grads_kernel(
     core_ref,
-    agg_ref,
-    hidden_ref,
-    grad_ref,
+    all_ref,
     m2_ref,
     wt_ref,
     degree_ref,
@@ -180,10 +155,11 @@
     agg2_ref,
 ):
     kinds = wt_ref.shape[1]
-    nodes = grad_ref.shape[0]
+    nodes = all_ref.shape[0]
     seeds = cot_ref.shape[0]
     inverse = 1.0 / degree_ref[...].astype(F32)
-    hidden = hidden_ref[...]
+    hidden = all_ref[:, kinds * nodes : (kinds + 1) * nodes]
+    grad_pre = all_ref[:, (kinds + 1) * nodes : (kinds + 2) * nodes]
     out = None
     for r in range(kinds):
         part = dot(hidden, m2_ref[:, r * seeds : (r + 1) * seeds])
@@ -196,7 +172,7 @@
     node_ref[...] = jnp.transpose(out).astype(BF)
 
     def bottom(r):
-        return dot(agg_ref[:, r * nodes : (r + 1) * nodes], grad_ref[...])
+        return dot(all_ref[:, r * nodes : (r + 1) * nodes], grad_pre)
 
     def top(r):
         return dot(agg2_ref[:, r * seeds : (r + 1) * seeds], cot_ref[...])
@@ -291,17 +267,16 @@
     degree1 = first_degree.reshape(1, -1)
     degree2 = second_degree.reshape(1, -1)
     cot = cotangent[0, 0]
-    m1, m2, wt, back, column = pl.pallas_call(
+    m1, m2, wt, extra = pl.pallas_call(
         prepare_kernel,
         out_shape=(
             shaped((slots, kinds * nodes), BF),
             shaped((nodes, kinds * seeds), BF),
             shaped(weights.shape, BF),
-            shaped((feature, nodes), F32),
-            shaped((nodes, 8), F32),
+            shaped((nodes + 8, nodes + 128), F32),
         ),
-        in_specs=whole(8),
-        out_specs=tuple(whole(5)),
+        in_specs=[smem] + whole(8),
+        out_specs=tuple(whole(4)),
         scratch_shapes=[
             pltpu.VMEM((kinds * seeds, feature), BF),
             pltpu.VMEM((kinds * seeds, feature), BF),
@@ -309,6 +284,7 @@
         compiler_params=PARAMS,
         name="prepare",
     )(
+        fetch_count[0],
         first_self[0],
         jnp.swapaxes(first_edges[0, 0], 1, 2),
         degree1,
@@ -322,30 +298,23 @@
     found = pl.pallas_call(
         gather_kernel,
         out_shape=shaped((slots, feature), BF),
-        in_specs=whole(1) + [far],
+        in_specs=whole(2),
         out_specs=whole(1)[0],
-        scratch_shapes=[
-            pltpu.VMEM((slots, rows), BF),
-            pltpu.VMEM((rows, feature), BF),
-            pltpu.SemaphoreType.DMA,
-        ],
+        scratch_shapes=[pltpu.VMEM((slots, rows), BF)],
         compiler_params=PARAMS,
         name="gather",
     )(asked, table)
     inputs = lax.all_to_all(found, "table", split_axis=0, concat_axis=0, tiled=True)
 
-    slot_grads, agg, hidden, grad_pre = pl.pallas_call(
+    slot_grads, packed = pl.pallas_call(
         step_kernel,
         out_shape=(
             shaped((slots, feature), BF),
-            shaped((feature, kinds * nodes), BF),
-            shaped((feature, nodes), BF),
-            shaped((nodes, feature), BF),
+            shaped((nodes, (kinds + 2) * nodes), BF),
         ),
-        in_specs=[smem] + whole(1) + [far] * 2 + whole(3),
-        out_specs=tuple(whole(4)),
+        in_specs=whole(1) + [far] * 2 + whole(1),
+        out_specs=tuple(whole(2)),
         scratch_shapes=[
-            pltpu.VMEM((slots, feature), F32),
             pltpu.VMEM((kinds * nodes, feature), BF),
             pltpu.VMEM((slots, kinds * nodes), BF),
             pltpu.VMEM((1, kinds, feature, feature), BF),
@@ -353,7 +322,7 @@
         ],
         compiler_params=PARAMS,
         name="step",
-    )(fetch_count[0], inputs, m1, wt, back, column, degree1)
+    )(inputs, m1, wt, extra)
     returned = lax.all_to_all(slot_grads, "table", split_axis=0, concat_axis=0, tiled=True)
 
     node_out, keep, send, send2 = pl.pallas_call(
@@ -364,12 +333,12 @@
             shaped((kinds // 2, feature, feature), BF),
             shaped((kinds // 2, feature, feature), BF),
         ),
-        in_specs=[smem] + whole(7),
+        in_specs=[smem] + whole(5),
         out_specs=tuple(whole(4)),
         scratch_shapes=[pltpu.VMEM((feature, kinds * seeds), BF)],
         compiler_params=PARAMS,
         name="grads",
-    )(core.reshape(1), agg, hidden, grad_pre, m2, wt, degree2, cot)
+    )(core.reshape(1), packed, m2, wt, degree2, cot)
     other = jnp.concatenate([lax.ppermute(send, "dp", swap), lax.ppermute(send2, "dp", swap)])
     half = (keep + other.astype(F32)).astype(BF).reshape(-1, feature)
     half, returned = lax.optimization_barrier((half, returned))
@@ -380,7 +349,7 @@
         in_specs=[smem] + whole(2),
         out_specs=tuple(whole(2)),
         scratch_shapes=[pltpu.VMEM((rows, slots), BF)],
-        compiler_params=ROOMY,
+        compiler_params=PARAMS,
         name="scatter",
     )(lax.axis_index("dp").reshape(1), asked.reshape(1, slots), returned)
 

time: 147 us -> 143 us (0.973)
  Pallas kernels: 25.1 us -> 20 us
  waiting for transfers between devices: 30.5 us -> 32 us
    pallas_call x1, Pallas kernels: 9.93 us -> 7.98 us  [body(): pl.pallas_call(prepare_kernel, out_shape=(shaped((slots, kinds * nodes),...]
    all_to_all x1, waiting for transfers between devices: 5 us -> 6.59 us  [body(): lax.all_to_all(found, 'table', split_axis=0, concat_axis=0, tiled=True)]
    pallas_call x1, Pallas kernels: 2.91 us -> 1.35 us  [body(): pl.pallas_call(gather_kernel, out_shape=shaped((slots, feature), BF), in_...]
  transfers between devices with their start and end apart: 12 -> 12, of which waited for: 8 -> 8; matrix products, arithmetic and copies ran while one was open for 4% -> 4% of each run, Pallas kernels for 10% -> 9%
where the time goes in v9:
time: 143 us; the launch traced here: 142 us
  starting transfers between devices  61.5 us (43%)
  waiting for transfers between devices  32 us (22%)
  Pallas kernels  20 us (14%)
  blocking collectives  19.2 us (13%)
  other arithmetic  5.36 us (4%)
  local copies, waits for them, and re-layouts  3.25 us (2%)
    all_to_all x1, blocking collectives, body(): lax.all_to_all(wanted, 'table', split_axis=0, concat_axis=0, tiled=True)  19.2 us
    ppermute x4, starting transfers between devices, halve(): got = lax.ppermute(give_rows, 'dp', [(i, i ^ bit) for i in range(groups)])  15.9 us
    ppermute x4, waiting for transfers between devices, halve(): got = lax.ppermute(give_rows, 'dp', [(i, i ^ bit) for i in range(groups)])  13.8 us
    all_to_all x1, starting transfers between devices, body(): lax.all_to_all(half, both, split_axis=0, concat_axis=0, tiled=True, axis_...  13.2 us
    pallas_call x1, Pallas kernels, body(): pl.pallas_call(prepare_kernel, out_shape=(shaped((slots, kinds * nodes),...  7.98 us
    all_to_all x1, waiting for transfers between devices, body(): lax.all_to_all(found, 'table', split_axis=0, concat_axis=0, tiled=True)  6.59 us
    all_to_all x1, waiting for transfers between devices, body(): lax.all_to_all(half, both, split_axis=0, concat_axis=0, tiled=True, axis_...  6.5 us
    all_to_all x1, starting transfers between devices, body(): lax.all_to_all(jnp.broadcast_to(partial[None], (chips,) + partial.shape)....  6.36 us
  transfers between devices with their start and end apart: 12, of which 8 were waited for; matrix products, arithmetic and copies ran while one was open for 4% of the time, Pallas kernels for 9%

profile of v9, /device:TPU:1, one launch (start us, length us, event | category | flops | bytes accessed | tf_op | source)
XLA Modules:
  0.0 142.2 jit_solution(15843468042569879043)
XLA Ops:
  0.7 19.2 %all_to_all.55 = s32[32,1,32]{2,1,0:T(1,128)S(1)} all-to-all(s32[32,1,32]{2,1,0:T(1,128)} %bitcast.45), channel_id=1, replica_groups=mesh['dp'=16,'table'=32] {'table'}, dimensions={0} | all-to-all | bytes 8192 | tf_op jit(solution)/shard_map/all_to_all | solution.py:265
  19.8 0.9 copy-done
  20.8 1.3 gather.1
  22.1 3.9 %all-to-all-start.1 = ((bf16[32,32,256]{2,1,0:T(8,128)(2,1)}), bf16[32,32,256]{2,1,0:T(8,128)(2,1)S(1)}, u32[]{:S(2)}, u32[]{:S(2)}) async-start(bf16[32,32,256]{2,1,0:T(8,128)(2,1)} %bitcast.3), calls=%async_computation.1 | async-start | bytes 1048576 | tf_op jit(solution)/shard_map/all_to_all | solution.py:307
  26.0 0.0 copy-done.4
  26.1 0.0 copy-done.3
  26.1 0.0 copy-done.8
  26.1 0.0 copy-done.2
  26.1 0.0 copy-done.6
  26.1 0.0 copy-done.7
  26.1 0.0 copy-done.1
  26.1 8.0 %prepare.1 = (bf16[1024,1536]{1,0:T(8,128)(2,1)}, bf16[256,768]{1,0:T(8,128)(2,1)S(1)}, bf16[2,6,256,256]{3,2,1,0:T(8,128)(2,1)}, f32[264,384]{1,0:T(8,128)S(1)}) custom-call(s32[1,32]{1,0:T(1,128)S(1)} %bitcast.40, s32[1,256]{1,0:T(1,128)S(1)} %bitcast.39, s32[5,4,256]{2,1,0:T(4,128)S(1)} %bitcast.34, s32[1,1280]{1,0:T(1,128)S(1)} %bitcast.38, ...), custom_call_target="tpu_custom_call" | custom-call | tf_op jit(solution)/shard_map/prepare/pallas_call | solution.py:270
  34.1 6.6 %all-to-all-done.1 = bf16[32,32,256]{2,1,0:T(8,128)(2,1)S(1)} async-done(((bf16[32,32,256]{2,1,0:T(8,128)(2,1)}), bf16[32,32,256]{2,1,0:T(8,128)(2,1)S(1)}, u32[]{:S(2)}, u32[]{:S(2)}) %all-to-all-start.1) | async-done | bytes 524320 | tf_op jit(solution)/shard_map/all_to_all | solution.py:307
  40.7 5.8 %step.1 = (bf16[1024,256]{1,0:T(8,128)(2,1)}, bf16[256,2048]{1,0:T(8,128)(2,1)}) custom-call(bf16[1024,256]{1,0:T(8,128)(2,1)S(1)} %bitcast.29, bf16[1024,1536]{1,0:T(8,128)(2,1)} %get-tuple-element.21.m1_far, bf16[2,6,256,256]{3,2,1,0:T(8,128)(2,1)} %get-tuple-element.22.wt_far.wt_ref, f32[264,384]{1,0:T(8,128)S(1)} %get-tuple-element.23.extra_ref), custom_call_target="tpu_custom_call" | custom-call | tf_op jit(solution)/shard_map/step/pallas_call | solution.py:309
  46.5 6.3 %all-to-all-start.2 = ((bf16[32,32,256]{2,1,0:T(8,128)(2,1)}), bf16[32,32,256]{2,1,0:T(8,128)(2,1)S(1)}, u32[]{:S(2)}, u32[]{:S(2)}) async-start(bf16[32,32,256]{2,1,0:T(8,128)(2,1)} %bitcast.17), calls=%async_computation.2 | async-start | bytes 1048576 | tf_op jit(solution)/shard_map/all_to_all | solution.py:326
  52.8 4.5 %grads.1 = (bf16[128,256]{1,0:T(8,128)(2,1)}, f32[6,256,256]{2,1,0:T(8,128)}, bf16[3,256,256]{2,1,0:T(8,128)(2,1)S(1)}, bf16[3,256,256]{2,1,0:T(8,128)(2,1)S(1)}) custom-call(s32[1]{0:T(128)} %bitcast.core_ref, bf16[256,2048]{1,0:T(8,128)(2,1)} %get-tuple-element.24.all_ref, bf16[256,768]{1,0:T(8,128)(2,1)S(1)} %get-tuple-element.25.m2_ref, ...), custom_call_target="tpu_custom_call" | custom-call | tf_op jit(solution)/shard_map/grads/pallas_call | solution.py:328
  57.2 4.3 %collective-permute-start = (bf16[3,256,256]{2,1,0:T(8,128)(2,1)S(1)}, bf16[3,256,256]{2,1,0:T(8,128)(2,1)S(1)}, u32[]{:S(2)}, u32[]{:S(2)}) collective-permute-start(bf16[3,256,256]{2,1,0:T(8,128)(2,1)S(1)} %get-tuple-element.28), channel_id=1, source_target_pairs={{0,32},{32,0},{64,96},{96,64},{128,160},{160,128},{192,224},{224,1... | collective-permute-start | bytes 1179656 | tf_op jit(solution)/shard_map/ppermute | solution.py:342
  61.5 1.9 %collective-permute-start.1 = (bf16[3,256,256]{2,1,0:T(8,128)(2,1)S(1)}, bf16[3,256,256]{2,1,0:T(8,128)(2,1)S(1)}, u32[]{:S(2)}, u32[]{:S(2)}) collective-permute-start(bf16[3,256,256]{2,1,0:T(8,128)(2,1)S(1)} %get-tuple-element.29), channel_id=1, source_target_pairs={{0,32},{32,0},{64,96},{96,64},{128,160},{160,128},{192,224},{224,1... | collective-permute-start | bytes 1179656 | tf_op jit(solution)/shard_map/ppermute | solution.py:342
  63.4 0.0 collective-permute-done
  63.4 1.7 %collective-permute-done.1 = bf16[3,256,256]{2,1,0:T(8,128)(2,1)S(1)} collective-permute-done((bf16[3,256,256]{2,1,0:T(8,128)(2,1)S(1)}, bf16[3,256,256]{2,1,0:T(8,128)(2,1)S(1)}, u32[]{:S(2)}, u32[]{:S(2)}) %collective-permute-start.1) | collective-permute-done | bytes 393248 | tf_op jit(solution)/shard_map/ppermute | solution.py:342
  65.1 2.5 %add_convert_fusion = bf16[6,256,256]{2,1,0:T(8,128)(2,1)} fusion(f32[6,256,256]{2,1,0:T(8,128)} %get-tuple-element.27, bf16[3,256,256]{2,1,0:T(8,128)(2,1)S(1)} %collective-permute-done.1, bf16[3,256,256]{2,1,0:T(8,128)(2,1)S(1)} %collective-permute-done), kind=kLoop, calls=%fused_computation.1 | loop fusion | flops 1572864 | bytes 3145728 | tf_op jit(solution)/shard_map/convert_element_type | solution.py:343
  67.6 0.0 all-to-all-done.2
  67.6 13.2 %all-to-all-start.3 = ((bf16[32,48,256]{2,1,0:T(8,128)(2,1)}), bf16[32,48,256]{2,1,0:T(8,128)(2,1)S(1)}, u32[]{:S(2)}, u32[]{:S(2)}) async-start(bf16[32,48,256]{2,1,0:T(8,128)(2,1)} %bitcast.19), calls=%async_computation.3 | async-start | bytes 1572864 | tf_op jit(solution)/shard_map/all_to_all | solution.py:360
  80.8 0.5 broadcast.7
  81.3 0.7 reduce.5
  82.0 0.1 reshape.57.asked_ref
  82.1 0.4 scatter.1
  82.5 1.9 %collective-permute-start.2 = (f32[256,256]{1,0:T(8,128)S(1)}, f32[256,256]{1,0:T(8,128)S(1)}, u32[]{:S(2)}, u32[]{:S(2)}) collective-permute-start(f32[256,256]{1,0:T(8,128)S(1)} %get-tuple-element.34), channel_id=1, source_target_pairs={{0,32},{32,0},{64,96},{96,64},{128,160},{160,128},{192,224},{224,1... | collective-permute-start | bytes 786440 | tf_op jit(solution)/shard_map/ppermute | solution.py:357
  84.4 1.5 %collective-permute-done.2 = f32[256,256]{1,0:T(8,128)S(1)} collective-permute-done((f32[256,256]{1,0:T(8,128)S(1)}, f32[256,256]{1,0:T(8,128)S(1)}, u32[]{:S(2)}, u32[]{:S(2)}) %collective-permute-start.2) | collective-permute-done | bytes 262176 | tf_op jit(solution)/shard_map/ppermute | solution.py:357
  86.0 3.1 %collective-permute-start.3 = (f32[128,256]{1,0:T(8,128)S(1)}, f32[128,256]{1,0:T(8,128)S(1)}, u32[]{:S(2)}, u32[]{:S(2)}) collective-permute-start(f32[128,256]{1,0:T(8,128)S(1)} %slice.25), channel_id=1, source_target_pairs={{0,64},{32,96},{64,0},{96,32},{128,192},{160,224},{192,128},{224,1... | collective-permute-start | bytes 393224 | tf_op jit(solution)/shard_map/ppermute | solution.py:357
  89.1 6.5 %all-to-all-done.3 = bf16[32,48,256]{2,1,0:T(8,128)(2,1)S(1)} async-done(((bf16[32,48,256]{2,1,0:T(8,128)(2,1)}), bf16[32,48,256]{2,1,0:T(8,128)(2,1)S(1)}, u32[]{:S(2)}, u32[]{:S(2)}) %all-to-all-start.3) | async-done | bytes 786464 | tf_op jit(solution)/shard_map/all_to_all | solution.py:360
  95.6 0.1 reduce_sum.21
  95.8 0.7 broadcast_in_dim.9
  96.5 6.4 %all-to-all-start.4 = ((bf16[8,48,256]{2,1,0:T(8,128)(2,1)}), bf16[8,48,256]{2,1,0:T(8,128)(2,1)S(1)}, u32[]{:S(2)}, u32[]{:S(2)}) async-start(bf16[8,48,256]{2,1,0:T(8,128)(2,1)} %broadcast_in_dim.9), calls=%async_computation.4 | async-start | bytes 393216 | tf_op jit(solution)/shard_map/all_to_all | solution.py:366
  102.8 0.0 collective-permute-done.3
  102.9 3.8 %collective-permute-start.4 = (f32[64,256]{1,0:T(8,128)S(1)}, f32[64,256]{1,0:T(8,128)S(1)}, u32[]{:S(2)}, u32[]{:S(2)}) collective-permute-start(f32[64,256]{1,0:T(8,128)S(1)} %slice.27), channel_id=1, source_target_pairs={{0,128},{32,160},{64,192},{96,224},{128,0},{160,32},{192,64},{224,... | collective-permute-start | bytes 196616 | tf_op jit(solution)/shard_map/ppermute | solution.py:357
  106.7 3.3 %collective-permute-done.4 = f32[64,256]{1,0:T(8,128)S(1)} collective-permute-done((f32[64,256]{1,0:T(8,128)S(1)}, f32[64,256]{1,0:T(8,128)S(1)}, u32[]{:S(2)}, u32[]{:S(2)}) %collective-permute-start.4) | collective-permute-done | bytes 65568 | tf_op jit(solution)/shard_map/ppermute | solution.py:357
  110.0 1.5 %all-to-all-done.4 = bf16[8,48,256]{2,1,0:T(8,128)(2,1)S(1)} async-done(((bf16[8,48,256]{2,1,0:T(8,128)(2,1)}), bf16[8,48,256]{2,1,0:T(8,128)(2,1)S(1)}, u32[]{:S(2)}, u32[]{:S(2)}) %all-to-all-start.4) | async-done | bytes 196640 | tf_op jit(solution)/shard_map/all_to_all | solution.py:366
  111.5 0.9 broadcast_in_dim.20
  112.4 4.7 %all-to-all-start.5 = ((bf16[32,48,256]{2,1,0:T(8,128)(2,1)}), bf16[32,48,256]{2,1,0:T(8,128)(2,1)S(1)}, u32[]{:S(2)}, u32[]{:S(2)}) async-start(bf16[32,48,256]{2,1,0:T(8,128)(2,1)} %broadcast_in_dim.20), calls=%async_computation.5 | async-start | bytes 1572864 | tf_op jit(solution)/shard_map/all_to_all | solution.py:379
  117.2 7.1 %collective-permute-start.5 = (f32[32,256]{1,0:T(8,128)S(1)}, f32[32,256]{1,0:T(8,128)S(1)}, u32[]{:S(2)}, u32[]{:S(2)}) collective-permute-start(f32[32,256]{1,0:T(8,128)S(1)} %slice.23), channel_id=1, source_target_pairs={{0,256},{32,288},{64,320},{96,352},{128,384},{160,416},{192,448},{... | collective-permute-start | bytes 98312 | tf_op jit(solution)/shard_map/ppermute | solution.py:357
  124.3 9.1 %collective-permute-done.5 = f32[32,256]{1,0:T(8,128)S(1)} collective-permute-done((f32[32,256]{1,0:T(8,128)S(1)}, f32[32,256]{1,0:T(8,128)S(1)}, u32[]{:S(2)}, u32[]{:S(2)}) %collective-permute-start.5) | collective-permute-done | bytes 32800 | tf_op jit(solution)/shard_map/ppermute | solution.py:357
  133.3 0.6 slice_add_fusion.2
  133.9 0.0 all-to-all-done.5
  133.9 4.9 %collective-permute-start.6 = (bf16[6,256,256]{2,1,0:T(8,128)(2,1)S(1)}, bf16[6,256,256]{2,1,0:T(8,128)(2,1)S(1)}, u32[]{:S(2)}, u32[]{:S(2)}) collective-permute-start(bf16[6,256,256]{2,1,0:T(8,128)(2,1)S(1)} %bitcast.42), channel_id=1, source_target_pairs={{0,32},{32,0},{64,96},{96,64},{128,160},{160,128},{192,224},{224,1... | collective-permute-start | bytes 2359304 | tf_op jit(solution)/shard_map/ppermute | solution.py:389
  138.9 1.9 %collective-permute-done.6 = bf16[6,256,256]{2,1,0:T(8,128)(2,1)S(1)} collective-permute-done((bf16[6,256,256]{2,1,0:T(8,128)(2,1)S(1)}, bf16[6,256,256]{2,1,0:T(8,128)(2,1)S(1)}, u32[]{:S(2)}, u32[]{:S(2)}) %collective-permute-start.6) | collective-permute-done | bytes 786464 | tf_op jit(solution)/shard_map/ppermute | solution.py:389
  140.8 0.1 select_bitcast_fusion.1
  140.9 1.3 pad_maximum_fusion
  (18 shorter events, 0.1 us)
Async XLA Ops:
  0.6 25.4 %copy-start.4 = (s32[1,1,5,128]{3,1,2,0:T(1,128)S(1)}, s32[1,1,5,128]{3,1,2,0:T(1,128)}, u32[]{:S(2)}) copy-start(s32[1,1,5,128]{3,1,2,0:T(1,128)} %param.20) | copy-start | bytes 7684
  0.6 25.4 %copy-start.3 = (s32[1,1,5,128,4]{3,4,2,1,0:T(4,128)S(1)}, s32[1,1,5,128,4]{3,4,2,1,0:T(4,128)}, u32[]{:S(2)}) copy-start(s32[1,1,5,128,4]{3,4,2,1,0:T(4,128)} %param.19) | copy-start | bytes 30724
  0.7 25.4 %copy-start.8 = (s32[1,1,128]{2,1,0:T(1,128)S(1)}, s32[1,1,128]{2,1,0:T(1,128)}, u32[]{:S(2)}) copy-start(s32[1,1,128]{2,1,0:T(1,128)} %param.18) | copy-start | bytes 1540
  0.7 25.4 %copy-start.2 = (s32[1,1,5,256,4]{3,4,2,1,0:T(4,128)S(1)}, s32[1,1,5,256,4]{3,4,2,1,0:T(4,128)}, u32[]{:S(2)}) copy-start(s32[1,1,5,256,4]{3,4,2,1,0:T(4,128)} %param.16) | copy-start | bytes 61444
  0.7 25.4 %copy-start.6 = (s32[1,1,256]{2,1,0:T(1,128)S(1)}, s32[1,1,256]{2,1,0:T(1,128)}, u32[]{:S(2)}) copy-start(s32[1,1,256]{2,1,0:T(1,128)} %param.15) | copy-start | bytes 3076
  0.7 25.4 %copy-start.7 = (s32[1,1,32]{2,1,0:T(1,128)S(1)}, s32[1,1,32]{2,1,0:T(1,128)}, u32[]{:S(2)}) copy-start(s32[1,1,32]{2,1,0:T(1,128)} %param.14) | copy-start | bytes 388
  19.8 1.0 copy-start
  20.8 5.3 %copy-start.1 = (bf16[1,1,128,256]{3,2,1,0:T(8,128)(2,1)S(1)}, bf16[1,1,128,256]{3,2,1,0:T(8,128)(2,1)}, u32[]{:S(2)}) copy-start(bf16[1,1,128,256]{3,2,1,0:T(8,128)(2,1)} %param.21) | copy-start | bytes 196612
  20.8 5.3 %copy-start.5 = (s32[1,1,5,256]{3,1,2,0:T(1,128)S(1)}, s32[1,1,5,256]{3,1,2,0:T(1,128)}, u32[]{:S(2)}) copy-start(s32[1,1,5,256]{3,1,2,0:T(1,128)} %param.17) | copy-start | bytes 15364
  22.1 18.5 %all-to-all-start.1 = ((bf16[32,32,256]{2,1,0:T(8,128)(2,1)}), bf16[32,32,256]{2,1,0:T(8,128)(2,1)S(1)}, u32[]{:S(2)}, u32[]{:S(2)}) async-start(bf16[32,32,256]{2,1,0:T(8,128)(2,1)} %bitcast.3), calls=%async_computation.1 | async-start | bytes 1048576 | tf_op jit(solution)/shard_map/all_to_all | solution.py:307
  46.5 21.1 %all-to-all-start.2 = ((bf16[32,32,256]{2,1,0:T(8,128)(2,1)}), bf16[32,32,256]{2,1,0:T(8,128)(2,1)S(1)}, u32[]{:S(2)}, u32[]{:S(2)}) async-start(bf16[32,32,256]{2,1,0:T(8,128)(2,1)} %bitcast.17), calls=%async_computation.2 | async-start | bytes 1048576 | tf_op jit(solution)/shard_map/all_to_all | solution.py:326
  57.2 6.2 %collective-permute-start = (bf16[3,256,256]{2,1,0:T(8,128)(2,1)S(1)}, bf16[3,256,256]{2,1,0:T(8,128)(2,1)S(1)}, u32[]{:S(2)}, u32[]{:S(2)}) collective-permute-start(bf16[3,256,256]{2,1,0:T(8,128)(2,1)S(1)} %get-tuple-element.28), channel_id=1, source_target_pairs={{0,32},{32,0},{64,96},{96,64},{128,160},{160,128},{192,224},{224,1... | collective-permute-start | bytes 1179656 | tf_op jit(solution)/shard_map/ppermute | solution.py:342
  61.5 3.6 %collective-permute-start.1 = (bf16[3,256,256]{2,1,0:T(8,128)(2,1)S(1)}, bf16[3,256,256]{2,1,0:T(8,128)(2,1)S(1)}, u32[]{:S(2)}, u32[]{:S(2)}) collective-permute-start(bf16[3,256,256]{2,1,0:T(8,128)(2,1)S(1)} %get-tuple-element.29), channel_id=1, source_target_pairs={{0,32},{32,0},{64,96},{96,64},{128,160},{160,128},{192,224},{224,1... | collective-permute-start | bytes 1179656 | tf_op jit(solution)/shard_map/ppermute | solution.py:342
  67.6 28.0 %all-to-all-start.3 = ((bf16[32,48,256]{2,1,0:T(8,128)(2,1)}), bf16[32,48,256]{2,1,0:T(8,128)(2,1)S(1)}, u32[]{:S(2)}, u32[]{:S(2)}) async-start(bf16[32,48,256]{2,1,0:T(8,128)(2,1)} %bitcast.19), calls=%async_computation.3 | async-start | bytes 1572864 | tf_op jit(solution)/shard_map/all_to_all | solution.py:360
  82.5 3.4 %collective-permute-start.2 = (f32[256,256]{1,0:T(8,128)S(1)}, f32[256,256]{1,0:T(8,128)S(1)}, u32[]{:S(2)}, u32[]{:S(2)}) collective-permute-start(f32[256,256]{1,0:T(8,128)S(1)} %get-tuple-element.34), channel_id=1, source_target_pairs={{0,32},{32,0},{64,96},{96,64},{128,160},{160,128},{192,224},{224,1... | collective-permute-start | bytes 786440 | tf_op jit(solution)/shard_map/ppermute | solution.py:357
  86.0 16.8 %collective-permute-start.3 = (f32[128,256]{1,0:T(8,128)S(1)}, f32[128,256]{1,0:T(8,128)S(1)}, u32[]{:S(2)}, u32[]{:S(2)}) collective-permute-start(f32[128,256]{1,0:T(8,128)S(1)} %slice.25), channel_id=1, source_target_pairs={{0,64},{32,96},{64,0},{96,32},{128,192},{160,224},{192,128},{224,1... | collective-permute-start | bytes 393224 | tf_op jit(solution)/shard_map/ppermute | solution.py:357
  96.5 15.0 %all-to-all-start.4 = ((bf16[8,48,256]{2,1,0:T(8,128)(2,1)}), bf16[8,48,256]{2,1,0:T(8,128)(2,1)S(1)}, u32[]{:S(2)}, u32[]{:S(2)}) async-start(bf16[8,48,256]{2,1,0:T(8,128)(2,1)} %broadcast_in_dim.9), calls=%async_computation.4 | async-start | bytes 393216 | tf_op jit(solution)/shard_map/all_to_all | solution.py:366
  102.9 7.1 %collective-permute-start.4 = (f32[64,256]{1,0:T(8,128)S(1)}, f32[64,256]{1,0:T(8,128)S(1)}, u32[]{:S(2)}, u32[]{:S(2)}) collective-permute-start(f32[64,256]{1,0:T(8,128)S(1)} %slice.27), channel_id=1, source_target_pairs={{0,128},{32,160},{64,192},{96,224},{128,0},{160,32},{192,64},{224,... | collective-permute-start | bytes 196616 | tf_op jit(solution)/shard_map/ppermute | solution.py:357
  112.4 21.5 %all-to-all-start.5 = ((bf16[32,48,256]{2,1,0:T(8,128)(2,1)}), bf16[32,48,256]{2,1,0:T(8,128)(2,1)S(1)}, u32[]{:S(2)}, u32[]{:S(2)}) async-start(bf16[32,48,256]{2,1,0:T(8,128)(2,1)} %broadcast_in_dim.20), calls=%async_computation.5 | async-start | bytes 1572864 | tf_op jit(solution)/shard_map/all_to_all | solution.py:379
  117.2 16.1 %collective-permute-start.5 = (f32[32,256]{1,0:T(8,128)S(1)}, f32[32,256]{1,0:T(8,128)S(1)}, u32[]{:S(2)}, u32[]{:S(2)}) collective-permute-start(f32[32,256]{1,0:T(8,128)S(1)} %slice.23), channel_id=1, source_target_pairs={{0,256},{32,288},{64,320},{96,352},{128,384},{160,416},{192,448},{... | collective-permute-start | bytes 98312 | tf_op jit(solution)/shard_map/ppermute | solution.py:357
  133.9 6.8 %collective-permute-start.6 = (bf16[6,256,256]{2,1,0:T(8,128)(2,1)S(1)}, bf16[6,256,256]{2,1,0:T(8,128)(2,1)S(1)}, u32[]{:S(2)}, u32[]{:S(2)}) collective-permute-start(bf16[6,256,256]{2,1,0:T(8,128)(2,1)S(1)} %bitcast.42), channel_id=1, source_target_pairs={{0,32},{32,0},{64,96},{96,64},{128,160},{160,128},{192,224},{224,1... | collective-permute-start | bytes 2359304 | tf_op jit(solution)/shard_map/ppermute | solution.py:389
